TPU v7x, 256 devices: a whole 4x4x8 slice. The times are simulated.
256 devices in a mesh: pair: 64 (over x_hi, z, y), sigma: 4 (over x_lo, core).
Axes of the slice: x: 4 (x_hi: 2, x_lo: 2; x = x_hi * 2 + x_lo), y: 4, z: 8, core: 2. Of those that a mesh axis runs over, the one named last changes fastest.
Arguments:
- pair_density_matrices: bfloat16 [131072, 1536], P('pair'), may hold values from -16 to 16
- energy_bins: int32 [131072, 2], P('pair'), may hold values from 0 to 63
- bin_weights: float32 [2, 64], replicated, may hold values from 0.05 to 1
- coulomb: float32 [1536], replicated, may hold values from 0.5 to 4
- state_matrices: bfloat16 [1536, 2048], P(None, 'sigma'), may hold values from -6 to 6
Outputs:
- screened_states: float32 [1536, 2, 2048], P('pair', None, 'sigma')
- sigma_diag: float32 [2, 2048], P(None, 'sigma')
All inputs are finite; a program needn't handle non-finite values.
Results may differ from a plain program's by a relative error of at most 0.00035.
Values sent between devices are 32-bit elements; how exact they have to be, the bound alone decides.
No kernel may reach another device: no remote copies, remote signals or barrier semaphores. Data moves between devices by JAX's collectives and lax.ppermute only.
A program may use at most 64 MiB of HBM per device.

v0:
```python
import jax
import jax.numpy as jnp
from jax import lax
from jax.experimental import pallas as pl
from jax.experimental.pallas import tpu as pltpu
from jax.sharding import PartitionSpec as P


NX, NZ, NY = 2, 8, 4
COLUMNS = 256
Y_GROUPS = [[base + y for y in range(NY)] for base in range(0, NX * NZ * NY, NY)]


def place(position):
    return position // (NZ * NY), position // NY % NZ, position % NY


def z_perm(dz):
    moves = []
    for position in range(NX * NZ * NY):
        x, z, y = place(position)
        moves.append((position, (x * NZ + (z + dz) % NZ) * NY + y))
    return moves


def x_swap(block):
    x = lax.axis_index("pair") // (NZ * NY)
    pair_count, sigma_count = lax.axis_size("pair"), lax.axis_size("sigma")
    moves = [
        (p * sigma_count + s, (p ^ (NZ * NY)) * sigma_count + (s ^ 2))
        for p in range(pair_count)
        for s in range(sigma_count)
    ]
    away = lax.dynamic_index_in_dim(block, 1 - x, 0, False)
    return lax.dynamic_index_in_dim(block, x, 0, False) + lax.ppermute(away, ("pair", "sigma"), moves)


def y_sum(block):
    return jnp.sum(lax.all_to_all(block, "pair", 0, 0, axis_index_groups=Y_GROUPS, tiled=True), axis=0)


def z_sum(block):
    z = lax.axis_index("pair") // NY % NZ
    half = block.shape[-1] // 2

    def own(*offsets):
        return jnp.stack([lax.dynamic_index_in_dim(block, (z + d) % NZ, 0, False) for d in offsets])

    def send(part, dz):
        return lax.ppermute(part, "pair", z_perm(dz))

    far, ahead, behind = lax.optimization_barrier((own(4)[0], own(1, 3), own(-1, -3)))
    low = send(far[..., :half], -2)
    high = send(far[..., half:], 2)
    up = send(ahead, 1)
    down = send(behind, -1)
    above, below = own(2, -2)
    above = above + up[1]
    below = below + down[1]
    above = jnp.concatenate([above[..., :half], above[..., half:] + high], axis=-1)
    below = jnp.concatenate([below[..., :half] + low, below[..., half:]], axis=-1)
    return own(0)[0] + up[0] + down[0] + send(above, 2) + send(below, -2)


def chi_columns(pairs, quarter, weight, first, blocks, block, where):
    pair_local, width = pairs.shape
    col_count = width // 4
    step_rows = 384

    def body(quarter_ref, pair_ref, slab_ref, weight_ref, out_ref, scaled_ref):
        @pl.when(pl.program_id(0) == 0)
        def _():
            by_pair = jnp.transpose(weight_ref[...])
            for t in range(COLUMNS // 128):
                f, column = divmod(first + 128 * t, col_count)
                product = by_pair[:, f : f + 1] * slab_ref[:, column : column + 128].astype(jnp.float32)
                scaled_ref[:, 128 * t : 128 * t + 128] = product.astype(jnp.bfloat16)

        result = lax.dot_general(
            pair_ref[...], scaled_ref[...], (((0,), (0,)), ((), ())), preferred_element_type=jnp.float32
        )
        for zz in range(4):
            for yy in range(NY):
                at = (zz * NY + yy) * 24
                out_ref[where(zz, yy)] = result[at : at + 24]

    return pl.pallas_call(
        body,
        grid_spec=pltpu.PrefetchScalarGridSpec(
            num_scalar_prefetch=1,
            grid=(width // step_rows,),
            in_specs=[
                pl.BlockSpec((pair_local, step_rows), lambda i, q: (0, i)),
                pl.BlockSpec((pair_local, col_count), lambda i, q: (0, q[0])),
                pl.BlockSpec(weight.shape, lambda i, q: (0, 0)),
            ],
            out_specs=pl.BlockSpec(block, lambda i, q: blocks[1](i)),
            scratch_shapes=[pltpu.VMEM((pair_local, COLUMNS), jnp.bfloat16)],
        ),
        out_shape=jax.ShapeDtypeStruct(blocks[0], jnp.float32),
    )(quarter, pairs, pairs, weight)


def local(pair_density_matrices, energy_bins, bin_weights, coulomb, state_matrices):
    pair_local, width = pair_density_matrices.shape
    pair_count = lax.axis_size("pair")
    sigma_count = lax.axis_size("sigma")
    row_count = width // pair_count
    col_count = width // sigma_count
    pair_position = lax.axis_index("pair")
    sigma_position = lax.axis_index("sigma")
    x = pair_position // (NZ * NY)
    quarter = sigma_position ^ (2 * x)

    bins = energy_bins.T
    bin_levels = jnp.arange(bin_weights.shape[1], dtype=jnp.int32)
    matches = (bins[:, None, :] == bin_levels[None, :, None]).astype(jnp.float32)
    weight = jnp.sum(matches * bin_weights[:, :, None], axis=1) / jnp.float32(pair_local * pair_count)
    weight = jnp.concatenate([weight, jnp.zeros((6, pair_local), jnp.float32)], axis=0)

    def columns(first, blocks, block, where):
        return chi_columns(
            pair_density_matrices, quarter.astype(jnp.int32)[None], weight, first, blocks, block, where
        )

    rc, n = row_count, COLUMNS
    b = columns(
        0, ((NY, NX, NZ, rc, n), lambda i: (0, i // 2, i % 2, 0, 0)), (NY, 1, 4, rc, n), lambda zz, yy: (yy, 0, zz)
    )
    c = columns(
        n, ((NX, NY, NZ, rc, n), lambda i: (i // 2, 0, i % 2, 0, 0)), (1, NY, 4, rc, n), lambda zz, yy: (0, yy, zz)
    )
    a = columns(
        2 * n, ((NZ, NY, NX, rc, n), lambda i: (i % 2, 0, i // 2, 0, 0)), (4, NY, 1, rc, n), lambda zz, yy: (zz, yy, 0)
    )
    b = x_swap(y_sum(b))
    c = y_sum(x_swap(c))
    bc = z_sum(jnp.concatenate([b, c], axis=2))
    a = x_swap(y_sum(z_sum(a)))
    polar = jnp.concatenate([bc, a], axis=1)

    root = jnp.sqrt(coulomb)
    root_rows = lax.dynamic_slice_in_dim(root, pair_position * row_count, row_count, 0)
    root_columns = lax.dynamic_slice_in_dim(root, quarter * col_count, col_count, 0)
    screened = -root_rows[:, None, None] * polar.reshape(row_count, -1, col_count) * root_columns[None, None, :]
    parts = [screened] + [
        lax.ppermute(screened, "sigma", [(s, s ^ k) for s in range(sigma_count)]) for k in range(1, sigma_count)
    ]
    for bit in (1, 2):
        odd = (quarter & bit) != 0
        parts = [jnp.where(odd, parts[k ^ bit], parts[k]) for k in range(sigma_count)]
    states_wide = state_matrices.astype(jnp.float32)
    applied = jnp.einsum(
        "rfc,cn->rfn", jnp.concatenate(parts, axis=2), states_wide, precision=lax.Precision.HIGHEST
    )
    own_states = lax.dynamic_slice_in_dim(states_wide, pair_position * row_count, row_count, 0)
    total = jnp.sum(own_states[:, None, :] * applied, axis=0) / jnp.float32(width)
    spread = jnp.broadcast_to(total.reshape(8, -1)[None], (pair_count, 8, total.size // 8))
    total = jnp.sum(lax.all_to_all(spread, "pair", 0, 0, tiled=True), axis=0).reshape(total.shape)
    return (applied, total)


def solution(mesh):
    return jax.shard_map(
        local,
        mesh=mesh,
        in_specs=(P("pair", None), P("pair", None), P(), P(), P(None, "sigma")),
        out_specs=(P("pair", None, "sigma"), P(None, "sigma")),
        check_vma=False,
    )
```

profile of v0, /device:TPU:2, one launch (start us, length us, event | category | flops | bytes accessed | tf_op | source)
XLA Modules:
  0.0 150.6 jit_solution(220285402382853633)
XLA Ops:
  0.8 1.0 select_reduce_fusion
  1.8 0.6 concatenate.24.weight_ref
  2.4 6.9 %shard_map.70 = f32[8,4,2,24,256]{4,3,2,1,0:T(8,128)} custom-call(s32[1]{0:T(128)} %bitcast.quarter_ref, bf16[2048,1536]{1,0:T(8,128)(2,1)} %slab_ref.5, bf16[2048,1536]{1,0:T(8,128)(2,1)} %slab_ref.5, f32[8,2048]{1,0:T(8,128)} %concatenate.24.weight_ref), custom_call_target="tpu_custom_call" | custom-call | tf_op jit(solution)/shard_map/pallas_call | solution.py:87
  9.4 1.4 constant_dynamic-slice_fusion.1
  10.7 0.1 pad_maximum_fusion
  10.8 2.0 %collective-permute-start.8 = (f32[2,4,2,24,256]{4,3,2,1,0:T(8,128)S(1)}, f32[2,4,2,24,256]{4,3,2,1,0:T(8,128)S(1)}, u32[]{:S(2)}, u32[]{:S(2)}) collective-permute-start(f32[2,4,2,24,256]{4,3,2,1,0:T(8,128)S(1)} %get-tuple-element.11), channel_id=1, source_target_pairs={{0,16},{4,20},{8,24},{12,28},{16,32},{20,36},{24,40},{28,44},{32,4... | collective-permute-start | bytes 1179656 | tf_op jit(solution)/shard_map/ppermute | solution.py:50
  12.8 4.0 %collective-permute-start.9 = (f32[2,4,2,24,256]{4,3,2,1,0:T(8,128)S(1)}, f32[2,4,2,24,256]{4,3,2,1,0:T(8,128)S(1)}, u32[]{:S(2)}, u32[]{:S(2)}) collective-permute-start(f32[2,4,2,24,256]{4,3,2,1,0:T(8,128)S(1)} %get-tuple-element.12), channel_id=1, source_target_pairs={{0,112},{4,116},{8,120},{12,124},{16,0},{20,4},{24,8},{28,12},{32,... | collective-permute-start | bytes 1179656 | tf_op jit(solution)/shard_map/ppermute | solution.py:50
  16.8 0.1 collective-permute-start.10
  16.9 4.1 %collective-permute-start.12 = (f32[4,2,24,128]{3,2,1,0:T(8,128)S(1)}, f32[4,2,24,128]{3,2,1,0:T(8,128)S(1)}, u32[]{:S(2)}, u32[]{:S(2)}) collective-permute-start(f32[4,2,24,128]{3,2,1,0:T(8,128)S(1)} %get-tuple-element.41), channel_id=1, source_target_pairs={{0,96},{4,100},{8,104},{12,108},{16,112},{20,116},{24,120},{28,124... | collective-permute-start | bytes 294920 | tf_op jit(solution)/shard_map/ppermute | solution.py:50
  21.1 6.1 %collective-permute-done.8 = f32[2,4,2,24,256]{4,3,2,1,0:T(8,128)S(1)} collective-permute-done((f32[2,4,2,24,256]{4,3,2,1,0:T(8,128)S(1)}, f32[2,4,2,24,256]{4,3,2,1,0:T(8,128)S(1)}, u32[]{:S(2)}, u32[]{:S(2)}) %collective-permute-start.8) | collective-permute-done | bytes 393248 | tf_op jit(solution)/shard_map/ppermute | solution.py:50
  27.2 1.2 collective-permute-done.9
  28.4 1.1 fusion.10
  29.4 0.6 collective-permute-done.10
  30.0 0.3 collective-permute-start.11
  30.3 0.0 collective-permute-done.12
  30.3 4.0 %collective-permute-start.13 = (f32[4,2,24,256]{3,2,1,0:T(8,128)S(1)}, f32[4,2,24,256]{3,2,1,0:T(8,128)S(1)}, u32[]{:S(2)}, u32[]{:S(2)}) collective-permute-start(f32[4,2,24,256]{3,2,1,0:T(8,128)S(1)} %pad_maximum_fusion.3), channel_id=1, source_target_pairs={{0,96},{4,100},{8,104},{12,108},{16,112},{20,116},{24,120},{28,124... | collective-permute-start | bytes 589832 | tf_op jit(solution)/shard_map/ppermute | solution.py:50
  34.4 6.0 %collective-permute-done.11 = f32[4,2,24,256]{3,2,1,0:T(8,128)S(1)} collective-permute-done((f32[4,2,24,256]{3,2,1,0:T(8,128)S(1)}, f32[4,2,24,256]{3,2,1,0:T(8,128)S(1)}, u32[]{:S(2)}, u32[]{:S(2)}) %collective-permute-start.11) | collective-permute-done | bytes 196640 | tf_op jit(solution)/shard_map/ppermute | solution.py:50
  40.3 2.1 %collective-permute-done.13 = f32[4,2,24,256]{3,2,1,0:T(8,128)S(1)} collective-permute-done((f32[4,2,24,256]{3,2,1,0:T(8,128)S(1)}, f32[4,2,24,256]{3,2,1,0:T(8,128)S(1)}, u32[]{:S(2)}, u32[]{:S(2)}) %collective-permute-start.13) | collective-permute-done | bytes 196640 | tf_op jit(solution)/shard_map/ppermute | solution.py:50
  42.5 1.7 %fusion.13 = f32[4,2,24,256]{3,2,1,0:T(8,128)} fusion(f32[4,2,24,256]{3,2,1,0:T(8,128)S(1)} %collective-permute-done.13, f32[4,2,24,256]{3,2,1,0:T(8,128)S(1)} %collective-permute-done.11, f32[2,4,2,24,256]{4,3,2,1,0:T(8,128)S(1)} %collective-permute-done.9, f32[2,4,2,24,256]{4,3,2,1,0:T(8,128)S(1)} %collective-permute-done.8, ...), kind=kLoop, calls=%fused_computation.38 | loop fusion | flops 196608 | bytes 1179652 | tf_op jit(solution)/shard_map/add | solution.py:62
  44.2 4.5 %all-to-all-start.2 = ((f32[4,2,24,256]{3,2,1,0:T(8,128)}), f32[4,2,24,256]{3,2,1,0:T(8,128)S(1)}, u32[]{:S(2)}, u32[]{:S(2)}) async-start(f32[4,2,24,256]{3,2,1,0:T(8,128)} %fusion.13), calls=%async_computation.2 | async-start | bytes 393216 | tf_op jit(solution)/shard_map/all_to_all | solution.py:39
  48.6 7.2 %shard_map.69 = f32[2,4,8,24,256]{4,3,2,1,0:T(8,128)} custom-call(s32[1]{0:T(128)} %bitcast.quarter_ref, bf16[2048,1536]{1,0:T(8,128)(2,1)} %slab_ref.5, bf16[2048,1536]{1,0:T(8,128)(2,1)} %slab_ref.5, f32[8,2048]{1,0:T(8,128)} %concatenate.24.weight_ref), custom_call_target="tpu_custom_call" | custom-call | tf_op jit(solution)/shard_map/pallas_call | solution.py:87
  55.8 6.9 %shard_map.68 = f32[4,2,8,24,256]{4,3,2,1,0:T(8,128)} custom-call(s32[1]{0:T(128)} %bitcast.quarter_ref, bf16[2048,1536]{1,0:T(8,128)(2,1)} %slab_ref.5, bf16[2048,1536]{1,0:T(8,128)(2,1)} %slab_ref.5, f32[8,2048]{1,0:T(8,128)} %concatenate.24.weight_ref), custom_call_target="tpu_custom_call" | custom-call | tf_op jit(solution)/shard_map/pallas_call | solution.py:87
  62.7 0.0 all-to-all-done.2
  62.7 4.9 %all-to-all-start = ((f32[4,2,8,24,256]{4,3,2,1,0:T(8,128)}), f32[4,2,8,24,256]{4,3,2,1,0:T(8,128)S(1)}, u32[]{:S(2)}, u32[]{:S(2)}) async-start(f32[4,2,8,24,256]{4,3,2,1,0:T(8,128)} %shard_map.68), calls=%async_computation | async-start | bytes 3145728 | tf_op jit(solution)/shard_map/all_to_all | solution.py:39
  67.7 1.0 dynamic-slice_bitcast_fusion
  68.6 1.5 collective-permute-start.1
  70.1 14.0 %collective-permute-done.1 = f32[4,8,24,256]{3,2,1,0:T(8,128)} collective-permute-done((f32[4,8,24,256]{3,2,1,0:T(8,128)}, f32[4,8,24,256]{3,2,1,0:T(8,128)}, u32[]{:S(2)}, u32[]{:S(2)}) %collective-permute-start.1) | collective-permute-done | bytes 786464 | tf_op jit(solution)/shard_map/ppermute | solution.py:35
  84.1 2.1 %bitcast_add_fusion = f32[4,8,24,256]{3,2,1,0:T(8,128)} fusion(f32[4,8,24,256]{3,2,1,0:T(8,128)} %collective-permute-done.1, f32[2,4,8,24,256]{4,3,2,1,0:T(8,128)S(1)} %copy-done, s32[]{:T(128)S(6)} %select_n.164), kind=kLoop, calls=%fused_computation.20 | loop fusion | flops 196608 | bytes 2359300 | tf_op jit(solution)/shard_map/add | solution.py:35
  86.2 0.0 all-to-all-done
  86.2 4.5 %all-to-all-start.1 = ((f32[4,8,24,256]{3,2,1,0:T(8,128)}), f32[4,8,24,256]{3,2,1,0:T(8,128)S(1)}, u32[]{:S(2)}, u32[]{:S(2)}) async-start(f32[4,8,24,256]{3,2,1,0:T(8,128)} %bitcast_add_fusion), calls=%async_computation.1 | async-start | bytes 1572864 | tf_op jit(solution)/shard_map/all_to_all | solution.py:39
  90.8 0.1 dynamic_slice.103
  90.8 0.1 reduce_sum.55
  91.0 1.6 %collective-permute-start = (f32[8,24,256]{2,1,0:T(8,128)S(1)}, f32[8,24,256]{2,1,0:T(8,128)S(1)}, u32[]{:S(2)}, u32[]{:S(2)}) collective-permute-start(f32[8,24,256]{2,1,0:T(8,128)S(1)} %dynamic-slice_bitcast_fusion.2), channel_id=1, source_target_pairs={{0,130},{1,131},{2,128},{3,129},{4,134},{5,135},{6,132},{7,133},{8... | collective-permute-start | bytes 589832 | tf_op jit(solution)/shard_map/ppermute | solution.py:35
  92.6 0.1 dynamic-slice_negate_fusion
  92.7 0.6 collective-permute-start.14
  93.3 6.9 %all-to-all-done.1 = f32[4,8,24,256]{3,2,1,0:T(8,128)S(1)} async-done(((f32[4,8,24,256]{3,2,1,0:T(8,128)}), f32[4,8,24,256]{3,2,1,0:T(8,128)S(1)}, u32[]{:S(2)}, u32[]{:S(2)}) %all-to-all-start.1) | async-done | bytes 786464 | tf_op jit(solution)/shard_map/all_to_all | solution.py:39
  100.2 0.1 reduce_sum.56
  100.3 0.0 collective-permute-done
  100.3 0.0 copy-start.1
  100.4 2.4 %collective-permute-start.2 = (f32[2,24,512]{2,1,0:T(8,128)S(1)}, f32[2,24,512]{2,1,0:T(8,128)S(1)}, u32[]{:S(2)}, u32[]{:S(2)}) collective-permute-start(f32[2,24,512]{2,1,0:T(8,128)S(1)} %get-tuple-element.8), channel_id=1, source_target_pairs={{0,16},{4,20},{8,24},{12,28},{16,32},{20,36},{24,40},{28,44},{32,4... | collective-permute-start | bytes 294920 | tf_op jit(solution)/shard_map/ppermute | solution.py:50
  102.8 1.7 %collective-permute-start.3 = (f32[2,24,512]{2,1,0:T(8,128)S(1)}, f32[2,24,512]{2,1,0:T(8,128)S(1)}, u32[]{:S(2)}, u32[]{:S(2)}) collective-permute-start(f32[2,24,512]{2,1,0:T(8,128)S(1)} %get-tuple-element.9), channel_id=1, source_target_pairs={{0,112},{4,116},{8,120},{12,124},{16,0},{20,4},{24,8},{28,12},{32,... | collective-permute-start | bytes 294920 | tf_op jit(solution)/shard_map/ppermute | solution.py:50
  104.6 2.8 %collective-permute-start.4 = (f32[24,256]{1,0:T(8,128)S(1)}, f32[24,256]{1,0:T(8,128)S(1)}, u32[]{:S(2)}, u32[]{:S(2)}) collective-permute-start(f32[24,256]{1,0:T(8,128)S(1)} %get-tuple-element.46), channel_id=1, source_target_pairs={{0,32},{4,36},{8,40},{12,44},{16,48},{20,52},{24,56},{28,60},{32,6... | collective-permute-start | bytes 73736 | tf_op jit(solution)/shard_map/ppermute | solution.py:50
  107.4 1.3 collective-permute-start.6
  108.7 0.0 collective-permute-done.2
  108.7 1.8 %collective-permute-done.4 = f32[24,256]{1,0:T(8,128)S(1)} collective-permute-done((f32[24,256]{1,0:T(8,128)S(1)}, f32[24,256]{1,0:T(8,128)S(1)}, u32[]{:S(2)}, u32[]{:S(2)}) %collective-permute-start.4) | collective-permute-done | bytes 24608 | tf_op jit(solution)/shard_map/ppermute | solution.py:50
  110.5 1.9 %collective-permute-start.5 = (f32[24,512]{1,0:T(8,128)S(1)}, f32[24,512]{1,0:T(8,128)S(1)}, u32[]{:S(2)}, u32[]{:S(2)}) collective-permute-start(f32[24,512]{1,0:T(8,128)S(1)} %pad_maximum_fusion.7), channel_id=1, source_target_pairs={{0,32},{4,36},{8,40},{12,44},{16,48},{20,52},{24,56},{28,60},{32,6... | collective-permute-start | bytes 147464 | tf_op jit(solution)/shard_map/ppermute | solution.py:50
  112.4 0.0 collective-permute-done.6
  112.4 2.6 %collective-permute-start.7 = (f32[24,512]{1,0:T(8,128)S(1)}, f32[24,512]{1,0:T(8,128)S(1)}, u32[]{:S(2)}, u32[]{:S(2)}) collective-permute-start(f32[24,512]{1,0:T(8,128)S(1)} %pad_maximum_fusion.8), channel_id=1, source_target_pairs={{0,96},{4,100},{8,104},{12,108},{16,112},{20,116},{24,120},{28,124... | collective-permute-start | bytes 147464 | tf_op jit(solution)/shard_map/ppermute | solution.py:50
  115.0 1.8 %collective-permute-done.5 = f32[24,512]{1,0:T(8,128)S(1)} collective-permute-done((f32[24,512]{1,0:T(8,128)S(1)}, f32[24,512]{1,0:T(8,128)S(1)}, u32[]{:S(2)}, u32[]{:S(2)}) %collective-permute-start.5) | collective-permute-done | bytes 49184 | tf_op jit(solution)/shard_map/ppermute | solution.py:50
  116.8 1.5 collective-permute-done.7
  118.3 0.1 fusion.14
  118.4 0.0 collective-permute-start.15
  118.5 1.5 collective-permute-start.16
  119.9 0.4 collective-permute-start.17
  120.3 2.7 %collective-permute-done.15 = f32[24,2,384]{2,0,1:T(8,128)S(1)} collective-permute-done((f32[24,2,384]{2,0,1:T(8,128)S(1)}, f32[24,2,384]{2,0,1:T(8,128)S(1)}, u32[]{:S(2)}, u32[]{:S(2)}) %collective-permute-start.15) | collective-permute-done | bytes 73760 | tf_op jit(solution)/shard_map/ppermute | solution.py:147
  123.0 1.5 collective-permute-done.16
  124.5 0.1 broadcast_select_fusion.7
  124.6 0.9 multiply_reduce_fusion
  125.5 0.7 broadcast_in_dim.5
  126.2 8.7 %all-to-all-start.3 = ((f32[64,8,128]{2,1,0:T(8,128)}), f32[64,8,128]{2,1,0:T(8,128)S(1)}, u32[]{:S(2)}, u32[]{:S(2)}) async-start(f32[64,8,128]{2,1,0:T(8,128)} %broadcast_in_dim.5), calls=%async_computation.3 | async-start | bytes 524288 | tf_op jit(solution)/shard_map/all_to_all | solution.py:159
  134.9 0.7 copy.11
  135.6 14.3 %all-to-all-done.3 = f32[64,8,128]{2,1,0:T(8,128)S(1)} async-done(((f32[64,8,128]{2,1,0:T(8,128)}), f32[64,8,128]{2,1,0:T(8,128)S(1)}, u32[]{:S(2)}, u32[]{:S(2)}) %all-to-all-start.3) | async-done | bytes 262176 | tf_op jit(solution)/shard_map/all_to_all | solution.py:159
  150.0 0.1 reduce_sum.59
  150.0 0.6 reshape.32
  (33 shorter events, 0.3 us)
Async XLA Ops:
  10.8 16.4 %collective-permute-start.8 = (f32[2,4,2,24,256]{4,3,2,1,0:T(8,128)S(1)}, f32[2,4,2,24,256]{4,3,2,1,0:T(8,128)S(1)}, u32[]{:S(2)}, u32[]{:S(2)}) collective-permute-start(f32[2,4,2,24,256]{4,3,2,1,0:T(8,128)S(1)} %get-tuple-element.11), channel_id=1, source_target_pairs={{0,16},{4,20},{8,24},{12,28},{16,32},{20,36},{24,40},{28,44},{32,4... | collective-permute-start | bytes 1179656 | tf_op jit(solution)/shard_map/ppermute | solution.py:50
  12.8 15.6 %collective-permute-start.9 = (f32[2,4,2,24,256]{4,3,2,1,0:T(8,128)S(1)}, f32[2,4,2,24,256]{4,3,2,1,0:T(8,128)S(1)}, u32[]{:S(2)}, u32[]{:S(2)}) collective-permute-start(f32[2,4,2,24,256]{4,3,2,1,0:T(8,128)S(1)} %get-tuple-element.12), channel_id=1, source_target_pairs={{0,112},{4,116},{8,120},{12,124},{16,0},{20,4},{24,8},{28,12},{32,... | collective-permute-start | bytes 1179656 | tf_op jit(solution)/shard_map/ppermute | solution.py:50
  16.8 13.1 %collective-permute-start.10 = (f32[4,2,24,128]{3,2,1,0:T(8,128)S(1)}, f32[4,2,24,128]{3,2,1,0:T(8,128)S(1)}, u32[]{:S(2)}, u32[]{:S(2)}) collective-permute-start(f32[4,2,24,128]{3,2,1,0:T(8,128)S(1)} %get-tuple-element.40), channel_id=1, source_target_pairs={{0,32},{4,36},{8,40},{12,44},{16,48},{20,52},{24,56},{28,60},{32,6... | collective-permute-start | bytes 294920 | tf_op jit(solution)/shard_map/ppermute | solution.py:50
  16.9 13.4 %collective-permute-start.12 = (f32[4,2,24,128]{3,2,1,0:T(8,128)S(1)}, f32[4,2,24,128]{3,2,1,0:T(8,128)S(1)}, u32[]{:S(2)}, u32[]{:S(2)}) collective-permute-start(f32[4,2,24,128]{3,2,1,0:T(8,128)S(1)} %get-tuple-element.41), channel_id=1, source_target_pairs={{0,96},{4,100},{8,104},{12,108},{16,112},{20,116},{24,120},{28,124... | collective-permute-start | bytes 294920 | tf_op jit(solution)/shard_map/ppermute | solution.py:50
  30.0 10.3 %collective-permute-start.11 = (f32[4,2,24,256]{3,2,1,0:T(8,128)S(1)}, f32[4,2,24,256]{3,2,1,0:T(8,128)S(1)}, u32[]{:S(2)}, u32[]{:S(2)}) collective-permute-start(f32[4,2,24,256]{3,2,1,0:T(8,128)S(1)} %pad_maximum_fusion.2), channel_id=1, source_target_pairs={{0,32},{4,36},{8,40},{12,44},{16,48},{20,52},{24,56},{28,60},{32,6... | collective-permute-start | bytes 589832 | tf_op jit(solution)/shard_map/ppermute | solution.py:50
  30.3 12.1 %collective-permute-start.13 = (f32[4,2,24,256]{3,2,1,0:T(8,128)S(1)}, f32[4,2,24,256]{3,2,1,0:T(8,128)S(1)}, u32[]{:S(2)}, u32[]{:S(2)}) collective-permute-start(f32[4,2,24,256]{3,2,1,0:T(8,128)S(1)} %pad_maximum_fusion.3), channel_id=1, source_target_pairs={{0,96},{4,100},{8,104},{12,108},{16,112},{20,116},{24,120},{28,124... | collective-permute-start | bytes 589832 | tf_op jit(solution)/shard_map/ppermute | solution.py:50
  44.2 18.6 %all-to-all-start.2 = ((f32[4,2,24,256]{3,2,1,0:T(8,128)}), f32[4,2,24,256]{3,2,1,0:T(8,128)S(1)}, u32[]{:S(2)}, u32[]{:S(2)}) async-start(f32[4,2,24,256]{3,2,1,0:T(8,128)} %fusion.13), calls=%async_computation.2 | async-start | bytes 393216 | tf_op jit(solution)/shard_map/all_to_all | solution.py:39
  62.7 4.9 %copy-start = (f32[2,4,8,24,256]{4,3,2,1,0:T(8,128)S(1)}, f32[2,4,8,24,256]{4,3,2,1,0:T(8,128)}, u32[]{:S(2)}) copy-start(f32[2,4,8,24,256]{4,3,2,1,0:T(8,128)} %shard_map.69) | copy-start | bytes 4718596
  62.7 23.5 %all-to-all-start = ((f32[4,2,8,24,256]{4,3,2,1,0:T(8,128)}), f32[4,2,8,24,256]{4,3,2,1,0:T(8,128)S(1)}, u32[]{:S(2)}, u32[]{:S(2)}) async-start(f32[4,2,8,24,256]{4,3,2,1,0:T(8,128)} %shard_map.68), calls=%async_computation | async-start | bytes 3145728 | tf_op jit(solution)/shard_map/all_to_all | solution.py:39
  68.6 15.5 %collective-permute-start.1 = (f32[4,8,24,256]{3,2,1,0:T(8,128)}, f32[4,8,24,256]{3,2,1,0:T(8,128)}, u32[]{:S(2)}, u32[]{:S(2)}) collective-permute-start(f32[4,8,24,256]{3,2,1,0:T(8,128)} %dynamic-slice_bitcast_fusion), channel_id=1, source_target_pairs={{0,130},{1,131},{2,128},{3,129},{4,134},{5,135},{6,132},{7,133},{8... | collective-permute-start | bytes 2359304 | tf_op jit(solution)/shard_map/ppermute | solution.py:35
  70.1 20.6 %copy-start.2 = (f32[1536]{0:T(1024)S(1)}, f32[1536]{0:T(1024)}, u32[]{:S(2)}) copy-start(f32[1536]{0:T(1024)} %param.8) | copy-start | bytes 18436
  86.2 14.0 %all-to-all-start.1 = ((f32[4,8,24,256]{3,2,1,0:T(8,128)}), f32[4,8,24,256]{3,2,1,0:T(8,128)S(1)}, u32[]{:S(2)}, u32[]{:S(2)}) async-start(f32[4,8,24,256]{3,2,1,0:T(8,128)} %bitcast_add_fusion), calls=%async_computation.1 | async-start | bytes 1572864 | tf_op jit(solution)/shard_map/all_to_all | solution.py:39
  91.0 9.3 %collective-permute-start = (f32[8,24,256]{2,1,0:T(8,128)S(1)}, f32[8,24,256]{2,1,0:T(8,128)S(1)}, u32[]{:S(2)}, u32[]{:S(2)}) collective-permute-start(f32[8,24,256]{2,1,0:T(8,128)S(1)} %dynamic-slice_bitcast_fusion.2), channel_id=1, source_target_pairs={{0,130},{1,131},{2,128},{3,129},{4,134},{5,135},{6,132},{7,133},{8... | collective-permute-start | bytes 589832 | tf_op jit(solution)/shard_map/ppermute | solution.py:35
  92.7 22.3 %collective-permute-start.14 = (f32[24,256]{1,0:T(8,128)S(1)}, f32[24,256]{1,0:T(8,128)S(1)}, u32[]{:S(2)}, u32[]{:S(2)}) collective-permute-start(f32[24,256]{1,0:T(8,128)S(1)} %dynamic-slice_bitcast_fusion.3), channel_id=1, source_target_pairs={{0,130},{1,131},{2,128},{3,129},{4,134},{5,135},{6,132},{7,133},{8... | collective-permute-start | bytes 73736 | tf_op jit(solution)/shard_map/ppermute | solution.py:35
  100.3 20.0 %copy-start.1 = (bf16[1536,512]{1,0:T(8,128)(2,1)S(1)}, bf16[1536,512]{1,0:T(8,128)(2,1)}, u32[]{:S(2)}) copy-start(bf16[1536,512]{1,0:T(8,128)(2,1)} %param.9) | copy-start | bytes 4718596
  100.4 8.3 %collective-permute-start.2 = (f32[2,24,512]{2,1,0:T(8,128)S(1)}, f32[2,24,512]{2,1,0:T(8,128)S(1)}, u32[]{:S(2)}, u32[]{:S(2)}) collective-permute-start(f32[2,24,512]{2,1,0:T(8,128)S(1)} %get-tuple-element.8), channel_id=1, source_target_pairs={{0,16},{4,20},{8,24},{12,28},{16,32},{20,36},{24,40},{28,44},{32,4... | collective-permute-start | bytes 294920 | tf_op jit(solution)/shard_map/ppermute | solution.py:50
  102.8 5.9 %collective-permute-start.3 = (f32[2,24,512]{2,1,0:T(8,128)S(1)}, f32[2,24,512]{2,1,0:T(8,128)S(1)}, u32[]{:S(2)}, u32[]{:S(2)}) collective-permute-start(f32[2,24,512]{2,1,0:T(8,128)S(1)} %get-tuple-element.9), channel_id=1, source_target_pairs={{0,112},{4,116},{8,120},{12,124},{16,0},{20,4},{24,8},{28,12},{32,... | collective-permute-start | bytes 294920 | tf_op jit(solution)/shard_map/ppermute | solution.py:50
  104.6 5.9 %collective-permute-start.4 = (f32[24,256]{1,0:T(8,128)S(1)}, f32[24,256]{1,0:T(8,128)S(1)}, u32[]{:S(2)}, u32[]{:S(2)}) collective-permute-start(f32[24,256]{1,0:T(8,128)S(1)} %get-tuple-element.46), channel_id=1, source_target_pairs={{0,32},{4,36},{8,40},{12,44},{16,48},{20,52},{24,56},{28,60},{32,6... | collective-permute-start | bytes 73736 | tf_op jit(solution)/shard_map/ppermute | solution.py:50
  107.4 5.0 %collective-permute-start.6 = (f32[24,256]{1,0:T(8,128)S(1)}, f32[24,256]{1,0:T(8,128)S(1)}, u32[]{:S(2)}, u32[]{:S(2)}) collective-permute-start(f32[24,256]{1,0:T(8,128)S(1)} %get-tuple-element.47), channel_id=1, source_target_pairs={{0,96},{4,100},{8,104},{12,108},{16,112},{20,116},{24,120},{28,124... | collective-permute-start | bytes 73736 | tf_op jit(solution)/shard_map/ppermute | solution.py:50
  110.5 6.3 %collective-permute-start.5 = (f32[24,512]{1,0:T(8,128)S(1)}, f32[24,512]{1,0:T(8,128)S(1)}, u32[]{:S(2)}, u32[]{:S(2)}) collective-permute-start(f32[24,512]{1,0:T(8,128)S(1)} %pad_maximum_fusion.7), channel_id=1, source_target_pairs={{0,32},{4,36},{8,40},{12,44},{16,48},{20,52},{24,56},{28,60},{32,6... | collective-permute-start | bytes 147464 | tf_op jit(solution)/shard_map/ppermute | solution.py:50
  112.4 5.9 %collective-permute-start.7 = (f32[24,512]{1,0:T(8,128)S(1)}, f32[24,512]{1,0:T(8,128)S(1)}, u32[]{:S(2)}, u32[]{:S(2)}) collective-permute-start(f32[24,512]{1,0:T(8,128)S(1)} %pad_maximum_fusion.8), channel_id=1, source_target_pairs={{0,96},{4,100},{8,104},{12,108},{16,112},{20,116},{24,120},{28,124... | collective-permute-start | bytes 147464 | tf_op jit(solution)/shard_map/ppermute | solution.py:50
  118.4 4.6 %collective-permute-start.15 = (f32[24,2,384]{2,0,1:T(8,128)S(1)}, f32[24,2,384]{2,0,1:T(8,128)S(1)}, u32[]{:S(2)}, u32[]{:S(2)}) collective-permute-start(f32[24,2,384]{2,0,1:T(8,128)S(1)} %fusion.14), channel_id=1, source_target_pairs={{0,3},{1,2},{2,1},{3,0},{4,7},{5,6},{6,5},{7,4},{8,11},{9,10},{10,... | collective-permute-start | bytes 221192 | tf_op jit(solution)/shard_map/ppermute | solution.py:147
  118.5 6.0 %collective-permute-start.16 = (f32[24,2,384]{2,0,1:T(8,128)S(1)}, f32[24,2,384]{2,0,1:T(8,128)S(1)}, u32[]{:S(2)}, u32[]{:S(2)}) collective-permute-start(f32[24,2,384]{2,0,1:T(8,128)S(1)} %fusion.14), channel_id=1, source_target_pairs={{0,2},{1,3},{2,0},{3,1},{4,6},{5,7},{6,4},{7,5},{8,10},{9,11},{10,... | collective-permute-start | bytes 221192 | tf_op jit(solution)/shard_map/ppermute | solution.py:147
  119.9 4.5 %collective-permute-start.17 = (f32[24,2,384]{2,0,1:T(8,128)S(1)}, f32[24,2,384]{2,0,1:T(8,128)S(1)}, u32[]{:S(2)}, u32[]{:S(2)}) collective-permute-start(f32[24,2,384]{2,0,1:T(8,128)S(1)} %fusion.14), channel_id=1, source_target_pairs={{0,1},{1,0},{2,3},{3,2},{4,5},{5,4},{6,7},{7,6},{8,9},{9,8},{10,11... | collective-permute-start | bytes 221192 | tf_op jit(solution)/shard_map/ppermute | solution.py:147
  126.2 23.7 %all-to-all-start.3 = ((f32[64,8,128]{2,1,0:T(8,128)}), f32[64,8,128]{2,1,0:T(8,128)S(1)}, u32[]{:S(2)}, u32[]{:S(2)}) async-start(f32[64,8,128]{2,1,0:T(8,128)} %broadcast_in_dim.5), calls=%async_computation.3 | async-start | bytes 524288 | tf_op jit(solution)/shard_map/all_to_all | solution.py:159
where the time goes:
time: 152 us; the launch traced here: 151 us
  waiting for transfers between devices  60.4 us (40%)
  starting transfers between devices  55.4 us (36%)
  Pallas kernels  21.1 us (14%)
  other arithmetic  6.66 us (4%)
  local copies, waits for them, and re-layouts  5.16 us (3%)
    ppermute x12, starting transfers between devices, send(): return lax.ppermute(part, 'pair', z_perm(dz))  27.2 us
    ppermute x12, waiting for transfers between devices, send(): return lax.ppermute(part, 'pair', z_perm(dz))  21.1 us
    pallas_call x3, Pallas kernels, chi_columns(): pl.pallas_call(body, grid_spec=pltpu.PrefetchScalarGridSpec(num_scalar_pr...  21.1 us
    all_to_all x1, waiting for transfers between devices, local(): lax.all_to_all(spread, 'pair', 0, 0, tiled=True)  14.3 us
    ppermute x3, waiting for transfers between devices, x_swap(): lax.ppermute(away, ('pair', 'sigma'), moves)  14 us
    all_to_all x3, starting transfers between devices, y_sum(): lax.all_to_all(block, 'pair', 0, 0, axis_index_groups=Y_GROUPS, tiled=True)  13.9 us
    all_to_all x1, starting transfers between devices, local(): lax.all_to_all(spread, 'pair', 0, 0, tiled=True)  8.67 us
    all_to_all x3, waiting for transfers between devices, y_sum(): lax.all_to_all(block, 'pair', 0, 0, axis_index_groups=Y_GROUPS, tiled=True)  6.92 us
  transfers between devices with their start and end apart: 22, of which 13 were waited for; matrix products, arithmetic and copies ran while one was open for 4% of the time, Pallas kernels for 9%

commit v1 on v0

v1 whole, which is shorter than its diff:
```python
import jax
import jax.numpy as jnp
from jax import lax
from jax.experimental import pallas as pl
from jax.experimental.pallas import tpu as pltpu
from jax.sharding import PartitionSpec as P


NX, NZ, NY = 2, 8, 4
COLUMNS = 256
STEP = 384
Z_ORDER = (4, 1, 3, -1, -3, 0, 2, -2)
Y_GROUPS = [[base + y for y in range(NY)] for base in range(0, NX * NZ * NY, NY)]


def place(position):
    return position // (NZ * NY), position // NY % NZ, position % NY


def z_perm(dz):
    moves = []
    for position in range(NX * NZ * NY):
        x, z, y = place(position)
        moves.append((position, (x * NZ + (z + dz) % NZ) * NY + y))
    return moves


def x_swap(away, keep):
    pair_count, sigma_count = lax.axis_size("pair"), lax.axis_size("sigma")
    moves = [
        (p * sigma_count + s, (p ^ (NZ * NY)) * sigma_count + (s ^ 2))
        for p in range(pair_count)
        for s in range(sigma_count)
    ]
    return keep + lax.ppermute(away, ("pair", "sigma"), moves)


def y_sum(block):
    return jnp.sum(lax.all_to_all(block, "pair", 0, 0, axis_index_groups=Y_GROUPS, tiled=True), axis=0)


def z_sum(low, high, up, down, keep):
    half = low.shape[-1]

    def send(part, dz):
        return lax.ppermute(part, "pair", z_perm(dz))

    low, high = send(low, -2), send(high, 2)
    up, down = send(up, 1), send(down, -1)
    above, below = keep[1] + up[1], keep[2] + down[1]
    above = jnp.concatenate([above[..., :half], above[..., half:] + high], axis=-1)
    below = jnp.concatenate([below[..., :half] + low, below[..., half:]], axis=-1)
    return keep[0] + up[0] + down[0] + send(above, 2) + send(below, -2)


def chi_columns(pairs, spot, weight, first, shapes, stores):
    pair_local, width = pairs.shape
    col_count = width // 4
    row_count = width // (NX * NZ * NY)
    steps = width // STEP

    def body(spot_ref, pair_ref, slab_ref, weight_ref, *refs):
        outs, scaled_ref, rows_ref = refs[: len(shapes)], refs[-2], refs[-1]
        step = pl.program_id(0)

        @pl.when(step == 0)
        def _():
            for t in range(COLUMNS // 128):
                f, column = divmod(first + 128 * t, col_count)
                turned = jnp.transpose(slab_ref[:, column : column + 128]).astype(jnp.float32)
                scaled_ref[128 * t : 128 * t + 128, :] = (weight_ref[f : f + 1, :] * turned).astype(jnp.bfloat16)

        result = jnp.dot(scaled_ref[...], pair_ref[...], preferred_element_type=jnp.float32)
        rows_ref[pl.ds(pl.multiple_of(step * STEP, STEP), STEP), :] = jnp.transpose(result)

        @pl.when(step == steps - 1)
        def _():
            x, z = spot_ref[1], spot_ref[2]
            for out, index, columns, keeps, dz, y in stores:
                at = ((x if keeps else 1 - x) * NZ + ((z + dz) & (NZ - 1))) * NY + y
                outs[out][index] = rows_ref[pl.ds(pl.multiple_of(at * row_count, 8), row_count), columns]

    whole = lambda shape: pl.BlockSpec(shape, lambda i, spot: (0,) * len(shape))
    return pl.pallas_call(
        body,
        grid_spec=pltpu.PrefetchScalarGridSpec(
            num_scalar_prefetch=1,
            grid=(steps,),
            in_specs=[
                pl.BlockSpec((pair_local, STEP), lambda i, spot: (0, i)),
                pl.BlockSpec((pair_local, col_count), lambda i, spot: (0, spot[0])),
                whole(weight.shape),
            ],
            out_specs=[whole(shape) for shape in shapes],
            scratch_shapes=[
                pltpu.VMEM((COLUMNS, pair_local), jnp.bfloat16),
                pltpu.VMEM((width, COLUMNS), jnp.float32),
            ],
        ),
        out_shape=[jax.ShapeDtypeStruct(shape, jnp.float32) for shape in shapes],
    )(spot, pairs, pairs, weight)


def local(pair_density_matrices, energy_bins, bin_weights, coulomb, state_matrices):
    pair_local, width = pair_density_matrices.shape
    pair_count = lax.axis_size("pair")
    sigma_count = lax.axis_size("sigma")
    row_count = width // pair_count
    col_count = width // sigma_count
    pair_position = lax.axis_index("pair")
    sigma_position = lax.axis_index("sigma")
    x = pair_position // (NZ * NY)
    quarter = sigma_position ^ (2 * x)

    bins = energy_bins.T
    bin_levels = jnp.arange(bin_weights.shape[1], dtype=jnp.int32)
    matches = (bins[:, None, :] == bin_levels[None, :, None]).astype(jnp.float32)
    weight = jnp.sum(matches * bin_weights[:, :, None], axis=1) / jnp.float32(pair_local * pair_count)
    spot = jnp.stack([quarter, x, pair_position // NY % NZ]).astype(jnp.int32)

    def columns(first, shapes, stores):
        return chi_columns(pair_density_matrices, spot, weight, first, shapes, stores)

    rc, n, half = row_count, COLUMNS, COLUMNS // 2
    every = slice(None)
    spots = [(y, keeps, k) for y in range(NY) for keeps in (0, 1) for k in range(NZ)]
    c = columns(n, [(NY, NZ, rc, n)] * 2, [(keeps, (y, k), every, keeps, Z_ORDER[k], y) for y, keeps, k in spots])
    b = columns(0, [(NY, NX, NZ, rc, n)], [(0, (y, keeps, k), every, keeps, Z_ORDER[k], y) for y, keeps, k in spots])[0]
    stores = []
    for y, keeps, k in spots:
        if Z_ORDER[k] == 4:
            stores += [(0, (y, keeps), slice(0, half), keeps, 4, y), (1, (y, keeps), slice(half, n), keeps, 4, y)]
        else:
            out, slot = divmod(k - 1, 2) if k < 5 else (2, k - 5)
            stores.append((2 + out, (slot, y, keeps), every, keeps, Z_ORDER[k], y))
    a = columns(2 * n, [(NY, NX, rc, half)] * 2 + [(k, NY, NX, rc, n) for k in (2, 2, 3)], stores)

    c = y_sum(x_swap(*c))
    b = x_swap(*y_sum(b))
    bc = jnp.concatenate([b, c], axis=2)
    bc = lax.optimization_barrier((bc[0, :, :n], bc[0, :, n:], bc[1:3], bc[3:5], bc[5:]))
    bc = z_sum(*bc)
    a = x_swap(*y_sum(z_sum(*a)))
    polar = jnp.concatenate([bc, a], axis=1)

    root = jnp.sqrt(coulomb)
    root_rows = lax.dynamic_slice_in_dim(root, pair_position * row_count, row_count, 0)
    root_columns = lax.dynamic_slice_in_dim(root, quarter * col_count, col_count, 0)
    screened = -root_rows[:, None, None] * polar.reshape(row_count, -1, col_count) * root_columns[None, None, :]
    parts = [screened] + [
        lax.ppermute(screened, "sigma", [(s, s ^ k) for s in range(sigma_count)]) for k in range(1, sigma_count)
    ]
    for bit in (1, 2):
        odd = (quarter & bit) != 0
        parts = [jnp.where(odd, parts[k ^ bit], parts[k]) for k in range(sigma_count)]
    states_wide = state_matrices.astype(jnp.float32)
    applied = jnp.einsum(
        "rfc,cn->rfn", jnp.concatenate(parts, axis=2), states_wide, precision=lax.Precision.HIGHEST
    )
    own_states = lax.dynamic_slice_in_dim(states_wide, pair_position * row_count, row_count, 0)
    total = jnp.sum(own_states[:, None, :] * applied, axis=0) / jnp.float32(width)
    spread = jnp.broadcast_to(total.reshape(8, -1)[None], (pair_count, 8, total.size // 8))
    total = jnp.sum(lax.all_to_all(spread, "pair", 0, 0, tiled=True), axis=0).reshape(total.shape)
    return (applied, total)


def solution(mesh):
    return jax.shard_map(
        local,
        mesh=mesh,
        in_specs=(P("pair", None), P("pair", None), P(), P(), P(None, "sigma")),
        out_specs=(P("pair", None, "sigma"), P(None, "sigma")),
        check_vma=False,
    )
```

time: 152 us -> 133 us (0.88)
  waiting for transfers between devices: 60.4 us -> 45.5 us
  Pallas kernels: 21.1 us -> 24.5 us
  starting transfers between devices: 55.4 us -> 52.2 us
  local copies, waits for them, and re-layouts: 5.16 us -> 2.18 us
    ppermute x3, waiting for transfers between devices: 14 us -> 0.01 us  [x_swap(): return keep + lax.ppermute(away, ('pair', 'sigma'), moves)]
    ppermute x12, waiting for transfers between devices: 21.1 us -> 13.4 us  [send(): return lax.ppermute(part, 'pair', z_perm(dz))]
    all_to_all x3, waiting for transfers between devices: 6.92 us -> 13.4 us  [y_sum(): lax.all_to_all(block, 'pair', 0, 0, axis_index_groups=Y_GROUPS, tiled=True)]
    pallas_call x3, Pallas kernels: 21.1 us -> 24.5 us  [chi_columns(): pl.pallas_call(body, grid_spec=pltpu.PrefetchScalarGridSpec(num_scalar_pr...]
    add x7, other arithmetic: 4.93 us -> 3 us  [the longest x3 2.17 us: x_swap(): return keep + lax.ppermute(away, ('pair', 'sigma'), moves)]
  transfers between devices with their start and end apart: 22 -> 22, of which waited for: 13 -> 11; matrix products, arithmetic and copies ran while one was open for 4% -> 3% of each run, Pallas kernels for 9% -> 12%
where the time goes in v1:
time: 133 us; the launch traced here: 132 us
  starting transfers between devices  52.2 us (39%)
  waiting for transfers between devices  45.5 us (34%)
  Pallas kernels  24.5 us (18%)
  other arithmetic  5.81 us (4%)
  local copies, waits for them, and re-layouts  2.18 us (2%)
    ppermute x12, starting transfers between devices, send(): return lax.ppermute(part, 'pair', z_perm(dz))  25.9 us
    pallas_call x3, Pallas kernels, chi_columns(): pl.pallas_call(body, grid_spec=pltpu.PrefetchScalarGridSpec(num_scalar_pr...  24.5 us
    all_to_all x1, waiting for transfers between devices, local(): lax.all_to_all(spread, 'pair', 0, 0, tiled=True)  14.5 us
    all_to_all x3, waiting for transfers between devices, y_sum(): lax.all_to_all(block, 'pair', 0, 0, axis_index_groups=Y_GROUPS, tiled=True)  13.4 us
    ppermute x12, waiting for transfers between devices, send(): return lax.ppermute(part, 'pair', z_perm(dz))  13.4 us
    all_to_all x3, starting transfers between devices, y_sum(): lax.all_to_all(block, 'pair', 0, 0, axis_index_groups=Y_GROUPS, tiled=True)  12.8 us
    all_to_all x1, starting transfers between devices, local(): lax.all_to_all(spread, 'pair', 0, 0, tiled=True)  7.79 us
    ppermute x3, waiting for transfers between devices, local(): lax.ppermute(screened, 'sigma', [(s, s ^ k) for s in range(sigma_count)])  4.22 us
  transfers between devices with their start and end apart: 22, of which 11 were waited for; matrix products, arithmetic and copies ran while one was open for 3% of the time, Pallas kernels for 12%

profile of v1, /device:TPU:2, one launch (start us, length us, event | category | flops | bytes accessed | tf_op | source)
XLA Modules:
  0.0 132.1 jit_solution(4113024332812633365)
XLA Ops:
  0.7 1.0 select_reduce_fusion
  1.7 0.6 broadcast_multiply_fusion.weight_ref
  2.3 0.6 pad_add_fusion.spot_ref
  2.8 8.2 %shard_map.70 = (f32[4,2,24,128]{3,2,1,0:T(8,128)}, f32[4,2,24,128]{3,2,1,0:T(8,128)}, f32[2,4,2,24,256]{4,3,2,1,0:T(8,128)}, f32[2,4,2,24,256]{4,3,2,1,0:T(8,128)}, f32[3,4,2,24,256]{4,3,2,1,0:T(8,128)}) custom-call(s32[3]{0:T(128)} %pad_add_fusion.spot_ref, bf16[2048,1536]{1,0:T(8,128)(2,1)} %slab_ref.5, bf16[2048,1536]{1,0:T(8,128)(2,1)} %slab_ref.5, ...), custom_call_target="tpu_custom_call" | custom-call | tf_op jit(solution)/shard_map/pallas_call | solution.py:84
  11.0 1.9 %collective-permute-start.8 = (f32[2,4,2,24,256]{4,3,2,1,0:T(8,128)}, f32[2,4,2,24,256]{4,3,2,1,0:T(8,128)S(1)}, u32[]{:S(2)}, u32[]{:S(2)}) collective-permute-start(f32[2,4,2,24,256]{4,3,2,1,0:T(8,128)} %get-tuple-element.22), channel_id=1, source_target_pairs={{0,16},{4,20},{8,24},{12,28},{16,32},{20,36},{24,40},{28,44},{32,4... | collective-permute-start | bytes 1179656 | tf_op jit(solution)/shard_map/ppermute | solution.py:46
  12.9 3.9 %collective-permute-start.9 = (f32[2,4,2,24,256]{4,3,2,1,0:T(8,128)}, f32[2,4,2,24,256]{4,3,2,1,0:T(8,128)S(1)}, u32[]{:S(2)}, u32[]{:S(2)}) collective-permute-start(f32[2,4,2,24,256]{4,3,2,1,0:T(8,128)} %get-tuple-element.23), channel_id=1, source_target_pairs={{0,112},{4,116},{8,120},{12,124},{16,0},{20,4},{24,8},{28,12},{32,... | collective-permute-start | bytes 1179656 | tf_op jit(solution)/shard_map/ppermute | solution.py:46
  16.9 8.2 %shard_map.68 = f32[4,2,8,24,256]{4,3,2,1,0:T(8,128)} custom-call(s32[3]{0:T(128)} %pad_add_fusion.spot_ref, bf16[2048,1536]{1,0:T(8,128)(2,1)} %slab_ref.5, bf16[2048,1536]{1,0:T(8,128)(2,1)} %slab_ref.5, f32[2,2048]{1,0:T(2,128)} %broadcast_multiply_fusion.weight_ref), custom_call_target="tpu_custom_call" | custom-call | tf_op jit(solution)/shard_map/pallas_call | solution.py:84
  25.0 4.6 %all-to-all-start = ((f32[4,2,8,24,256]{4,3,2,1,0:T(8,128)}), f32[4,2,8,24,256]{4,3,2,1,0:T(8,128)S(1)}, u32[]{:S(2)}, u32[]{:S(2)}) async-start(f32[4,2,8,24,256]{4,3,2,1,0:T(8,128)} %shard_map.68), calls=%async_computation | async-start | bytes 3145728 | tf_op jit(solution)/shard_map/all_to_all | solution.py:39
  29.6 0.0 collective-permute-start.10
  29.7 4.1 %collective-permute-start.12 = (f32[4,2,24,128]{3,2,1,0:T(8,128)S(1)}, f32[4,2,24,128]{3,2,1,0:T(8,128)S(1)}, u32[]{:S(2)}, u32[]{:S(2)}) collective-permute-start(f32[4,2,24,128]{3,2,1,0:T(8,128)S(1)} %copy-done.4), channel_id=1, source_target_pairs={{0,96},{4,100},{8,104},{12,108},{16,112},{20,116},{24,120},{28,124... | collective-permute-start | bytes 294920 | tf_op jit(solution)/shard_map/ppermute | solution.py:46
  33.8 8.1 %shard_map.69 = (f32[4,8,24,256]{3,2,1,0:T(8,128)}, f32[4,8,24,256]{3,2,1,0:T(8,128)}) custom-call(s32[3]{0:T(128)} %pad_add_fusion.spot_ref, bf16[2048,1536]{1,0:T(8,128)(2,1)} %slab_ref.5, bf16[2048,1536]{1,0:T(8,128)(2,1)} %slab_ref.5, f32[2,2048]{1,0:T(2,128)} %broadcast_multiply_fusion.weight_ref), custom_call_target="tpu_custom_call" | custom-call | tf_op jit(solution)/shard_map/pallas_call | solution.py:84
  41.9 1.5 %collective-permute-start.1 = (f32[4,8,24,256]{3,2,1,0:T(8,128)}, f32[4,8,24,256]{3,2,1,0:T(8,128)}, u32[]{:S(2)}, u32[]{:S(2)}) collective-permute-start(f32[4,8,24,256]{3,2,1,0:T(8,128)} %get-tuple-element.15), channel_id=1, source_target_pairs={{0,130},{1,131},{2,128},{3,129},{4,134},{5,135},{6,132},{7,133},{8... | collective-permute-start | bytes 2359304 | tf_op jit(solution)/shard_map/ppermute | solution.py:35
  43.4 0.0 collective-permute-done.8
  43.4 0.0 collective-permute-done.9
  43.4 0.1 fusion.10
  43.5 0.0 collective-permute-done.10
  43.5 0.0 collective-permute-done.12
  43.6 1.2 collective-permute-start.11
  44.8 3.1 %collective-permute-start.13 = (f32[4,2,24,256]{3,2,1,0:T(8,128)S(1)}, f32[4,2,24,256]{3,2,1,0:T(8,128)S(1)}, u32[]{:S(2)}, u32[]{:S(2)}) collective-permute-start(f32[4,2,24,256]{3,2,1,0:T(8,128)S(1)} %pad_maximum_fusion.1), channel_id=1, source_target_pairs={{0,96},{4,100},{8,104},{12,108},{16,112},{20,116},{24,120},{28,124... | collective-permute-start | bytes 589832 | tf_op jit(solution)/shard_map/ppermute | solution.py:46
  47.9 6.1 %collective-permute-done.11 = f32[4,2,24,256]{3,2,1,0:T(8,128)S(1)} collective-permute-done((f32[4,2,24,256]{3,2,1,0:T(8,128)S(1)}, f32[4,2,24,256]{3,2,1,0:T(8,128)S(1)}, u32[]{:S(2)}, u32[]{:S(2)}) %collective-permute-start.11) | collective-permute-done | bytes 196640 | tf_op jit(solution)/shard_map/ppermute | solution.py:46
  54.0 1.3 collective-permute-done.13
  55.3 0.7 fusion.13
  56.0 0.0 all-to-all-done
  56.0 4.7 %all-to-all-start.2 = ((f32[4,2,24,256]{3,2,1,0:T(8,128)}), f32[4,2,24,256]{3,2,1,0:T(8,128)S(1)}, u32[]{:S(2)}, u32[]{:S(2)}) async-start(f32[4,2,24,256]{3,2,1,0:T(8,128)} %fusion.13), calls=%async_computation.2 | async-start | bytes 393216 | tf_op jit(solution)/shard_map/all_to_all | solution.py:39
  60.7 0.1 reduce_sum.55
  60.9 0.6 collective-permute-start
  61.5 0.0 collective-permute-done.1
  61.5 2.1 %add.93 = f32[4,8,24,256]{3,2,1,0:T(8,128)} add(f32[4,8,24,256]{3,2,1,0:T(8,128)S(1)} %copy-done.1, f32[4,8,24,256]{3,2,1,0:T(8,128)} %collective-permute-done.1) | non-fusion elementwise | flops 196608 | bytes 2359296 | tf_op jit(solution)/shard_map/add | solution.py:35
  63.6 3.4 %all-to-all-done.2 = f32[4,2,24,256]{3,2,1,0:T(8,128)S(1)} async-done(((f32[4,2,24,256]{3,2,1,0:T(8,128)}), f32[4,2,24,256]{3,2,1,0:T(8,128)S(1)}, u32[]{:S(2)}, u32[]{:S(2)}) %all-to-all-start.2) | async-done | bytes 196640 | tf_op jit(solution)/shard_map/all_to_all | solution.py:39
  67.0 3.5 %all-to-all-start.1 = ((f32[4,8,24,256]{3,2,1,0:T(8,128)}), f32[4,8,24,256]{3,2,1,0:T(8,128)S(1)}, u32[]{:S(2)}, u32[]{:S(2)}) async-start(f32[4,8,24,256]{3,2,1,0:T(8,128)} %add.93), calls=%async_computation.1 | async-start | bytes 1572864 | tf_op jit(solution)/shard_map/all_to_all | solution.py:39
  70.6 0.1 dynamic_slice.10
  70.7 0.1 dynamic-slice_negate_fusion
  70.8 0.0 collective-permute-done
  70.8 0.0 copy-start
  70.8 10.0 %all-to-all-done.1 = f32[4,8,24,256]{3,2,1,0:T(8,128)S(1)} async-done(((f32[4,8,24,256]{3,2,1,0:T(8,128)}), f32[4,8,24,256]{3,2,1,0:T(8,128)S(1)}, u32[]{:S(2)}, u32[]{:S(2)}) %all-to-all-start.1) | async-done | bytes 786464 | tf_op jit(solution)/shard_map/all_to_all | solution.py:39
  80.8 0.1 reduce_sum.56
  80.9 0.1 collective-permute-start.2
  81.0 3.2 %collective-permute-start.3 = (f32[2,24,512]{2,1,0:T(8,128)S(1)}, f32[2,24,512]{2,1,0:T(8,128)S(1)}, u32[]{:S(2)}, u32[]{:S(2)}) collective-permute-start(f32[2,24,512]{2,1,0:T(8,128)S(1)} %get-tuple-element.18), channel_id=1, source_target_pairs={{0,112},{4,116},{8,120},{12,124},{16,0},{20,4},{24,8},{28,12},{32,... | collective-permute-start | bytes 294920 | tf_op jit(solution)/shard_map/ppermute | solution.py:46
  84.3 0.5 collective-permute-start.14
  84.8 2.0 %collective-permute-start.4 = (f32[24,256]{1,0:T(8,128)S(1)}, f32[24,256]{1,0:T(8,128)S(1)}, u32[]{:S(2)}, u32[]{:S(2)}) collective-permute-start(f32[24,256]{1,0:T(8,128)S(1)} %slice_bitcast_fusion.4), channel_id=1, source_target_pairs={{0,32},{4,36},{8,40},{12,44},{16,48},{20,52},{24,56},{28,60},{32,6... | collective-permute-start | bytes 73736 | tf_op jit(solution)/shard_map/ppermute | solution.py:46
  86.8 2.2 %collective-permute-start.6 = (f32[24,256]{1,0:T(8,128)S(1)}, f32[24,256]{1,0:T(8,128)S(1)}, u32[]{:S(2)}, u32[]{:S(2)}) collective-permute-start(f32[24,256]{1,0:T(8,128)S(1)} %slice_bitcast_fusion.5), channel_id=1, source_target_pairs={{0,96},{4,100},{8,104},{12,108},{16,112},{20,116},{24,120},{28,124... | collective-permute-start | bytes 73736 | tf_op jit(solution)/shard_map/ppermute | solution.py:46
  88.9 0.0 collective-permute-done.2
  89.0 2.1 %collective-permute-done.4 = f32[24,256]{1,0:T(8,128)S(1)} collective-permute-done((f32[24,256]{1,0:T(8,128)S(1)}, f32[24,256]{1,0:T(8,128)S(1)}, u32[]{:S(2)}, u32[]{:S(2)}) %collective-permute-start.4) | collective-permute-done | bytes 24608 | tf_op jit(solution)/shard_map/ppermute | solution.py:46
  91.0 0.5 collective-permute-done.6
  91.6 2.5 %collective-permute-start.5 = (f32[24,512]{1,0:T(8,128)S(1)}, f32[24,512]{1,0:T(8,128)S(1)}, u32[]{:S(2)}, u32[]{:S(2)}) collective-permute-start(f32[24,512]{1,0:T(8,128)S(1)} %pad_maximum_fusion.6), channel_id=1, source_target_pairs={{0,32},{4,36},{8,40},{12,44},{16,48},{20,52},{24,56},{28,60},{32,6... | collective-permute-start | bytes 147464 | tf_op jit(solution)/shard_map/ppermute | solution.py:46
  94.1 1.7 %collective-permute-start.7 = (f32[24,512]{1,0:T(8,128)S(1)}, f32[24,512]{1,0:T(8,128)S(1)}, u32[]{:S(2)}, u32[]{:S(2)}) collective-permute-start(f32[24,512]{1,0:T(8,128)S(1)} %pad_maximum_fusion.7), channel_id=1, source_target_pairs={{0,96},{4,100},{8,104},{12,108},{16,112},{20,116},{24,120},{28,124... | collective-permute-start | bytes 147464 | tf_op jit(solution)/shard_map/ppermute | solution.py:46
  95.8 0.0 collective-permute-done.14
  95.8 2.0 %collective-permute-done.5 = f32[24,512]{1,0:T(8,128)S(1)} collective-permute-done((f32[24,512]{1,0:T(8,128)S(1)}, f32[24,512]{1,0:T(8,128)S(1)}, u32[]{:S(2)}, u32[]{:S(2)}) %collective-permute-start.5) | collective-permute-done | bytes 49184 | tf_op jit(solution)/shard_map/ppermute | solution.py:46
  97.9 1.3 %collective-permute-done.7 = f32[24,512]{1,0:T(8,128)S(1)} collective-permute-done((f32[24,512]{1,0:T(8,128)S(1)}, f32[24,512]{1,0:T(8,128)S(1)}, u32[]{:S(2)}, u32[]{:S(2)}) %collective-permute-start.7) | collective-permute-done | bytes 49184 | tf_op jit(solution)/shard_map/ppermute | solution.py:46
  99.2 0.1 fusion.15
  99.3 0.0 collective-permute-start.17
  99.4 3.0 %collective-permute-start.16 = (f32[24,2,384]{2,0,1:T(8,128)S(1)}, f32[24,2,384]{2,0,1:T(8,128)S(1)}, u32[]{:S(2)}, u32[]{:S(2)}) collective-permute-start(f32[24,2,384]{2,0,1:T(8,128)S(1)} %fusion.15), channel_id=1, source_target_pairs={{0,2},{1,3},{2,0},{3,1},{4,6},{5,7},{6,4},{7,5},{8,10},{9,11},{10,... | collective-permute-start | bytes 221192 | tf_op jit(solution)/shard_map/ppermute | solution.py:151
  102.4 0.0 collective-permute-start.15
  102.4 0.0 collective-permute-done.17
  102.4 2.8 %collective-permute-done.16 = f32[24,2,384]{2,0,1:T(8,128)S(1)} collective-permute-done((f32[24,2,384]{2,0,1:T(8,128)S(1)}, f32[24,2,384]{2,0,1:T(8,128)S(1)}, u32[]{:S(2)}, u32[]{:S(2)}) %collective-permute-start.16) | collective-permute-done | bytes 73760 | tf_op jit(solution)/shard_map/ppermute | solution.py:151
  105.2 1.4 %collective-permute-done.15 = f32[24,2,384]{2,0,1:T(8,128)S(1)} collective-permute-done((f32[24,2,384]{2,0,1:T(8,128)S(1)}, f32[24,2,384]{2,0,1:T(8,128)S(1)}, u32[]{:S(2)}, u32[]{:S(2)}) %collective-permute-start.15) | collective-permute-done | bytes 73760 | tf_op jit(solution)/shard_map/ppermute | solution.py:151
  106.7 0.1 broadcast_select_fusion.7
  106.7 0.9 multiply_reduce_fusion
  107.7 0.7 broadcast_in_dim.2
  108.4 7.8 %all-to-all-start.3 = ((f32[64,8,128]{2,1,0:T(8,128)}), f32[64,8,128]{2,1,0:T(8,128)S(1)}, u32[]{:S(2)}, u32[]{:S(2)}) async-start(f32[64,8,128]{2,1,0:T(8,128)} %broadcast_in_dim.2), calls=%async_computation.3 | async-start | bytes 524288 | tf_op jit(solution)/shard_map/all_to_all | solution.py:163
  116.2 0.7 copy.11
  116.9 14.5 %all-to-all-done.3 = f32[64,8,128]{2,1,0:T(8,128)S(1)} async-done(((f32[64,8,128]{2,1,0:T(8,128)}), f32[64,8,128]{2,1,0:T(8,128)S(1)}, u32[]{:S(2)}, u32[]{:S(2)}) %all-to-all-start.3) | async-done | bytes 262176 | tf_op jit(solution)/shard_map/all_to_all | solution.py:163
  131.4 0.1 reduce_sum.59
  131.5 0.6 reshape.32
  (34 shorter events, 0.3 us)
Async XLA Ops:
  11.0 32.4 %collective-permute-start.8 = (f32[2,4,2,24,256]{4,3,2,1,0:T(8,128)}, f32[2,4,2,24,256]{4,3,2,1,0:T(8,128)S(1)}, u32[]{:S(2)}, u32[]{:S(2)}) collective-permute-start(f32[2,4,2,24,256]{4,3,2,1,0:T(8,128)} %get-tuple-element.22), channel_id=1, source_target_pairs={{0,16},{4,20},{8,24},{12,28},{16,32},{20,36},{24,40},{28,44},{32,4... | collective-permute-start | bytes 1179656 | tf_op jit(solution)/shard_map/ppermute | solution.py:46
  12.9 30.5 %collective-permute-start.9 = (f32[2,4,2,24,256]{4,3,2,1,0:T(8,128)}, f32[2,4,2,24,256]{4,3,2,1,0:T(8,128)S(1)}, u32[]{:S(2)}, u32[]{:S(2)}) collective-permute-start(f32[2,4,2,24,256]{4,3,2,1,0:T(8,128)} %get-tuple-element.23), channel_id=1, source_target_pairs={{0,112},{4,116},{8,120},{12,124},{16,0},{20,4},{24,8},{28,12},{32,... | collective-permute-start | bytes 1179656 | tf_op jit(solution)/shard_map/ppermute | solution.py:46
  25.0 4.6 %copy-start.5 = (f32[4,2,24,128]{3,2,1,0:T(8,128)S(1)}, f32[4,2,24,128]{3,2,1,0:T(8,128)}, u32[]{:S(2)}) copy-start(f32[4,2,24,128]{3,2,1,0:T(8,128)} %get-tuple-element.24) | copy-start | bytes 294916
  25.0 4.6 %copy-start.4 = (f32[4,2,24,128]{3,2,1,0:T(8,128)S(1)}, f32[4,2,24,128]{3,2,1,0:T(8,128)}, u32[]{:S(2)}) copy-start(f32[4,2,24,128]{3,2,1,0:T(8,128)} %get-tuple-element.25) | copy-start | bytes 294916
  25.0 31.0 %all-to-all-start = ((f32[4,2,8,24,256]{4,3,2,1,0:T(8,128)}), f32[4,2,8,24,256]{4,3,2,1,0:T(8,128)S(1)}, u32[]{:S(2)}, u32[]{:S(2)}) async-start(f32[4,2,8,24,256]{4,3,2,1,0:T(8,128)} %shard_map.68), calls=%async_computation | async-start | bytes 3145728 | tf_op jit(solution)/shard_map/all_to_all | solution.py:39
  29.6 13.9 %collective-permute-start.10 = (f32[4,2,24,128]{3,2,1,0:T(8,128)S(1)}, f32[4,2,24,128]{3,2,1,0:T(8,128)S(1)}, u32[]{:S(2)}, u32[]{:S(2)}) collective-permute-start(f32[4,2,24,128]{3,2,1,0:T(8,128)S(1)} %copy-done.5), channel_id=1, source_target_pairs={{0,32},{4,36},{8,40},{12,44},{16,48},{20,52},{24,56},{28,60},{32,6... | collective-permute-start | bytes 294920 | tf_op jit(solution)/shard_map/ppermute | solution.py:46
  29.6 13.8 %copy-start.2 = (f32[3,4,2,24,256]{4,3,2,1,0:T(8,128)S(1)}, f32[3,4,2,24,256]{4,3,2,1,0:T(8,128)}, u32[]{:S(2)}) copy-start(f32[3,4,2,24,256]{4,3,2,1,0:T(8,128)} %get-tuple-element.21) | copy-start | bytes 1769476
  29.7 13.8 %collective-permute-start.12 = (f32[4,2,24,128]{3,2,1,0:T(8,128)S(1)}, f32[4,2,24,128]{3,2,1,0:T(8,128)S(1)}, u32[]{:S(2)}, u32[]{:S(2)}) collective-permute-start(f32[4,2,24,128]{3,2,1,0:T(8,128)S(1)} %copy-done.4), channel_id=1, source_target_pairs={{0,96},{4,100},{8,104},{12,108},{16,112},{20,116},{24,120},{28,124... | collective-permute-start | bytes 294920 | tf_op jit(solution)/shard_map/ppermute | solution.py:46
  41.9 19.6 %collective-permute-start.1 = (f32[4,8,24,256]{3,2,1,0:T(8,128)}, f32[4,8,24,256]{3,2,1,0:T(8,128)}, u32[]{:S(2)}, u32[]{:S(2)}) collective-permute-start(f32[4,8,24,256]{3,2,1,0:T(8,128)} %get-tuple-element.15), channel_id=1, source_target_pairs={{0,130},{1,131},{2,128},{3,129},{4,134},{5,135},{6,132},{7,133},{8... | collective-permute-start | bytes 2359304 | tf_op jit(solution)/shard_map/ppermute | solution.py:35
  43.6 10.4 %collective-permute-start.11 = (f32[4,2,24,256]{3,2,1,0:T(8,128)S(1)}, f32[4,2,24,256]{3,2,1,0:T(8,128)S(1)}, u32[]{:S(2)}, u32[]{:S(2)}) collective-permute-start(f32[4,2,24,256]{3,2,1,0:T(8,128)S(1)} %pad_maximum_fusion), channel_id=1, source_target_pairs={{0,32},{4,36},{8,40},{12,44},{16,48},{20,52},{24,56},{28,60},{32,6... | collective-permute-start | bytes 589832 | tf_op jit(solution)/shard_map/ppermute | solution.py:46
  44.8 10.5 %collective-permute-start.13 = (f32[4,2,24,256]{3,2,1,0:T(8,128)S(1)}, f32[4,2,24,256]{3,2,1,0:T(8,128)S(1)}, u32[]{:S(2)}, u32[]{:S(2)}) collective-permute-start(f32[4,2,24,256]{3,2,1,0:T(8,128)S(1)} %pad_maximum_fusion.1), channel_id=1, source_target_pairs={{0,96},{4,100},{8,104},{12,108},{16,112},{20,116},{24,120},{28,124... | collective-permute-start | bytes 589832 | tf_op jit(solution)/shard_map/ppermute | solution.py:46
  56.0 5.5 %copy-start.1 = (f32[4,8,24,256]{3,2,1,0:T(8,128)S(1)}, f32[4,8,24,256]{3,2,1,0:T(8,128)}, u32[]{:S(2)}) copy-start(f32[4,8,24,256]{3,2,1,0:T(8,128)} %get-tuple-element.14) | copy-start | bytes 2359300
  56.0 11.0 %all-to-all-start.2 = ((f32[4,2,24,256]{3,2,1,0:T(8,128)}), f32[4,2,24,256]{3,2,1,0:T(8,128)S(1)}, u32[]{:S(2)}, u32[]{:S(2)}) async-start(f32[4,2,24,256]{3,2,1,0:T(8,128)} %fusion.13), calls=%async_computation.2 | async-start | bytes 393216 | tf_op jit(solution)/shard_map/all_to_all | solution.py:39
  60.9 9.9 %collective-permute-start = (f32[8,24,256]{2,1,0:T(8,128)S(1)}, f32[8,24,256]{2,1,0:T(8,128)S(1)}, u32[]{:S(2)}, u32[]{:S(2)}) collective-permute-start(f32[8,24,256]{2,1,0:T(8,128)S(1)} %slice_bitcast_fusion), channel_id=1, source_target_pairs={{0,130},{1,131},{2,128},{3,129},{4,134},{5,135},{6,132},{7,133},{8... | collective-permute-start | bytes 589832 | tf_op jit(solution)/shard_map/ppermute | solution.py:35
  61.5 9.1 %copy-start.3 = (f32[1536]{0:T(1024)S(1)}, f32[1536]{0:T(1024)}, u32[]{:S(2)}) copy-start(f32[1536]{0:T(1024)} %param.8) | copy-start | bytes 18436
  67.0 13.8 %all-to-all-start.1 = ((f32[4,8,24,256]{3,2,1,0:T(8,128)}), f32[4,8,24,256]{3,2,1,0:T(8,128)S(1)}, u32[]{:S(2)}, u32[]{:S(2)}) async-start(f32[4,8,24,256]{3,2,1,0:T(8,128)} %add.93), calls=%async_computation.1 | async-start | bytes 1572864 | tf_op jit(solution)/shard_map/all_to_all | solution.py:39
  70.8 31.6 %copy-start = (bf16[1536,512]{1,0:T(8,128)(2,1)S(1)}, bf16[1536,512]{1,0:T(8,128)(2,1)}, u32[]{:S(2)}) copy-start(bf16[1536,512]{1,0:T(8,128)(2,1)} %param.9) | copy-start | bytes 4718596
  80.9 8.0 %collective-permute-start.2 = (f32[2,24,512]{2,1,0:T(8,128)S(1)}, f32[2,24,512]{2,1,0:T(8,128)S(1)}, u32[]{:S(2)}, u32[]{:S(2)}) collective-permute-start(f32[2,24,512]{2,1,0:T(8,128)S(1)} %get-tuple-element.17), channel_id=1, source_target_pairs={{0,16},{4,20},{8,24},{12,28},{16,32},{20,36},{24,40},{28,44},{32,4... | collective-permute-start | bytes 294920 | tf_op jit(solution)/shard_map/ppermute | solution.py:46
  81.0 7.9 %collective-permute-start.3 = (f32[2,24,512]{2,1,0:T(8,128)S(1)}, f32[2,24,512]{2,1,0:T(8,128)S(1)}, u32[]{:S(2)}, u32[]{:S(2)}) collective-permute-start(f32[2,24,512]{2,1,0:T(8,128)S(1)} %get-tuple-element.18), channel_id=1, source_target_pairs={{0,112},{4,116},{8,120},{12,124},{16,0},{20,4},{24,8},{28,12},{32,... | collective-permute-start | bytes 294920 | tf_op jit(solution)/shard_map/ppermute | solution.py:46
  84.3 11.5 %collective-permute-start.14 = (f32[24,256]{1,0:T(8,128)S(1)}, f32[24,256]{1,0:T(8,128)S(1)}, u32[]{:S(2)}, u32[]{:S(2)}) collective-permute-start(f32[24,256]{1,0:T(8,128)S(1)} %slice_bitcast_fusion.2), channel_id=1, source_target_pairs={{0,130},{1,131},{2,128},{3,129},{4,134},{5,135},{6,132},{7,133},{8... | collective-permute-start | bytes 73736 | tf_op jit(solution)/shard_map/ppermute | solution.py:35
  84.8 6.2 %collective-permute-start.4 = (f32[24,256]{1,0:T(8,128)S(1)}, f32[24,256]{1,0:T(8,128)S(1)}, u32[]{:S(2)}, u32[]{:S(2)}) collective-permute-start(f32[24,256]{1,0:T(8,128)S(1)} %slice_bitcast_fusion.4), channel_id=1, source_target_pairs={{0,32},{4,36},{8,40},{12,44},{16,48},{20,52},{24,56},{28,60},{32,6... | collective-permute-start | bytes 73736 | tf_op jit(solution)/shard_map/ppermute | solution.py:46
  86.8 4.8 %collective-permute-start.6 = (f32[24,256]{1,0:T(8,128)S(1)}, f32[24,256]{1,0:T(8,128)S(1)}, u32[]{:S(2)}, u32[]{:S(2)}) collective-permute-start(f32[24,256]{1,0:T(8,128)S(1)} %slice_bitcast_fusion.5), channel_id=1, source_target_pairs={{0,96},{4,100},{8,104},{12,108},{16,112},{20,116},{24,120},{28,124... | collective-permute-start | bytes 73736 | tf_op jit(solution)/shard_map/ppermute | solution.py:46
  91.6 6.3 %collective-permute-start.5 = (f32[24,512]{1,0:T(8,128)S(1)}, f32[24,512]{1,0:T(8,128)S(1)}, u32[]{:S(2)}, u32[]{:S(2)}) collective-permute-start(f32[24,512]{1,0:T(8,128)S(1)} %pad_maximum_fusion.6), channel_id=1, source_target_pairs={{0,32},{4,36},{8,40},{12,44},{16,48},{20,52},{24,56},{28,60},{32,6... | collective-permute-start | bytes 147464 | tf_op jit(solution)/shard_map/ppermute | solution.py:46
  94.1 5.1 %collective-permute-start.7 = (f32[24,512]{1,0:T(8,128)S(1)}, f32[24,512]{1,0:T(8,128)S(1)}, u32[]{:S(2)}, u32[]{:S(2)}) collective-permute-start(f32[24,512]{1,0:T(8,128)S(1)} %pad_maximum_fusion.7), channel_id=1, source_target_pairs={{0,96},{4,100},{8,104},{12,108},{16,112},{20,116},{24,120},{28,124... | collective-permute-start | bytes 147464 | tf_op jit(solution)/shard_map/ppermute | solution.py:46
  99.3 3.1 %collective-permute-start.17 = (f32[24,2,384]{2,0,1:T(8,128)S(1)}, f32[24,2,384]{2,0,1:T(8,128)S(1)}, u32[]{:S(2)}, u32[]{:S(2)}) collective-permute-start(f32[24,2,384]{2,0,1:T(8,128)S(1)} %fusion.15), channel_id=1, source_target_pairs={{0,1},{1,0},{2,3},{3,2},{4,5},{5,4},{6,7},{7,6},{8,9},{9,8},{10,11... | collective-permute-start | bytes 221192 | tf_op jit(solution)/shard_map/ppermute | solution.py:151
  99.4 5.9 %collective-permute-start.16 = (f32[24,2,384]{2,0,1:T(8,128)S(1)}, f32[24,2,384]{2,0,1:T(8,128)S(1)}, u32[]{:S(2)}, u32[]{:S(2)}) collective-permute-start(f32[24,2,384]{2,0,1:T(8,128)S(1)} %fusion.15), channel_id=1, source_target_pairs={{0,2},{1,3},{2,0},{3,1},{4,6},{5,7},{6,4},{7,5},{8,10},{9,11},{10,... | collective-permute-start | bytes 221192 | tf_op jit(solution)/shard_map/ppermute | solution.py:151
  102.4 4.3 %collective-permute-start.15 = (f32[24,2,384]{2,0,1:T(8,128)S(1)}, f32[24,2,384]{2,0,1:T(8,128)S(1)}, u32[]{:S(2)}, u32[]{:S(2)}) collective-permute-start(f32[24,2,384]{2,0,1:T(8,128)S(1)} %fusion.15), channel_id=1, source_target_pairs={{0,3},{1,2},{2,1},{3,0},{4,7},{5,6},{6,5},{7,4},{8,11},{9,10},{10,... | collective-permute-start | bytes 221192 | tf_op jit(solution)/shard_map/ppermute | solution.py:151
  108.4 23.0 %all-to-all-start.3 = ((f32[64,8,128]{2,1,0:T(8,128)}), f32[64,8,128]{2,1,0:T(8,128)S(1)}, u32[]{:S(2)}, u32[]{:S(2)}) async-start(f32[64,8,128]{2,1,0:T(8,128)} %broadcast_in_dim.2), calls=%async_computation.3 | async-start | bytes 524288 | tf_op jit(solution)/shard_map/all_to_all | solution.py:163

commit v2 on v1

v2 whole, which is shorter than its diff:
```python
import jax
import jax.numpy as jnp
from jax import lax
from jax.experimental import pallas as pl
from jax.experimental.pallas import tpu as pltpu
from jax.sharding import PartitionSpec as P


NX, NZ, NY = 2, 8, 4
COLUMNS = 256
QUARTERS = 4
Z_ORDER = (4, 1, 3, -1, -3, 0, 2, -2)
Y_GROUPS = [[base + y for y in range(NY)] for base in range(0, NX * NZ * NY, NY)]


def place(position):
    return position // (NZ * NY), position // NY % NZ, position % NY


def z_perm(dz):
    moves = []
    for position in range(NX * NZ * NY):
        x, z, y = place(position)
        moves.append((position, (x * NZ + (z + dz) % NZ) * NY + y))
    return moves


def x_swap(away, keep):
    pair_count, sigma_count = lax.axis_size("pair"), lax.axis_size("sigma")
    moves = [
        (p * sigma_count + s, (p ^ (NZ * NY)) * sigma_count + (s ^ 2))
        for p in range(pair_count)
        for s in range(sigma_count)
    ]
    return keep + lax.ppermute(away, ("pair", "sigma"), moves)


def y_sum(block):
    return jnp.sum(lax.all_to_all(block, "pair", 0, 0, axis_index_groups=Y_GROUPS, tiled=True), axis=0)


def z_sum(low, high, up, down, keep):
    half = low.shape[-1]

    def send(part, dz):
        return lax.ppermute(part, "pair", z_perm(dz))

    low, high = send(low, -2), send(high, 2)
    up, down = send(up, 1), send(down, -1)
    above, below = keep[1] + up[1], keep[2] + down[1]
    above = jnp.concatenate([above[..., :half], above[..., half:] + high], axis=-1)
    below = jnp.concatenate([below[..., :half] + low, below[..., half:]], axis=-1)
    return keep[0] + up[0] + down[0] + send(above, 2) + send(below, -2)


def spots():
    position = lax.axis_index("pair")
    x = position // (NZ * NY)
    return lax.axis_index("sigma") ^ (2 * x), x, (position // NY) & (NZ - 1)


def chi_streams(pairs, bins, table, streams):
    pair_local, width = pairs.shape
    col_count = width // QUARTERS
    row_count = width // (NX * NZ * NY)
    total = COLUMNS * len(streams)
    shapes = [shape for stream, _ in streams for shape in stream]

    def body(pairs_ref, bins_ref, table_ref, *refs):
        pair_ref, scaled_ref, rows_ref, done = refs[len(shapes) :]
        quarter, x, z = spots()

        def first_column(step):
            return pl.multiple_of(((quarter + step) & (QUARTERS - 1)) * col_count, 128)

        def fetch(step):
            part = pairs_ref.at[:, pl.ds(first_column(step), col_count)]
            return pltpu.make_async_copy(part, pair_ref.at[step], done.at[step])

        for step in range(QUARTERS):
            fetch(step).start()
        index = bins_ref[...]
        upper = lax.broadcasted_iota(jnp.int32, index.shape, 0) > 0
        picked = jnp.zeros(index.shape, jnp.float32)
        for level in range(table.shape[1]):
            picked = jnp.where(index == level, jnp.where(upper, table_ref[1, level], table_ref[0, level]), picked)
        weight = picked / jnp.float32(pair_local * NX * NZ * NY)
        by_pair = jnp.transpose(jnp.concatenate([weight, jnp.zeros((6, pair_local), jnp.float32)], axis=0))
        fetch(0).wait()
        for t in range(total // 128):
            f, column = divmod(128 * t, col_count)
            product = by_pair[:, f : f + 1] * pair_ref[0, :, column : column + 128].astype(jnp.float32)
            scaled_ref[:, 128 * t : 128 * t + 128] = product.astype(jnp.bfloat16)
        for step in range(QUARTERS):
            if step:
                fetch(step).wait()
            rows_ref[pl.ds(first_column(step), col_count), :] = lax.dot_general(
                pair_ref[step], scaled_ref[...], (((0,), (0,)), ((), ())), preferred_element_type=jnp.float32
            )
        before = 0
        for k, (stream, stores) in enumerate(streams):
            for out, index, (left, right), keeps, dz, y in stores:
                at = ((x if keeps else 1 - x) * NZ + ((z + dz) & (NZ - 1))) * NY + y
                rows = pl.ds(pl.multiple_of(at * row_count, 8), row_count)
                refs[before + out][index] = rows_ref[rows, k * COLUMNS + left : k * COLUMNS + right]
            before += len(stream)

    outs = pl.pallas_call(
        body,
        in_specs=[
            pl.BlockSpec(memory_space=pltpu.HBM),
            pl.BlockSpec(memory_space=pltpu.VMEM),
            pl.BlockSpec(memory_space=pltpu.SMEM),
        ],
        out_specs=[pl.BlockSpec(memory_space=pltpu.VMEM)] * len(shapes),
        out_shape=[jax.ShapeDtypeStruct(shape, jnp.float32) for shape in shapes],
        scratch_shapes=[
            pltpu.VMEM((QUARTERS, pair_local, col_count), jnp.bfloat16),
            pltpu.VMEM((pair_local, total), jnp.bfloat16),
            pltpu.VMEM((width, total), jnp.float32),
            pltpu.SemaphoreType.DMA((QUARTERS,)),
        ],
        compiler_params=pltpu.CompilerParams(vmem_limit_bytes=36 << 20),
    )(pltpu.with_memory_space_constraint(pairs, pltpu.HBM), bins, table)
    split = []
    for stream, _ in streams:
        split.append(outs[: len(stream)])
        outs = outs[len(stream) :]
    return split


def local(pair_density_matrices, energy_bins, bin_weights, coulomb, state_matrices):
    width = pair_density_matrices.shape[1]
    pair_count = lax.axis_size("pair")
    sigma_count = lax.axis_size("sigma")
    row_count = width // pair_count
    col_count = width // sigma_count
    pair_position = lax.axis_index("pair")
    quarter = spots()[0]
    rc, n, half = row_count, COLUMNS, COLUMNS // 2
    every = (0, n)
    slots = [(y, keeps, k) for y in range(NY) for keeps in (0, 1) for k in range(NZ)]
    b_stores = [(0, (y, keeps, k), every, keeps, Z_ORDER[k], y) for y, keeps, k in slots]
    c_stores = [(keeps, (y, k), every, keeps, Z_ORDER[k], y) for y, keeps, k in slots]
    a_stores = []
    for y, keeps, k in slots:
        if Z_ORDER[k] == 4:
            a_stores += [(0, (y, keeps), (0, half), keeps, 4, y), (1, (y, keeps), (half, n), keeps, 4, y)]
        else:
            out, slot = divmod(k - 1, 2) if k < 5 else (2, k - 5)
            a_stores.append((2 + out, (slot, y, keeps), every, keeps, Z_ORDER[k], y))
    (b,), c, a = chi_streams(
        pair_density_matrices,
        energy_bins.T,
        bin_weights,
        [
            ([(NY, NX, NZ, rc, n)], b_stores),
            ([(NY, NZ, rc, n)] * 2, c_stores),
            ([(NY, NX, rc, half)] * 2 + [(k, NY, NX, rc, n) for k in (2, 2, 3)], a_stores),
        ],
    )

    c = y_sum(x_swap(*c))
    b = x_swap(*y_sum(b))
    bc = jnp.concatenate([b, c], axis=2)
    bc = lax.optimization_barrier((bc[0, :, :n], bc[0, :, n:], bc[1:3], bc[3:5], bc[5:]))
    bc = z_sum(*bc)
    a = x_swap(*y_sum(z_sum(*a)))
    polar = jnp.concatenate([bc, a], axis=1)

    root = jnp.sqrt(coulomb)
    root_rows = lax.dynamic_slice_in_dim(root, pair_position * row_count, row_count, 0)
    root_columns = lax.dynamic_slice_in_dim(root, quarter * col_count, col_count, 0)
    screened = -root_rows[:, None, None] * polar.reshape(row_count, -1, col_count) * root_columns[None, None, :]
    parts = [screened] + [
        lax.ppermute(screened, "sigma", [(s, s ^ k) for s in range(sigma_count)]) for k in range(1, sigma_count)
    ]
    for bit in (1, 2):
        odd = (quarter & bit) != 0
        parts = [jnp.where(odd, parts[k ^ bit], parts[k]) for k in range(sigma_count)]
    states_wide = state_matrices.astype(jnp.float32)
    applied = jnp.einsum(
        "rfc,cn->rfn", jnp.concatenate(parts, axis=2), states_wide, precision=lax.Precision.HIGHEST
    )
    own_states = lax.dynamic_slice_in_dim(states_wide, pair_position * row_count, row_count, 0)
    total = jnp.sum(own_states[:, None, :] * applied, axis=0) / jnp.float32(width)
    spread = jnp.broadcast_to(total.reshape(8, -1)[None], (pair_count, 8, total.size // 8))
    total = jnp.sum(lax.all_to_all(spread, "pair", 0, 0, tiled=True), axis=0).reshape(total.shape)
    return (applied, total)


def solution(mesh):
    return jax.shard_map(
        local,
        mesh=mesh,
        in_specs=(P("pair", None), P("pair", None), P(), P(), P(None, "sigma")),
        out_specs=(P("pair", None, "sigma"), P(None, "sigma")),
        check_vma=False,
    )
```

time: 133 us -> 125 us (0.940)
  Pallas kernels: 24.5 us -> 11.1 us
  waiting for transfers between devices: 45.5 us -> 53.3 us
  starting transfers between devices: 52.2 us -> 47.2 us
  local copies, waits for them, and re-layouts: 2.18 us -> 3.55 us
    pallas_call x3 -> x1, Pallas kernels: 24.5 us -> 11.1 us  [chi_streams(): pl.pallas_call(body, in_specs=[pl.BlockSpec(memory_space=pltpu.HBM), pl.B...]
    ppermute x12, waiting for transfers between devices: 13.4 us -> 23.3 us  [send(): return lax.ppermute(part, 'pair', z_perm(dz))]
    ppermute x12, starting transfers between devices: 25.9 us -> 21.4 us  [send(): return lax.ppermute(part, 'pair', z_perm(dz))]
    all_to_all x3, waiting for transfers between devices: 13.4 us -> 11.4 us  [y_sum(): lax.all_to_all(block, 'pair', 0, 0, axis_index_groups=Y_GROUPS, tiled=True)]
    reduce_sum x3, other arithmetic: 0.19 us -> 1.62 us  [y_sum(): jnp.sum(lax.all_to_all(block, 'pair', 0, 0, axis_index_groups=Y_GROUPS, t...]
    unnamed x13 -> x9, local copies, waits for them, and re-layouts: 0.74 us -> 2.12 us
  transfers between devices with their start and end apart: 22 -> 22, of which waited for: 11 -> 15; matrix products, arithmetic and copies ran while one was open for 3% -> 6% of each run, Pallas kernels for 12% -> 0%
where the time goes in v2:
time: 125 us; the launch traced here: 124 us
  waiting for transfers between devices  53.3 us (43%)
  starting transfers between devices  47.2 us (38%)
  Pallas kernels  11.1 us (9%)
  other arithmetic  6.92 us (6%)
  local copies, waits for them, and re-layouts  3.55 us (3%)
    ppermute x12, waiting for transfers between devices, send(): return lax.ppermute(part, 'pair', z_perm(dz))  23.3 us
    ppermute x12, starting transfers between devices, send(): return lax.ppermute(part, 'pair', z_perm(dz))  21.4 us
    all_to_all x1, waiting for transfers between devices, local(): lax.all_to_all(spread, 'pair', 0, 0, tiled=True)  14.3 us
    all_to_all x3, starting transfers between devices, y_sum(): lax.all_to_all(block, 'pair', 0, 0, axis_index_groups=Y_GROUPS, tiled=True)  13.1 us
    all_to_all x3, waiting for transfers between devices, y_sum(): lax.all_to_all(block, 'pair', 0, 0, axis_index_groups=Y_GROUPS, tiled=True)  11.4 us
    pallas_call x1, Pallas kernels, chi_streams(): pl.pallas_call(body, in_specs=[pl.BlockSpec(memory_space=pltpu.HBM), pl.B...  11.1 us
    all_to_all x1, starting transfers between devices, local(): lax.all_to_all(spread, 'pair', 0, 0, tiled=True)  6.87 us
    ppermute x3, waiting for transfers between devices, local(): lax.ppermute(screened, 'sigma', [(s, s ^ k) for s in range(sigma_count)])  4.22 us
  transfers between devices with their start and end apart: 22, of which 15 were waited for; matrix products, arithmetic and copies ran while one was open for 6% of the time, Pallas kernels for 0%

profile of v2, /device:TPU:2, one launch (start us, length us, event | category | flops | bytes accessed | tf_op | source)
XLA Modules:
  0.0 123.9 jit_solution(2497877935059602782)
XLA Ops:
  0.6 0.0 copy-start
  0.6 0.7 copy-done
  1.4 0.7 copy-done.1
  2.0 11.1 %shard_map.68 = (f32[4,2,8,24,256]{4,3,2,1,0:T(8,128)}, f32[4,8,24,256]{3,2,1,0:T(8,128)S(1)}, f32[4,8,24,256]{3,2,1,0:T(8,128)S(1)}, f32[4,2,24,128]{3,2,1,0:T(...) custom-call(bf16[2048,1536]{1,0:T(8,128)(2,1)} %pairs_ref.1, ...), custom_call_target="tpu_custom_call" | custom-call | tf_op jit(solution)/shard_map/pallas_call | solution.py:108
  13.2 2.0 %collective-permute-start.8 = (f32[2,4,2,24,256]{4,3,2,1,0:T(8,128)S(1)}, f32[2,4,2,24,256]{4,3,2,1,0:T(8,128)S(1)}, u32[]{:S(2)}, u32[]{:S(2)}) collective-permute-start(f32[2,4,2,24,256]{4,3,2,1,0:T(8,128)S(1)} %get-tuple-element.24), channel_id=1, source_target_pairs={{0,16},{4,20},{8,24},{12,28},{16,32},{20,36},{24,40},{28,44},{32,4... | collective-permute-start | bytes 1179656 | tf_op jit(solution)/shard_map/ppermute | solution.py:46
  15.2 4.0 %collective-permute-start.9 = (f32[2,4,2,24,256]{4,3,2,1,0:T(8,128)S(1)}, f32[2,4,2,24,256]{4,3,2,1,0:T(8,128)}, u32[]{:S(2)}, u32[]{:S(2)}) collective-permute-start(f32[2,4,2,24,256]{4,3,2,1,0:T(8,128)S(1)} %get-tuple-element.25), channel_id=1, source_target_pairs={{0,112},{4,116},{8,120},{12,124},{16,0},{20,4},{24,8},{28,12},{32,... | collective-permute-start | bytes 1179656 | tf_op jit(solution)/shard_map/ppermute | solution.py:46
  19.2 4.5 %all-to-all-start = ((f32[4,2,8,24,256]{4,3,2,1,0:T(8,128)}), f32[4,2,8,24,256]{4,3,2,1,0:T(8,128)}, u32[]{:S(2)}, u32[]{:S(2)}) async-start(f32[4,2,8,24,256]{4,3,2,1,0:T(8,128)} %get-tuple-element.15), calls=%async_computation | async-start | bytes 3145728 | tf_op jit(solution)/shard_map/all_to_all | solution.py:39
  23.7 2.4 %collective-permute-start.12 = (f32[4,2,24,128]{3,2,1,0:T(8,128)S(1)}, f32[4,2,24,128]{3,2,1,0:T(8,128)S(1)}, u32[]{:S(2)}, u32[]{:S(2)}) collective-permute-start(f32[4,2,24,128]{3,2,1,0:T(8,128)S(1)} %get-tuple-element.27), channel_id=1, source_target_pairs={{0,96},{4,100},{8,104},{12,108},{16,112},{20,116},{24,120},{28,124... | collective-permute-start | bytes 294920 | tf_op jit(solution)/shard_map/ppermute | solution.py:46
  26.0 0.5 collective-permute-start.10
  26.6 1.5 %collective-permute-start.1 = (f32[4,8,24,256]{3,2,1,0:T(8,128)S(1)}, f32[4,8,24,256]{3,2,1,0:T(8,128)}, u32[]{:S(2)}, u32[]{:S(2)}) collective-permute-start(f32[4,8,24,256]{3,2,1,0:T(8,128)S(1)} %get-tuple-element.17), channel_id=1, source_target_pairs={{0,130},{1,131},{2,128},{3,129},{4,134},{5,135},{6,132},{7,133},{8... | collective-permute-start | bytes 2359304 | tf_op jit(solution)/shard_map/ppermute | solution.py:35
  28.1 0.1 collective-permute-done.8
  28.2 2.4 %collective-permute-done.9 = f32[2,4,2,24,256]{4,3,2,1,0:T(8,128)} collective-permute-done((f32[2,4,2,24,256]{4,3,2,1,0:T(8,128)S(1)}, f32[2,4,2,24,256]{4,3,2,1,0:T(8,128)}, u32[]{:S(2)}, u32[]{:S(2)}) %collective-permute-start.9) | collective-permute-done | bytes 393248 | tf_op jit(solution)/shard_map/ppermute | solution.py:46
  30.7 1.0 fusion.10
  31.6 0.1 collective-permute-done.12
  31.8 2.2 %collective-permute-done.10 = f32[4,2,24,128]{3,2,1,0:T(8,128)S(1)} collective-permute-done((f32[4,2,24,128]{3,2,1,0:T(8,128)S(1)}, f32[4,2,24,128]{3,2,1,0:T(8,128)S(1)}, u32[]{:S(2)}, u32[]{:S(2)}) %collective-permute-start.10) | collective-permute-done | bytes 98336 | tf_op jit(solution)/shard_map/ppermute | solution.py:46
  34.1 2.5 %collective-permute-start.13 = (f32[4,2,24,256]{3,2,1,0:T(8,128)S(1)}, f32[4,2,24,256]{3,2,1,0:T(8,128)S(1)}, u32[]{:S(2)}, u32[]{:S(2)}) collective-permute-start(f32[4,2,24,256]{3,2,1,0:T(8,128)S(1)} %pad_maximum_fusion.1), channel_id=1, source_target_pairs={{0,96},{4,100},{8,104},{12,108},{16,112},{20,116},{24,120},{28,124... | collective-permute-start | bytes 589832 | tf_op jit(solution)/shard_map/ppermute | solution.py:46
  36.5 0.8 collective-permute-start.11
  37.3 7.5 %collective-permute-done.13 = f32[4,2,24,256]{3,2,1,0:T(8,128)S(1)} collective-permute-done((f32[4,2,24,256]{3,2,1,0:T(8,128)S(1)}, f32[4,2,24,256]{3,2,1,0:T(8,128)S(1)}, u32[]{:S(2)}, u32[]{:S(2)}) %collective-permute-start.13) | collective-permute-done | bytes 196640 | tf_op jit(solution)/shard_map/ppermute | solution.py:46
  44.8 1.4 %collective-permute-done.11 = f32[4,2,24,256]{3,2,1,0:T(8,128)S(1)} collective-permute-done((f32[4,2,24,256]{3,2,1,0:T(8,128)S(1)}, f32[4,2,24,256]{3,2,1,0:T(8,128)S(1)}, u32[]{:S(2)}, u32[]{:S(2)}) %collective-permute-start.11) | collective-permute-done | bytes 196640 | tf_op jit(solution)/shard_map/ppermute | solution.py:46
  46.2 1.7 %fusion.13 = f32[4,2,24,256]{3,2,1,0:T(8,128)} fusion(f32[4,2,24,256]{3,2,1,0:T(8,128)S(1)} %collective-permute-done.13, f32[4,2,24,256]{3,2,1,0:T(8,128)S(1)} %collective-permute-done.11, f32[2,4,2,24,256]{4,3,2,1,0:T(8,128)} %collective-permute-done.9, f32[2,4,2,24,256]{4,3,2,1,0:T(8,128)S(1)} %collective-permute-done.8, ...), kind=kLoop, calls=%fused_computation.16 | loop fusion | flops 196608 | bytes 1179648 | tf_op jit(solution)/shard_map/add | solution.py:53
  47.9 0.0 all-to-all-done
  47.9 4.7 %all-to-all-start.2 = ((f32[4,2,24,256]{3,2,1,0:T(8,128)}), f32[4,2,24,256]{3,2,1,0:T(8,128)S(1)}, u32[]{:S(2)}, u32[]{:S(2)}) async-start(f32[4,2,24,256]{3,2,1,0:T(8,128)} %fusion.13), calls=%async_computation.2 | async-start | bytes 393216 | tf_op jit(solution)/shard_map/all_to_all | solution.py:39
  52.6 1.6 %reduce_sum.45 = f32[2,8,24,256]{3,2,1,0:T(8,128)S(1)} reduce(f32[4,2,8,24,256]{4,3,2,1,0:T(8,128)} %all-to-all-done, f32[]{:T(128)} %constant.37.clone.1), dimensions={0}, to_apply=%region_0.1 | reduce | flops 294912 | bytes 1966084 | tf_op jit(solution)/shard_map/reduce_sum | solution.py:39
  54.1 1.7 %collective-permute-start = (f32[8,24,256]{2,1,0:T(8,128)S(1)}, f32[8,24,256]{2,1,0:T(8,128)S(1)}, u32[]{:S(2)}, u32[]{:S(2)}) collective-permute-start(f32[8,24,256]{2,1,0:T(8,128)S(1)} %slice_bitcast_fusion), channel_id=1, source_target_pairs={{0,130},{1,131},{2,128},{3,129},{4,134},{5,135},{6,132},{7,133},{8... | collective-permute-start | bytes 589832 | tf_op jit(solution)/shard_map/ppermute | solution.py:35
  55.9 0.0 collective-permute-done.1
  55.9 2.1 %add.87 = f32[4,8,24,256]{3,2,1,0:T(8,128)} add(f32[4,8,24,256]{3,2,1,0:T(8,128)S(1)} %get-tuple-element.16, f32[4,8,24,256]{3,2,1,0:T(8,128)} %collective-permute-done.1) | non-fusion elementwise | flops 196608 | bytes 2359296 | tf_op jit(solution)/shard_map/add | solution.py:35
  58.0 0.9 all-to-all-done.2
  58.9 3.9 %all-to-all-start.1 = ((f32[4,8,24,256]{3,2,1,0:T(8,128)}), f32[4,8,24,256]{3,2,1,0:T(8,128)S(1)}, u32[]{:S(2)}, u32[]{:S(2)}) async-start(f32[4,8,24,256]{3,2,1,0:T(8,128)} %add.87), calls=%async_computation.1 | async-start | bytes 1572864 | tf_op jit(solution)/shard_map/all_to_all | solution.py:39
  62.8 0.0 copy-done.3
  62.8 0.1 dynamic_slice.10
  62.9 0.1 dynamic-slice_negate_fusion
  63.0 0.0 collective-permute-done
  63.1 0.0 copy-start.2
  63.1 10.6 %all-to-all-done.1 = f32[4,8,24,256]{3,2,1,0:T(8,128)S(1)} async-done(((f32[4,8,24,256]{3,2,1,0:T(8,128)}), f32[4,8,24,256]{3,2,1,0:T(8,128)S(1)}, u32[]{:S(2)}, u32[]{:S(2)}) %all-to-all-start.1) | async-done | bytes 786464 | tf_op jit(solution)/shard_map/all_to_all | solution.py:39
  73.7 0.1 reduce_sum.46
  73.8 0.5 collective-permute-start.2
  74.3 2.8 %collective-permute-start.3 = (f32[2,24,512]{2,1,0:T(8,128)S(1)}, f32[2,24,512]{2,1,0:T(8,128)S(1)}, u32[]{:S(2)}, u32[]{:S(2)}) collective-permute-start(f32[2,24,512]{2,1,0:T(8,128)S(1)} %get-tuple-element.20), channel_id=1, source_target_pairs={{0,112},{4,116},{8,120},{12,124},{16,0},{20,4},{24,8},{28,12},{32,... | collective-permute-start | bytes 294920 | tf_op jit(solution)/shard_map/ppermute | solution.py:46
  77.1 0.7 collective-permute-start.14
  77.8 1.5 %collective-permute-start.6 = (f32[24,256]{1,0:T(8,128)S(1)}, f32[24,256]{1,0:T(8,128)S(1)}, u32[]{:S(2)}, u32[]{:S(2)}) collective-permute-start(f32[24,256]{1,0:T(8,128)S(1)} %slice_bitcast_fusion.5), channel_id=1, source_target_pairs={{0,96},{4,100},{8,104},{12,108},{16,112},{20,116},{24,120},{28,124... | collective-permute-start | bytes 73736 | tf_op jit(solution)/shard_map/ppermute | solution.py:46
  79.3 1.4 %collective-permute-start.4 = (f32[24,256]{1,0:T(8,128)S(1)}, f32[24,256]{1,0:T(8,128)S(1)}, u32[]{:S(2)}, u32[]{:S(2)}) collective-permute-start(f32[24,256]{1,0:T(8,128)S(1)} %slice_bitcast_fusion.4), channel_id=1, source_target_pairs={{0,32},{4,36},{8,40},{12,44},{16,48},{20,52},{24,56},{28,60},{32,6... | collective-permute-start | bytes 73736 | tf_op jit(solution)/shard_map/ppermute | solution.py:46
  80.7 0.0 collective-permute-done.2
  80.7 0.0 collective-permute-done.3
  80.7 1.9 %collective-permute-done.6 = f32[24,256]{1,0:T(8,128)S(1)} collective-permute-done((f32[24,256]{1,0:T(8,128)S(1)}, f32[24,256]{1,0:T(8,128)S(1)}, u32[]{:S(2)}, u32[]{:S(2)}) %collective-permute-start.6) | collective-permute-done | bytes 24608 | tf_op jit(solution)/shard_map/ppermute | solution.py:46
  82.6 2.7 %collective-permute-done.4 = f32[24,256]{1,0:T(8,128)S(1)} collective-permute-done((f32[24,256]{1,0:T(8,128)S(1)}, f32[24,256]{1,0:T(8,128)S(1)}, u32[]{:S(2)}, u32[]{:S(2)}) %collective-permute-start.4) | collective-permute-done | bytes 24608 | tf_op jit(solution)/shard_map/ppermute | solution.py:46
  85.4 1.1 collective-permute-start.7
  86.5 1.9 %collective-permute-start.5 = (f32[24,512]{1,0:T(8,128)S(1)}, f32[24,512]{1,0:T(8,128)S(1)}, u32[]{:S(2)}, u32[]{:S(2)}) collective-permute-start(f32[24,512]{1,0:T(8,128)S(1)} %pad_maximum_fusion.6), channel_id=1, source_target_pairs={{0,32},{4,36},{8,40},{12,44},{16,48},{20,52},{24,56},{28,60},{32,6... | collective-permute-start | bytes 147464 | tf_op jit(solution)/shard_map/ppermute | solution.py:46
  88.4 0.0 collective-permute-done.14
  88.4 2.0 %collective-permute-done.7 = f32[24,512]{1,0:T(8,128)S(1)} collective-permute-done((f32[24,512]{1,0:T(8,128)S(1)}, f32[24,512]{1,0:T(8,128)S(1)}, u32[]{:S(2)}, u32[]{:S(2)}) %collective-permute-start.7) | collective-permute-done | bytes 49184 | tf_op jit(solution)/shard_map/ppermute | solution.py:46
  90.4 2.8 %collective-permute-done.5 = f32[24,512]{1,0:T(8,128)S(1)} collective-permute-done((f32[24,512]{1,0:T(8,128)S(1)}, f32[24,512]{1,0:T(8,128)S(1)}, u32[]{:S(2)}, u32[]{:S(2)}) %collective-permute-start.5) | collective-permute-done | bytes 49184 | tf_op jit(solution)/shard_map/ppermute | solution.py:46
  93.3 0.1 fusion.15
  93.3 0.0 collective-permute-start.15
  93.4 1.9 %collective-permute-start.16 = (f32[24,2,384]{2,0,1:T(8,128)S(1)}, f32[24,2,384]{2,0,1:T(8,128)S(1)}, u32[]{:S(2)}, u32[]{:S(2)}) collective-permute-start(f32[24,2,384]{2,0,1:T(8,128)S(1)} %fusion.15), channel_id=1, source_target_pairs={{0,2},{1,3},{2,0},{3,1},{4,6},{5,7},{6,4},{7,5},{8,10},{9,11},{10,... | collective-permute-start | bytes 221192 | tf_op jit(solution)/shard_map/ppermute | solution.py:176
  95.3 0.0 collective-permute-start.17
  95.3 2.3 %collective-permute-done.15 = f32[24,2,384]{2,0,1:T(8,128)S(1)} collective-permute-done((f32[24,2,384]{2,0,1:T(8,128)S(1)}, f32[24,2,384]{2,0,1:T(8,128)S(1)}, u32[]{:S(2)}, u32[]{:S(2)}) %collective-permute-start.15) | collective-permute-done | bytes 73760 | tf_op jit(solution)/shard_map/ppermute | solution.py:176
  97.6 1.9 %collective-permute-done.16 = f32[24,2,384]{2,0,1:T(8,128)S(1)} collective-permute-done((f32[24,2,384]{2,0,1:T(8,128)S(1)}, f32[24,2,384]{2,0,1:T(8,128)S(1)}, u32[]{:S(2)}, u32[]{:S(2)}) %collective-permute-start.16) | collective-permute-done | bytes 73760 | tf_op jit(solution)/shard_map/ppermute | solution.py:176
  99.5 0.0 collective-permute-done.17
  99.5 0.1 broadcast_select_fusion.7
  99.6 0.9 multiply_reduce_fusion
  100.6 0.7 broadcast_in_dim.2
  101.3 6.9 %all-to-all-start.3 = ((f32[64,8,128]{2,1,0:T(8,128)}), f32[64,8,128]{2,1,0:T(8,128)S(1)}, u32[]{:S(2)}, u32[]{:S(2)}) async-start(f32[64,8,128]{2,1,0:T(8,128)} %broadcast_in_dim.2), calls=%async_computation.3 | async-start | bytes 524288 | tf_op jit(solution)/shard_map/all_to_all | solution.py:188
  108.2 0.7 copy.11
  108.9 14.3 %all-to-all-done.3 = f32[64,8,128]{2,1,0:T(8,128)S(1)} async-done(((f32[64,8,128]{2,1,0:T(8,128)}), f32[64,8,128]{2,1,0:T(8,128)S(1)}, u32[]{:S(2)}, u32[]{:S(2)}) %all-to-all-start.3) | async-done | bytes 262176 | tf_op jit(solution)/shard_map/all_to_all | solution.py:188
  123.2 0.1 reduce_sum.49
  123.3 0.6 reshape.30
  (25 shorter events, 0.3 us)
Async XLA Ops:
  0.6 0.7 copy-start
  1.3 0.7 copy-start.1
  13.2 15.0 %collective-permute-start.8 = (f32[2,4,2,24,256]{4,3,2,1,0:T(8,128)S(1)}, f32[2,4,2,24,256]{4,3,2,1,0:T(8,128)S(1)}, u32[]{:S(2)}, u32[]{:S(2)}) collective-permute-start(f32[2,4,2,24,256]{4,3,2,1,0:T(8,128)S(1)} %get-tuple-element.24), channel_id=1, source_target_pairs={{0,16},{4,20},{8,24},{12,28},{16,32},{20,36},{24,40},{28,44},{32,4... | collective-permute-start | bytes 1179656 | tf_op jit(solution)/shard_map/ppermute | solution.py:46
  15.2 15.5 %collective-permute-start.9 = (f32[2,4,2,24,256]{4,3,2,1,0:T(8,128)S(1)}, f32[2,4,2,24,256]{4,3,2,1,0:T(8,128)}, u32[]{:S(2)}, u32[]{:S(2)}) collective-permute-start(f32[2,4,2,24,256]{4,3,2,1,0:T(8,128)S(1)} %get-tuple-element.25), channel_id=1, source_target_pairs={{0,112},{4,116},{8,120},{12,124},{16,0},{20,4},{24,8},{28,12},{32,... | collective-permute-start | bytes 1179656 | tf_op jit(solution)/shard_map/ppermute | solution.py:46
  19.2 28.7 %all-to-all-start = ((f32[4,2,8,24,256]{4,3,2,1,0:T(8,128)}), f32[4,2,8,24,256]{4,3,2,1,0:T(8,128)}, u32[]{:S(2)}, u32[]{:S(2)}) async-start(f32[4,2,8,24,256]{4,3,2,1,0:T(8,128)} %get-tuple-element.15), calls=%async_computation | async-start | bytes 3145728 | tf_op jit(solution)/shard_map/all_to_all | solution.py:39
  23.7 8.1 %collective-permute-start.12 = (f32[4,2,24,128]{3,2,1,0:T(8,128)S(1)}, f32[4,2,24,128]{3,2,1,0:T(8,128)S(1)}, u32[]{:S(2)}, u32[]{:S(2)}) collective-permute-start(f32[4,2,24,128]{3,2,1,0:T(8,128)S(1)} %get-tuple-element.27), channel_id=1, source_target_pairs={{0,96},{4,100},{8,104},{12,108},{16,112},{20,116},{24,120},{28,124... | collective-permute-start | bytes 294920 | tf_op jit(solution)/shard_map/ppermute | solution.py:46
  26.0 8.0 %collective-permute-start.10 = (f32[4,2,24,128]{3,2,1,0:T(8,128)S(1)}, f32[4,2,24,128]{3,2,1,0:T(8,128)S(1)}, u32[]{:S(2)}, u32[]{:S(2)}) collective-permute-start(f32[4,2,24,128]{3,2,1,0:T(8,128)S(1)} %get-tuple-element.26), channel_id=1, source_target_pairs={{0,32},{4,36},{8,40},{12,44},{16,48},{20,52},{24,56},{28,60},{32,6... | collective-permute-start | bytes 294920 | tf_op jit(solution)/shard_map/ppermute | solution.py:46
  26.6 29.3 %collective-permute-start.1 = (f32[4,8,24,256]{3,2,1,0:T(8,128)S(1)}, f32[4,8,24,256]{3,2,1,0:T(8,128)}, u32[]{:S(2)}, u32[]{:S(2)}) collective-permute-start(f32[4,8,24,256]{3,2,1,0:T(8,128)S(1)} %get-tuple-element.17), channel_id=1, source_target_pairs={{0,130},{1,131},{2,128},{3,129},{4,134},{5,135},{6,132},{7,133},{8... | collective-permute-start | bytes 2359304 | tf_op jit(solution)/shard_map/ppermute | solution.py:35
  34.1 10.8 %collective-permute-start.13 = (f32[4,2,24,256]{3,2,1,0:T(8,128)S(1)}, f32[4,2,24,256]{3,2,1,0:T(8,128)S(1)}, u32[]{:S(2)}, u32[]{:S(2)}) collective-permute-start(f32[4,2,24,256]{3,2,1,0:T(8,128)S(1)} %pad_maximum_fusion.1), channel_id=1, source_target_pairs={{0,96},{4,100},{8,104},{12,108},{16,112},{20,116},{24,120},{28,124... | collective-permute-start | bytes 589832 | tf_op jit(solution)/shard_map/ppermute | solution.py:46
  36.5 9.7 %collective-permute-start.11 = (f32[4,2,24,256]{3,2,1,0:T(8,128)S(1)}, f32[4,2,24,256]{3,2,1,0:T(8,128)S(1)}, u32[]{:S(2)}, u32[]{:S(2)}) collective-permute-start(f32[4,2,24,256]{3,2,1,0:T(8,128)S(1)} %pad_maximum_fusion), channel_id=1, source_target_pairs={{0,32},{4,36},{8,40},{12,44},{16,48},{20,52},{24,56},{28,60},{32,6... | collective-permute-start | bytes 589832 | tf_op jit(solution)/shard_map/ppermute | solution.py:46
  47.9 11.0 %all-to-all-start.2 = ((f32[4,2,24,256]{3,2,1,0:T(8,128)}), f32[4,2,24,256]{3,2,1,0:T(8,128)S(1)}, u32[]{:S(2)}, u32[]{:S(2)}) async-start(f32[4,2,24,256]{3,2,1,0:T(8,128)} %fusion.13), calls=%async_computation.2 | async-start | bytes 393216 | tf_op jit(solution)/shard_map/all_to_all | solution.py:39
  54.1 8.9 %collective-permute-start = (f32[8,24,256]{2,1,0:T(8,128)S(1)}, f32[8,24,256]{2,1,0:T(8,128)S(1)}, u32[]{:S(2)}, u32[]{:S(2)}) collective-permute-start(f32[8,24,256]{2,1,0:T(8,128)S(1)} %slice_bitcast_fusion), channel_id=1, source_target_pairs={{0,130},{1,131},{2,128},{3,129},{4,134},{5,135},{6,132},{7,133},{8... | collective-permute-start | bytes 589832 | tf_op jit(solution)/shard_map/ppermute | solution.py:35
  55.9 6.9 %copy-start.3 = (f32[1536]{0:T(1024)S(1)}, f32[1536]{0:T(1024)}, u32[]{:S(2)}) copy-start(f32[1536]{0:T(1024)} %param.8) | copy-start | bytes 18436
  58.9 14.8 %all-to-all-start.1 = ((f32[4,8,24,256]{3,2,1,0:T(8,128)}), f32[4,8,24,256]{3,2,1,0:T(8,128)S(1)}, u32[]{:S(2)}, u32[]{:S(2)}) async-start(f32[4,8,24,256]{3,2,1,0:T(8,128)} %add.87), calls=%async_computation.1 | async-start | bytes 1572864 | tf_op jit(solution)/shard_map/all_to_all | solution.py:39
  63.1 32.2 %copy-start.2 = (bf16[1536,512]{1,0:T(8,128)(2,1)S(1)}, bf16[1536,512]{1,0:T(8,128)(2,1)}, u32[]{:S(2)}) copy-start(bf16[1536,512]{1,0:T(8,128)(2,1)} %param.9) | copy-start | bytes 4718596
  73.8 6.9 %collective-permute-start.2 = (f32[2,24,512]{2,1,0:T(8,128)S(1)}, f32[2,24,512]{2,1,0:T(8,128)S(1)}, u32[]{:S(2)}, u32[]{:S(2)}) collective-permute-start(f32[2,24,512]{2,1,0:T(8,128)S(1)} %get-tuple-element.19), channel_id=1, source_target_pairs={{0,16},{4,20},{8,24},{12,28},{16,32},{20,36},{24,40},{28,44},{32,4... | collective-permute-start | bytes 294920 | tf_op jit(solution)/shard_map/ppermute | solution.py:46
  74.3 6.4 %collective-permute-start.3 = (f32[2,24,512]{2,1,0:T(8,128)S(1)}, f32[2,24,512]{2,1,0:T(8,128)S(1)}, u32[]{:S(2)}, u32[]{:S(2)}) collective-permute-start(f32[2,24,512]{2,1,0:T(8,128)S(1)} %get-tuple-element.20), channel_id=1, source_target_pairs={{0,112},{4,116},{8,120},{12,124},{16,0},{20,4},{24,8},{28,12},{32,... | collective-permute-start | bytes 294920 | tf_op jit(solution)/shard_map/ppermute | solution.py:46
  77.1 11.3 %collective-permute-start.14 = (f32[24,256]{1,0:T(8,128)S(1)}, f32[24,256]{1,0:T(8,128)S(1)}, u32[]{:S(2)}, u32[]{:S(2)}) collective-permute-start(f32[24,256]{1,0:T(8,128)S(1)} %slice_bitcast_fusion.2), channel_id=1, source_target_pairs={{0,130},{1,131},{2,128},{3,129},{4,134},{5,135},{6,132},{7,133},{8... | collective-permute-start | bytes 73736 | tf_op jit(solution)/shard_map/ppermute | solution.py:35
  77.8 4.9 %collective-permute-start.6 = (f32[24,256]{1,0:T(8,128)S(1)}, f32[24,256]{1,0:T(8,128)S(1)}, u32[]{:S(2)}, u32[]{:S(2)}) collective-permute-start(f32[24,256]{1,0:T(8,128)S(1)} %slice_bitcast_fusion.5), channel_id=1, source_target_pairs={{0,96},{4,100},{8,104},{12,108},{16,112},{20,116},{24,120},{28,124... | collective-permute-start | bytes 73736 | tf_op jit(solution)/shard_map/ppermute | solution.py:46
  79.3 6.0 %collective-permute-start.4 = (f32[24,256]{1,0:T(8,128)S(1)}, f32[24,256]{1,0:T(8,128)S(1)}, u32[]{:S(2)}, u32[]{:S(2)}) collective-permute-start(f32[24,256]{1,0:T(8,128)S(1)} %slice_bitcast_fusion.4), channel_id=1, source_target_pairs={{0,32},{4,36},{8,40},{12,44},{16,48},{20,52},{24,56},{28,60},{32,6... | collective-permute-start | bytes 73736 | tf_op jit(solution)/shard_map/ppermute | solution.py:46
  85.4 5.1 %collective-permute-start.7 = (f32[24,512]{1,0:T(8,128)S(1)}, f32[24,512]{1,0:T(8,128)S(1)}, u32[]{:S(2)}, u32[]{:S(2)}) collective-permute-start(f32[24,512]{1,0:T(8,128)S(1)} %pad_maximum_fusion.7), channel_id=1, source_target_pairs={{0,96},{4,100},{8,104},{12,108},{16,112},{20,116},{24,120},{28,124... | collective-permute-start | bytes 147464 | tf_op jit(solution)/shard_map/ppermute | solution.py:46
  86.5 6.7 %collective-permute-start.5 = (f32[24,512]{1,0:T(8,128)S(1)}, f32[24,512]{1,0:T(8,128)S(1)}, u32[]{:S(2)}, u32[]{:S(2)}) collective-permute-start(f32[24,512]{1,0:T(8,128)S(1)} %pad_maximum_fusion.6), channel_id=1, source_target_pairs={{0,32},{4,36},{8,40},{12,44},{16,48},{20,52},{24,56},{28,60},{32,6... | collective-permute-start | bytes 147464 | tf_op jit(solution)/shard_map/ppermute | solution.py:46
  93.3 4.3 %collective-permute-start.15 = (f32[24,2,384]{2,0,1:T(8,128)S(1)}, f32[24,2,384]{2,0,1:T(8,128)S(1)}, u32[]{:S(2)}, u32[]{:S(2)}) collective-permute-start(f32[24,2,384]{2,0,1:T(8,128)S(1)} %fusion.15), channel_id=1, source_target_pairs={{0,3},{1,2},{2,1},{3,0},{4,7},{5,6},{6,5},{7,4},{8,11},{9,10},{10,... | collective-permute-start | bytes 221192 | tf_op jit(solution)/shard_map/ppermute | solution.py:176
  93.4 6.1 %collective-permute-start.16 = (f32[24,2,384]{2,0,1:T(8,128)S(1)}, f32[24,2,384]{2,0,1:T(8,128)S(1)}, u32[]{:S(2)}, u32[]{:S(2)}) collective-permute-start(f32[24,2,384]{2,0,1:T(8,128)S(1)} %fusion.15), channel_id=1, source_target_pairs={{0,2},{1,3},{2,0},{3,1},{4,6},{5,7},{6,4},{7,5},{8,10},{9,11},{10,... | collective-permute-start | bytes 221192 | tf_op jit(solution)/shard_map/ppermute | solution.py:176
  95.3 4.3 %collective-permute-start.17 = (f32[24,2,384]{2,0,1:T(8,128)S(1)}, f32[24,2,384]{2,0,1:T(8,128)S(1)}, u32[]{:S(2)}, u32[]{:S(2)}) collective-permute-start(f32[24,2,384]{2,0,1:T(8,128)S(1)} %fusion.15), channel_id=1, source_target_pairs={{0,1},{1,0},{2,3},{3,2},{4,5},{5,4},{6,7},{7,6},{8,9},{9,8},{10,11... | collective-permute-start | bytes 221192 | tf_op jit(solution)/shard_map/ppermute | solution.py:176
  101.3 21.9 %all-to-all-start.3 = ((f32[64,8,128]{2,1,0:T(8,128)}), f32[64,8,128]{2,1,0:T(8,128)S(1)}, u32[]{:S(2)}, u32[]{:S(2)}) async-start(f32[64,8,128]{2,1,0:T(8,128)} %broadcast_in_dim.2), calls=%async_computation.3 | async-start | bytes 524288 | tf_op jit(solution)/shard_map/all_to_all | solution.py:188

commit v3 on v2

--- a/solution.py
+++ b/solution.py
@@ -10,6 +10,7 @@
 COLUMNS = 256
 QUARTERS = 4
 Z_ORDER = (4, 1, 3, -1, -3, 0, 2, -2)
+Z_SLICES = ((0, 1), (1, 3), (3, 5), (5, 6), (6, 7), (7, 8))
 Y_GROUPS = [[base + y for y in range(NY)] for base in range(0, NX * NZ * NY, NY)]
 
 
@@ -35,22 +36,24 @@
     return keep + lax.ppermute(away, ("pair", "sigma"), moves)
 
 
-def y_sum(block):
-    return jnp.sum(lax.all_to_all(block, "pair", 0, 0, axis_index_groups=Y_GROUPS, tiled=True), axis=0)
-
-
-def z_sum(low, high, up, down, keep):
-    half = low.shape[-1]
+def y_parts(block):
+    return lax.all_to_all(block, "pair", 0, 0, axis_index_groups=Y_GROUPS, tiled=True)
+
+
+def added(parts, rows=slice(None)):
+    return (parts[0, rows] + parts[1, rows]) + (parts[2, rows] + parts[3, rows])
+
+
+def z_sum(far, up, down, keep, above, below):
+    rows = keep.shape[0]
 
     def send(part, dz):
         return lax.ppermute(part, "pair", z_perm(dz))
 
-    low, high = send(low, -2), send(high, 2)
-    up, down = send(up, 1), send(down, -1)
-    above, below = keep[1] + up[1], keep[2] + down[1]
-    above = jnp.concatenate([above[..., :half], above[..., half:] + high], axis=-1)
-    below = jnp.concatenate([below[..., :half] + low, below[..., half:]], axis=-1)
-    return keep[0] + up[0] + down[0] + send(above, 2) + send(below, -2)
+    far, up, down = send(far, -2), send(up, 1), send(down, -1)
+    above = send(above + up[rows:], 2)
+    below = send(below + down[rows:] + far, -2)
+    return (keep + up[:rows] + down[:rows]) + (above + below)
 
 
 def spots():
@@ -59,7 +62,7 @@
     return lax.axis_index("sigma") ^ (2 * x), x, (position // NY) & (NZ - 1)
 
 
-def chi_streams(pairs, bins, table, streams):
+def chi_streams(pairs, bins, table, first, streams):
     pair_local, width = pairs.shape
     col_count = width // QUARTERS
     row_count = width // (NX * NZ * NY)
@@ -88,7 +91,7 @@
         by_pair = jnp.transpose(jnp.concatenate([weight, jnp.zeros((6, pair_local), jnp.float32)], axis=0))
         fetch(0).wait()
         for t in range(total // 128):
-            f, column = divmod(128 * t, col_count)
+            f, column = divmod(first + 128 * t, col_count)
             product = by_pair[:, f : f + 1] * pair_ref[0, :, column : column + 128].astype(jnp.float32)
             scaled_ref[:, 128 * t : 128 * t + 128] = product.astype(jnp.bfloat16)
         for step in range(QUARTERS):
@@ -137,36 +140,42 @@
     col_count = width // sigma_count
     pair_position = lax.axis_index("pair")
     quarter = spots()[0]
-    rc, n, half = row_count, COLUMNS, COLUMNS // 2
+    rc, n = row_count, COLUMNS
     every = (0, n)
     slots = [(y, keeps, k) for y in range(NY) for keeps in (0, 1) for k in range(NZ)]
-    b_stores = [(0, (y, keeps, k), every, keeps, Z_ORDER[k], y) for y, keeps, k in slots]
-    c_stores = [(keeps, (y, k), every, keeps, Z_ORDER[k], y) for y, keeps, k in slots]
+
+    def block(k):
+        return slice(k * rc, k * rc + rc)
+
+    b_stores = [(0, (y, block(keeps * NZ + k)), every, keeps, Z_ORDER[k], y) for y, keeps, k in slots]
+    c_stores = [(keeps, (block(y * NZ + k),), every, keeps, Z_ORDER[k], y) for y, keeps, k in slots]
     a_stores = []
     for y, keeps, k in slots:
-        if Z_ORDER[k] == 4:
-            a_stores += [(0, (y, keeps), (0, half), keeps, 4, y), (1, (y, keeps), (half, n), keeps, 4, y)]
-        else:
-            out, slot = divmod(k - 1, 2) if k < 5 else (2, k - 5)
-            a_stores.append((2 + out, (slot, y, keeps), every, keeps, Z_ORDER[k], y))
-    (b,), c, a = chi_streams(
-        pair_density_matrices,
-        energy_bins.T,
-        bin_weights,
-        [
-            ([(NY, NX, NZ, rc, n)], b_stores),
-            ([(NY, NZ, rc, n)] * 2, c_stores),
-            ([(NY, NX, rc, half)] * 2 + [(k, NY, NX, rc, n) for k in (2, 2, 3)], a_stores),
-        ],
+        out, (low, _) = next((j, span) for j, span in enumerate(Z_SLICES) if span[0] <= k < span[1])
+        a_stores.append((out, (block(((k - low) * NY + y) * NX + keeps),), every, keeps, Z_ORDER[k], y))
+
+    def streams(first, parts):
+        return chi_streams(pair_density_matrices, energy_bins.T, bin_weights, first, parts)
+
+    (b,), c = streams(0, [([(NY, NX * NZ * rc, n)], b_stores), ([(NY * NZ * rc, n)] * 2, c_stores)])
+    (a,) = streams(2 * n, [([((high - low) * NY * NX * rc, n) for low, high in Z_SLICES], a_stores)])
+
+    c = x_swap(*c)
+    b = y_parts(b)
+    b = x_swap(added(b, slice(0, NZ * rc)), added(b, slice(NZ * rc, None)))
+    c = y_parts(c.reshape(NY, NZ * rc, n))
+    bc = []
+    for low, high in Z_SLICES:
+        for k in range(low, high):
+            bc.append(jnp.concatenate([b[block(k)], added(c, block(k))], axis=0))
+    bc = lax.optimization_barrier(
+        (bc[0], jnp.concatenate(bc[1:3]), jnp.concatenate(bc[3:5]), bc[5], bc[6], bc[7])
     )
-
-    c = y_sum(x_swap(*c))
-    b = x_swap(*y_sum(b))
-    bc = jnp.concatenate([b, c], axis=2)
-    bc = lax.optimization_barrier((bc[0, :, :n], bc[0, :, n:], bc[1:3], bc[3:5], bc[5:]))
     bc = z_sum(*bc)
-    a = x_swap(*y_sum(z_sum(*a)))
-    polar = jnp.concatenate([bc, a], axis=1)
+    a = z_sum(*a).reshape(NY, NX * rc, n)
+    a = y_parts(a)
+    a = x_swap(added(a, slice(0, rc)), added(a, slice(rc, None)))
+    polar = jnp.concatenate([bc[:rc], bc[rc:], a], axis=1)
 
     root = jnp.sqrt(coulomb)
     root_rows = lax.dynamic_slice_in_dim(root, pair_position * row_count, row_count, 0)

time: 125 us -> 125 us (level)
  waiting for transfers between devices: 53.3 us -> 48 us
  Pallas kernels: 11.1 us -> 14.4 us
  other arithmetic: 6.92 us -> 8.83 us
    all_to_all x3, waiting for transfers between devices: 11.4 us -> 7.08 us  [y_parts(): lax.all_to_all(block, 'pair', 0, 0, axis_index_groups=Y_GROUPS, tiled=True)]
    ppermute x12 -> x10, waiting for transfers between devices: 23.3 us -> 19.8 us  [send(): return lax.ppermute(part, 'pair', z_perm(dz))]
    ppermute x3, waiting for transfers between devices: 0.01 us -> 3.38 us  [x_swap(): return keep + lax.ppermute(away, ('pair', 'sigma'), moves)]
    pallas_call x1 -> x2, Pallas kernels: 11.1 us -> 14.4 us  [chi_streams(): pl.pallas_call(body, in_specs=[pl.BlockSpec(memory_space=pltpu.HBM), pl.B...]
    all_to_all x1, starting transfers between devices: 6.87 us -> 10 us  [local(): lax.all_to_all(spread, 'pair', 0, 0, tiled=True)]
    ppermute x12 -> x10, starting transfers between devices: 21.4 us -> 18.7 us  [send(): return lax.ppermute(part, 'pair', z_perm(dz))]
    add x6 -> x10, other arithmetic: 2.73 us -> 5.05 us  [the longest x2 1.78 us: z_sum(): return keep + up[:rows] + down[:rows] + (above + below)]
    reduce_sum x3 -> x0, other arithmetic: 1.62 us -> none  [y_sum(): jnp.sum(lax.all_to_all(block, 'pair', 0, 0, axis_index_groups=Y_GROUPS, t...]
  transfers between devices with their start and end apart: 22 -> 20, of which waited for: 15 -> 11; matrix products, arithmetic and copies ran while one was open for 6% -> 8% of each run, Pallas kernels for 0% -> 5%
where the time goes in v3:
time: 125 us; the launch traced here: 124 us
  waiting for transfers between devices  48 us (38%)
  starting transfers between devices  47.4 us (38%)
  Pallas kernels  14.4 us (12%)
  other arithmetic  8.83 us (7%)
  local copies, waits for them, and re-layouts  3.56 us (3%)
    ppermute x10, waiting for transfers between devices, send(): return lax.ppermute(part, 'pair', z_perm(dz))  19.8 us
    ppermute x10, starting transfers between devices, send(): return lax.ppermute(part, 'pair', z_perm(dz))  18.7 us
    pallas_call x2, Pallas kernels, chi_streams(): pl.pallas_call(body, in_specs=[pl.BlockSpec(memory_space=pltpu.HBM), pl.B...  14.4 us
    all_to_all x1, waiting for transfers between devices, local(): lax.all_to_all(spread, 'pair', 0, 0, tiled=True)  14.3 us
    all_to_all x3, starting transfers between devices, y_parts(): lax.all_to_all(block, 'pair', 0, 0, axis_index_groups=Y_GROUPS, tiled=True)  12.7 us
    all_to_all x1, starting transfers between devices, local(): lax.all_to_all(spread, 'pair', 0, 0, tiled=True)  10 us
    all_to_all x3, waiting for transfers between devices, y_parts(): lax.all_to_all(block, 'pair', 0, 0, axis_index_groups=Y_GROUPS, tiled=True)  7.08 us
    add x3, other arithmetic, x_swap(): return keep + lax.ppermute(away, ('pair', 'sigma'), moves)  3.41 us
  transfers between devices with their start and end apart: 20, of which 11 were waited for; matrix products, arithmetic and copies ran while one was open for 8% of the time, Pallas kernels for 5%

profile of v3, /device:TPU:2, one launch (start us, length us, event | category | flops | bytes accessed | tf_op | source)
XLA Modules:
  0.0 123.9 jit_solution(8526390908905567452)
XLA Ops:
  0.6 0.0 copy-start
  0.6 0.7 copy-done
  1.4 0.7 copy-done.2
  2.0 8.1 %shard_map.68 = (f32[4,384,256]{2,1,0:T(8,128)}, f32[768,256]{1,0:T(8,128)S(1)}, f32[768,256]{1,0:T(8,128)S(1)}) custom-call(bf16[2048,1536]{1,0:T(8,128)(2,1)} %pairs_ref.3, s32[2,2048]{1,0:T(2,128)S(1)} %bitcast.43, f32[2,64]{1,0:T(2,128)S(1)} %copy-done.2), custom_call_target="tpu_custom_call" | custom-call | tf_op jit(solution)/shard_map/pallas_call | solution.py:111
  10.1 0.0 copy-start.1
  10.1 0.0 copy-start.3
  10.1 4.5 %all-to-all-start = ((f32[4,384,256]{2,1,0:T(8,128)}), f32[4,384,256]{2,1,0:T(8,128)}, u32[]{:S(2)}, u32[]{:S(2)}) async-start(f32[4,384,256]{2,1,0:T(8,128)} %get-tuple-element.17), calls=%async_computation | async-start | bytes 3145728 | tf_op jit(solution)/shard_map/all_to_all | solution.py:40
  14.6 0.0 copy-done.1
  14.6 0.0 copy-done.3
  14.6 6.3 %shard_map.69 = (f32[192,256]{1,0:T(8,128)S(1)}, f32[384,256]{1,0:T(8,128)S(1)}, f32[384,256]{1,0:T(8,128)S(1)}, f32[192,256]{1,0:T(8,128)S(1)}, f32[192,256]{1,0:T(8,128)S(1)}, /*index=5*/f32[192,256]{1,0:T(8,128)S(1)}) custom-call(bf16[2048,1536]{1,0:T(8,128)(2,1)} %pairs_ref.3, s32[2,2048]{1,0:T(2,128)S(1)} %bitcast.44, f32[2,64]{1,0:T(2,128)S(1)} %copy-done.3), custom_call_target="tpu_custom_call" | custom-call | tf_op jit(solution)/shard_map/pallas_call | solution.py:111
  21.0 2.0 %collective-permute-start.7 = (f32[384,256]{1,0:T(8,128)S(1)}, f32[384,256]{1,0:T(8,128)}, u32[]{:S(2)}, u32[]{:S(2)}) collective-permute-start(f32[384,256]{1,0:T(8,128)S(1)} %get-tuple-element.27), channel_id=1, source_target_pairs={{0,16},{4,20},{8,24},{12,28},{16,32},{20,36},{24,40},{28,44},{32,4... | collective-permute-start | bytes 1179656 | tf_op jit(solution)/shard_map/ppermute | solution.py:51
  22.9 1.5 %collective-permute-start.1 = (f32[768,256]{1,0:T(8,128)S(1)}, f32[768,256]{1,0:T(8,128)}, u32[]{:S(2)}, u32[]{:S(2)}) collective-permute-start(f32[768,256]{1,0:T(8,128)S(1)} %get-tuple-element.19), channel_id=1, source_target_pairs={{0,130},{1,131},{2,128},{3,129},{4,134},{5,135},{6,132},{7,133},{8... | collective-permute-start | bytes 2359304 | tf_op jit(solution)/shard_map/ppermute | solution.py:36
  24.4 4.0 %collective-permute-start.8 = (f32[384,256]{1,0:T(8,128)S(1)}, f32[384,256]{1,0:T(8,128)}, u32[]{:S(2)}, u32[]{:S(2)}) collective-permute-start(f32[384,256]{1,0:T(8,128)S(1)} %get-tuple-element.28), channel_id=1, source_target_pairs={{0,112},{4,116},{8,120},{12,124},{16,0},{20,4},{24,8},{28,12},{32,... | collective-permute-start | bytes 1179656 | tf_op jit(solution)/shard_map/ppermute | solution.py:51
  28.5 2.4 %collective-permute-start.10 = (f32[192,256]{1,0:T(8,128)S(1)}, f32[192,256]{1,0:T(8,128)S(1)}, u32[]{:S(2)}, u32[]{:S(2)}) collective-permute-start(f32[192,256]{1,0:T(8,128)S(1)} %get-tuple-element.31), channel_id=1, source_target_pairs={{0,96},{4,100},{8,104},{12,108},{16,112},{20,116},{24,120},{28,124... | collective-permute-start | bytes 589832 | tf_op jit(solution)/shard_map/ppermute | solution.py:51
  30.9 0.1 dynamic_slice.10
  30.9 0.1 dynamic-slice_negate_fusion
  31.0 5.0 %collective-permute-done.7 = f32[384,256]{1,0:T(8,128)} collective-permute-done((f32[384,256]{1,0:T(8,128)S(1)}, f32[384,256]{1,0:T(8,128)}, u32[]{:S(2)}, u32[]{:S(2)}) %collective-permute-start.7) | collective-permute-done | bytes 393248 | tf_op jit(solution)/shard_map/ppermute | solution.py:51
  36.0 1.0 slice_add_fusion.1
  37.0 0.1 collective-permute-start.9
  37.1 10.0 %collective-permute-done.10 = f32[192,256]{1,0:T(8,128)S(1)} collective-permute-done((f32[192,256]{1,0:T(8,128)S(1)}, f32[192,256]{1,0:T(8,128)S(1)}, u32[]{:S(2)}, u32[]{:S(2)}) %collective-permute-start.10) | collective-permute-done | bytes 196640 | tf_op jit(solution)/shard_map/ppermute | solution.py:51
  47.0 0.0 collective-permute-done.8
  47.1 1.0 fusion.9
  48.0 4.7 %collective-permute-start.11 = (f32[192,256]{1,0:T(8,128)S(1)}, f32[192,256]{1,0:T(8,128)S(1)}, u32[]{:S(2)}, u32[]{:S(2)}) collective-permute-start(f32[192,256]{1,0:T(8,128)S(1)} %fusion.9), channel_id=1, source_target_pairs={{0,96},{4,100},{8,104},{12,108},{16,112},{20,116},{24,120},{28,124... | collective-permute-start | bytes 589832 | tf_op jit(solution)/shard_map/ppermute | solution.py:51
  52.8 0.0 collective-permute-done.1
  52.8 2.1 %add.237 = f32[768,256]{1,0:T(8,128)} add(f32[768,256]{1,0:T(8,128)S(1)} %get-tuple-element.18, f32[768,256]{1,0:T(8,128)} %collective-permute-done.1) | non-fusion elementwise | flops 196608 | bytes 2359296 | tf_op jit(solution)/shard_map/add | solution.py:36
  54.9 0.0 all-to-all-done
  54.9 4.4 %all-to-all-start.1 = ((f32[4,192,256]{2,1,0:T(8,128)}), f32[4,192,256]{2,1,0:T(8,128)S(1)}, u32[]{:S(2)}, u32[]{:S(2)}) async-start(f32[4,192,256]{2,1,0:T(8,128)} %bitcast.3), calls=%async_computation.1 | async-start | bytes 1572864 | tf_op jit(solution)/shard_map/all_to_all | solution.py:40
  59.3 1.3 %fusion.12 = f32[192,256]{1,0:T(8,128)S(1)} fusion(f32[4,384,256]{2,1,0:T(8,128)} %all-to-all-done), kind=kLoop, calls=%fused_computation.17 | loop fusion | flops 147456 | bytes 983040 | tf_op jit(solution)/shard_map/add | solution.py:44
  60.5 0.8 collective-permute-start
  61.3 0.0 collective-permute-done.9
  61.3 0.0 collective-permute-done.11
  61.3 1.8 %fusion.10 = f32[192,256]{1,0:T(8,128)} fusion(f32[384,256]{1,0:T(8,128)} %collective-permute-done.8, f32[192,256]{1,0:T(8,128)S(1)} %get-tuple-element.26, f32[384,256]{1,0:T(8,128)} %collective-permute-done.7, f32[192,256]{1,0:T(8,128)S(1)} %collective-permute-done.9, f32[192,256]{1,0:T(8,128)S(1)} %collective-permute-done.11), kind=kLoop, calls=%fused_computation.13 | loop fusion | flops 196608 | bytes 1179648 | tf_op jit(solution)/shard_map/add | solution.py:56
  63.1 3.4 %collective-permute-done = f32[192,256]{1,0:T(8,128)S(1)} collective-permute-done((f32[192,256]{1,0:T(8,128)S(1)}, f32[192,256]{1,0:T(8,128)S(1)}, u32[]{:S(2)}, u32[]{:S(2)}) %collective-permute-start) | collective-permute-done | bytes 196640 | tf_op jit(solution)/shard_map/ppermute | solution.py:36
  66.5 1.3 %fusion.15 = f32[192,256]{1,0:T(8,128)S(1)} fusion(f32[192,256]{1,0:T(8,128)S(1)} %collective-permute-done, f32[4,384,256]{2,1,0:T(8,128)} %all-to-all-done), kind=kLoop, calls=%fused_computation.22 | loop fusion | flops 196608 | bytes 1179648 | tf_op jit(solution)/shard_map/add | solution.py:36
  67.8 1.0 all-to-all-done.1
  68.7 3.9 %all-to-all-start.2 = ((f32[4,48,256]{2,1,0:T(8,128)}), f32[4,48,256]{2,1,0:T(8,128)S(1)}, u32[]{:S(2)}, u32[]{:S(2)}) async-start(f32[4,48,256]{2,1,0:T(8,128)} %bitcast.12), calls=%async_computation.2 | async-start | bytes 393216 | tf_op jit(solution)/shard_map/all_to_all | solution.py:40
  72.7 0.1 collective-permute-start.2
  72.8 6.1 %all-to-all-done.2 = f32[4,48,256]{2,1,0:T(8,128)S(1)} async-done(((f32[4,48,256]{2,1,0:T(8,128)}), f32[4,48,256]{2,1,0:T(8,128)S(1)}, u32[]{:S(2)}, u32[]{:S(2)}) %all-to-all-start.2) | async-done | bytes 196640 | tf_op jit(solution)/shard_map/all_to_all | solution.py:40
  78.9 0.6 collective-permute-start.12
  79.6 0.0 collective-permute-start.3
  79.6 0.0 collective-permute-start.5
  79.6 0.1 collective-permute-done.2
  79.7 2.9 %collective-permute-start.4 = (f32[48,256]{1,0:T(8,128)S(1)}, f32[48,256]{1,0:T(8,128)S(1)}, u32[]{:S(2)}, u32[]{:S(2)}) collective-permute-start(f32[48,256]{1,0:T(8,128)S(1)} %slice_add_fusion.9), channel_id=1, source_target_pairs={{0,32},{4,36},{8,40},{12,44},{16,48},{20,52},{24,56},{28,60},{32,6... | collective-permute-start | bytes 147464 | tf_op jit(solution)/shard_map/ppermute | solution.py:51
  82.6 2.1 %collective-permute-done.5 = f32[48,256]{1,0:T(8,128)S(1)} collective-permute-done((f32[48,256]{1,0:T(8,128)S(1)}, f32[48,256]{1,0:T(8,128)S(1)}, u32[]{:S(2)}, u32[]{:S(2)}) %collective-permute-start.5) | collective-permute-done | bytes 49184 | tf_op jit(solution)/shard_map/ppermute | solution.py:51
  84.7 0.0 collective-permute-done.3
  84.7 2.5 %collective-permute-start.6 = (f32[48,256]{1,0:T(8,128)S(1)}, f32[48,256]{1,0:T(8,128)S(1)}, u32[]{:S(2)}, u32[]{:S(2)}) collective-permute-start(f32[48,256]{1,0:T(8,128)S(1)} %fusion.17), channel_id=1, source_target_pairs={{0,96},{4,100},{8,104},{12,108},{16,112},{20,116},{24,120},{28,124... | collective-permute-start | bytes 147464 | tf_op jit(solution)/shard_map/ppermute | solution.py:51
  87.2 0.0 collective-permute-done.12
  87.2 0.0 collective-permute-done.4
  87.2 2.6 %collective-permute-done.6 = f32[48,256]{1,0:T(8,128)S(1)} collective-permute-done((f32[48,256]{1,0:T(8,128)S(1)}, f32[48,256]{1,0:T(8,128)S(1)}, u32[]{:S(2)}, u32[]{:S(2)}) %collective-permute-start.6) | collective-permute-done | bytes 49184 | tf_op jit(solution)/shard_map/ppermute | solution.py:51
  89.8 0.1 fusion.16
  89.9 0.0 collective-permute-start.13
  90.0 3.0 %collective-permute-start.14 = (f32[24,2,384]{2,0,1:T(8,128)S(1)}, f32[24,2,384]{2,0,1:T(8,128)S(1)}, u32[]{:S(2)}, u32[]{:S(2)}) collective-permute-start(f32[24,2,384]{2,0,1:T(8,128)S(1)} %fusion.16), channel_id=1, source_target_pairs={{0,2},{1,3},{2,0},{3,1},{4,6},{5,7},{6,4},{7,5},{8,10},{9,11},{10,... | collective-permute-start | bytes 221192 | tf_op jit(solution)/shard_map/ppermute | solution.py:185
  93.0 0.0 collective-permute-start.15
  93.0 0.7 collective-permute-done.13
  93.7 2.7 %collective-permute-done.14 = f32[24,2,384]{2,0,1:T(8,128)S(1)} collective-permute-done((f32[24,2,384]{2,0,1:T(8,128)S(1)}, f32[24,2,384]{2,0,1:T(8,128)S(1)}, u32[]{:S(2)}, u32[]{:S(2)}) %collective-permute-start.14) | collective-permute-done | bytes 73760 | tf_op jit(solution)/shard_map/ppermute | solution.py:185
  96.4 0.0 collective-permute-done.15
  96.4 0.1 broadcast_select_fusion.7
  96.5 0.9 multiply_reduce_fusion
  97.5 0.7 broadcast_in_dim.2
  98.2 10.0 %all-to-all-start.3 = ((f32[64,8,128]{2,1,0:T(8,128)}), f32[64,8,128]{2,1,0:T(8,128)S(1)}, u32[]{:S(2)}, u32[]{:S(2)}) async-start(f32[64,8,128]{2,1,0:T(8,128)} %broadcast_in_dim.2), calls=%async_computation.3 | async-start | bytes 524288 | tf_op jit(solution)/shard_map/all_to_all | solution.py:197
  108.2 0.7 copy.10
  109.0 14.3 %all-to-all-done.3 = f32[64,8,128]{2,1,0:T(8,128)S(1)} async-done(((f32[64,8,128]{2,1,0:T(8,128)}), f32[64,8,128]{2,1,0:T(8,128)S(1)}, u32[]{:S(2)}, u32[]{:S(2)}) %all-to-all-start.3) | async-done | bytes 262176 | tf_op jit(solution)/shard_map/all_to_all | solution.py:197
  123.3 0.1 reduce_sum.19
  123.3 0.6 reshape.66
  (22 shorter events, 0.2 us)
Async XLA Ops:
  0.6 0.7 copy-start
  1.3 0.7 copy-start.2
  10.1 4.5 %copy-start.1 = (s32[2048,2]{0,1:T(2,128)S(1)}, s32[2048,2]{0,1:T(2,128)}, u32[]{:S(2)}) copy-start(s32[2048,2]{0,1:T(2,128)} %param.6) | copy-start | bytes 49156
  10.1 4.5 %copy-start.3 = (f32[2,64]{1,0:T(2,128)S(1)}, f32[2,64]{1,0:T(2,128)}, u32[]{:S(2)}) copy-start(f32[2,64]{1,0:T(2,128)} %table_ref.3) | copy-start | bytes 1540
  10.1 44.8 %all-to-all-start = ((f32[4,384,256]{2,1,0:T(8,128)}), f32[4,384,256]{2,1,0:T(8,128)}, u32[]{:S(2)}, u32[]{:S(2)}) async-start(f32[4,384,256]{2,1,0:T(8,128)} %get-tuple-element.17), calls=%async_computation | async-start | bytes 3145728 | tf_op jit(solution)/shard_map/all_to_all | solution.py:40
  14.6 16.3 %copy-start.5 = (f32[1536]{0:T(1024)S(1)}, f32[1536]{0:T(1024)}, u32[]{:S(2)}) copy-start(f32[1536]{0:T(1024)} %param.8) | copy-start | bytes 18436
  21.0 15.1 %collective-permute-start.7 = (f32[384,256]{1,0:T(8,128)S(1)}, f32[384,256]{1,0:T(8,128)}, u32[]{:S(2)}, u32[]{:S(2)}) collective-permute-start(f32[384,256]{1,0:T(8,128)S(1)} %get-tuple-element.27), channel_id=1, source_target_pairs={{0,16},{4,20},{8,24},{12,28},{16,32},{20,36},{24,40},{28,44},{32,4... | collective-permute-start | bytes 1179656 | tf_op jit(solution)/shard_map/ppermute | solution.py:51
  22.9 29.8 %collective-permute-start.1 = (f32[768,256]{1,0:T(8,128)S(1)}, f32[768,256]{1,0:T(8,128)}, u32[]{:S(2)}, u32[]{:S(2)}) collective-permute-start(f32[768,256]{1,0:T(8,128)S(1)} %get-tuple-element.19), channel_id=1, source_target_pairs={{0,130},{1,131},{2,128},{3,129},{4,134},{5,135},{6,132},{7,133},{8... | collective-permute-start | bytes 2359304 | tf_op jit(solution)/shard_map/ppermute | solution.py:36
  24.4 22.6 %collective-permute-start.8 = (f32[384,256]{1,0:T(8,128)S(1)}, f32[384,256]{1,0:T(8,128)}, u32[]{:S(2)}, u32[]{:S(2)}) collective-permute-start(f32[384,256]{1,0:T(8,128)S(1)} %get-tuple-element.28), channel_id=1, source_target_pairs={{0,112},{4,116},{8,120},{12,124},{16,0},{20,4},{24,8},{28,12},{32,... | collective-permute-start | bytes 1179656 | tf_op jit(solution)/shard_map/ppermute | solution.py:51
  28.5 18.6 %collective-permute-start.10 = (f32[192,256]{1,0:T(8,128)S(1)}, f32[192,256]{1,0:T(8,128)S(1)}, u32[]{:S(2)}, u32[]{:S(2)}) collective-permute-start(f32[192,256]{1,0:T(8,128)S(1)} %get-tuple-element.31), channel_id=1, source_target_pairs={{0,96},{4,100},{8,104},{12,108},{16,112},{20,116},{24,120},{28,124... | collective-permute-start | bytes 589832 | tf_op jit(solution)/shard_map/ppermute | solution.py:51
  37.0 24.4 %collective-permute-start.9 = (f32[192,256]{1,0:T(8,128)S(1)}, f32[192,256]{1,0:T(8,128)S(1)}, u32[]{:S(2)}, u32[]{:S(2)}) collective-permute-start(f32[192,256]{1,0:T(8,128)S(1)} %slice_add_fusion.1), channel_id=1, source_target_pairs={{0,32},{4,36},{8,40},{12,44},{16,48},{20,52},{24,56},{28,60},{32,6... | collective-permute-start | bytes 589832 | tf_op jit(solution)/shard_map/ppermute | solution.py:51
  48.0 13.3 %collective-permute-start.11 = (f32[192,256]{1,0:T(8,128)S(1)}, f32[192,256]{1,0:T(8,128)S(1)}, u32[]{:S(2)}, u32[]{:S(2)}) collective-permute-start(f32[192,256]{1,0:T(8,128)S(1)} %fusion.9), channel_id=1, source_target_pairs={{0,96},{4,100},{8,104},{12,108},{16,112},{20,116},{24,120},{28,124... | collective-permute-start | bytes 589832 | tf_op jit(solution)/shard_map/ppermute | solution.py:51
  54.9 13.9 %all-to-all-start.1 = ((f32[4,192,256]{2,1,0:T(8,128)}), f32[4,192,256]{2,1,0:T(8,128)S(1)}, u32[]{:S(2)}, u32[]{:S(2)}) async-start(f32[4,192,256]{2,1,0:T(8,128)} %bitcast.3), calls=%async_computation.1 | async-start | bytes 1572864 | tf_op jit(solution)/shard_map/all_to_all | solution.py:40
  60.5 5.9 %collective-permute-start = (f32[192,256]{1,0:T(8,128)S(1)}, f32[192,256]{1,0:T(8,128)S(1)}, u32[]{:S(2)}, u32[]{:S(2)}) collective-permute-start(f32[192,256]{1,0:T(8,128)S(1)} %fusion.12), channel_id=1, source_target_pairs={{0,130},{1,131},{2,128},{3,129},{4,134},{5,135},{6,132},{7,133},{8... | collective-permute-start | bytes 589832 | tf_op jit(solution)/shard_map/ppermute | solution.py:36
  68.7 10.2 %all-to-all-start.2 = ((f32[4,48,256]{2,1,0:T(8,128)}), f32[4,48,256]{2,1,0:T(8,128)S(1)}, u32[]{:S(2)}, u32[]{:S(2)}) async-start(f32[4,48,256]{2,1,0:T(8,128)} %bitcast.12), calls=%async_computation.2 | async-start | bytes 393216 | tf_op jit(solution)/shard_map/all_to_all | solution.py:40
  72.6 20.4 %copy-start.4 = (bf16[1536,512]{1,0:T(8,128)(2,1)S(1)}, bf16[1536,512]{1,0:T(8,128)(2,1)}, u32[]{:S(2)}) copy-start(bf16[1536,512]{1,0:T(8,128)(2,1)} %param.9) | copy-start | bytes 4718596
  72.7 7.0 %collective-permute-start.2 = (f32[96,256]{1,0:T(8,128)S(1)}, f32[96,256]{1,0:T(8,128)S(1)}, u32[]{:S(2)}, u32[]{:S(2)}) collective-permute-start(f32[96,256]{1,0:T(8,128)S(1)} %get-tuple-element.21), channel_id=1, source_target_pairs={{0,16},{4,20},{8,24},{12,28},{16,32},{20,36},{24,40},{28,44},{32,4... | collective-permute-start | bytes 294920 | tf_op jit(solution)/shard_map/ppermute | solution.py:51
  78.9 8.2 %collective-permute-start.12 = (f32[24,256]{1,0:T(8,128)S(1)}, f32[24,256]{1,0:T(8,128)S(1)}, u32[]{:S(2)}, u32[]{:S(2)}) collective-permute-start(f32[24,256]{1,0:T(8,128)S(1)} %fusion.20), channel_id=1, source_target_pairs={{0,130},{1,131},{2,128},{3,129},{4,134},{5,135},{6,132},{7,133},{8... | collective-permute-start | bytes 73736 | tf_op jit(solution)/shard_map/ppermute | solution.py:36
  79.6 5.1 %collective-permute-start.3 = (f32[96,256]{1,0:T(8,128)S(1)}, f32[96,256]{1,0:T(8,128)S(1)}, u32[]{:S(2)}, u32[]{:S(2)}) collective-permute-start(f32[96,256]{1,0:T(8,128)S(1)} %get-tuple-element.22), channel_id=1, source_target_pairs={{0,112},{4,116},{8,120},{12,124},{16,0},{20,4},{24,8},{28,12},{32,... | collective-permute-start | bytes 294920 | tf_op jit(solution)/shard_map/ppermute | solution.py:51
  79.6 5.1 %collective-permute-start.5 = (f32[48,256]{1,0:T(8,128)S(1)}, f32[48,256]{1,0:T(8,128)S(1)}, u32[]{:S(2)}, u32[]{:S(2)}) collective-permute-start(f32[48,256]{1,0:T(8,128)S(1)} %get-tuple-element.25), channel_id=1, source_target_pairs={{0,96},{4,100},{8,104},{12,108},{16,112},{20,116},{24,120},{28,124... | collective-permute-start | bytes 147464 | tf_op jit(solution)/shard_map/ppermute | solution.py:51
  79.7 7.5 %collective-permute-start.4 = (f32[48,256]{1,0:T(8,128)S(1)}, f32[48,256]{1,0:T(8,128)S(1)}, u32[]{:S(2)}, u32[]{:S(2)}) collective-permute-start(f32[48,256]{1,0:T(8,128)S(1)} %slice_add_fusion.9), channel_id=1, source_target_pairs={{0,32},{4,36},{8,40},{12,44},{16,48},{20,52},{24,56},{28,60},{32,6... | collective-permute-start | bytes 147464 | tf_op jit(solution)/shard_map/ppermute | solution.py:51
  84.7 5.1 %collective-permute-start.6 = (f32[48,256]{1,0:T(8,128)S(1)}, f32[48,256]{1,0:T(8,128)S(1)}, u32[]{:S(2)}, u32[]{:S(2)}) collective-permute-start(f32[48,256]{1,0:T(8,128)S(1)} %fusion.17), channel_id=1, source_target_pairs={{0,96},{4,100},{8,104},{12,108},{16,112},{20,116},{24,120},{28,124... | collective-permute-start | bytes 147464 | tf_op jit(solution)/shard_map/ppermute | solution.py:51
  89.9 3.8 %collective-permute-start.13 = (f32[24,2,384]{2,0,1:T(8,128)S(1)}, f32[24,2,384]{2,0,1:T(8,128)S(1)}, u32[]{:S(2)}, u32[]{:S(2)}) collective-permute-start(f32[24,2,384]{2,0,1:T(8,128)S(1)} %fusion.16), channel_id=1, source_target_pairs={{0,3},{1,2},{2,1},{3,0},{4,7},{5,6},{6,5},{7,4},{8,11},{9,10},{10,... | collective-permute-start | bytes 221192 | tf_op jit(solution)/shard_map/ppermute | solution.py:185
  90.0 6.5 %collective-permute-start.14 = (f32[24,2,384]{2,0,1:T(8,128)S(1)}, f32[24,2,384]{2,0,1:T(8,128)S(1)}, u32[]{:S(2)}, u32[]{:S(2)}) collective-permute-start(f32[24,2,384]{2,0,1:T(8,128)S(1)} %fusion.16), channel_id=1, source_target_pairs={{0,2},{1,3},{2,0},{3,1},{4,6},{5,7},{6,4},{7,5},{8,10},{9,11},{10,... | collective-permute-start | bytes 221192 | tf_op jit(solution)/shard_map/ppermute | solution.py:185
  93.0 3.4 %collective-permute-start.15 = (f32[24,2,384]{2,0,1:T(8,128)S(1)}, f32[24,2,384]{2,0,1:T(8,128)S(1)}, u32[]{:S(2)}, u32[]{:S(2)}) collective-permute-start(f32[24,2,384]{2,0,1:T(8,128)S(1)} %fusion.16), channel_id=1, source_target_pairs={{0,1},{1,0},{2,3},{3,2},{4,5},{5,4},{6,7},{7,6},{8,9},{9,8},{10,11... | collective-permute-start | bytes 221192 | tf_op jit(solution)/shard_map/ppermute | solution.py:185
  98.2 25.1 %all-to-all-start.3 = ((f32[64,8,128]{2,1,0:T(8,128)}), f32[64,8,128]{2,1,0:T(8,128)S(1)}, u32[]{:S(2)}, u32[]{:S(2)}) async-start(f32[64,8,128]{2,1,0:T(8,128)} %broadcast_in_dim.2), calls=%async_computation.3 | async-start | bytes 524288 | tf_op jit(solution)/shard_map/all_to_all | solution.py:197

commit v4 on v3

v4 whole, which is shorter than its diff:
```python
import jax
import jax.numpy as jnp
from jax import lax
from jax.experimental import pallas as pl
from jax.experimental.pallas import tpu as pltpu
from jax.sharding import PartitionSpec as P


NX, NZ, NY = 2, 8, 4
COLUMNS = 256
QUARTERS = 4
Z_ORDER = (4, 1, 3, -1, -3, 0, 2, -2)
Z_SLICES = ((0, 1), (1, 3), (3, 5), (5, 6), (6, 7), (7, 8))
Y_GROUPS = [[base + y for y in range(NY)] for base in range(0, NX * NZ * NY, NY)]


def place(position):
    return position // (NZ * NY), position // NY % NZ, position % NY


def z_perm(dz):
    moves = []
    for position in range(NX * NZ * NY):
        x, z, y = place(position)
        moves.append((position, (x * NZ + (z + dz) % NZ) * NY + y))
    return moves


def x_swap(away, keep):
    pair_count, sigma_count = lax.axis_size("pair"), lax.axis_size("sigma")
    moves = [
        (p * sigma_count + s, (p ^ (NZ * NY)) * sigma_count + (s ^ 2))
        for p in range(pair_count)
        for s in range(sigma_count)
    ]
    return keep + lax.ppermute(away, ("pair", "sigma"), moves)


def y_parts(block):
    return lax.all_to_all(block, "pair", 0, 0, axis_index_groups=Y_GROUPS, tiled=True)


def added(parts, rows=slice(None)):
    return (parts[0, rows] + parts[1, rows]) + (parts[2, rows] + parts[3, rows])


def z_send(part, dz):
    return lax.ppermute(part, "pair", z_perm(dz))


def z_sum(far, up, down, keep, above, below):
    rows = keep.shape[0]
    far, up, down = z_send(far, -2), z_send(up, 1), z_send(down, -1)
    above = z_send(above + up[rows:], 2)
    below = z_send(below + down[rows:] + far, -2)
    return (keep + up[:rows] + down[:rows]) + (above + below)


def z_sum_both(low, high, up, down, keep, above, below):
    rows, columns = keep.shape
    half = rows // 2
    low, high = z_send(low, -2), z_send(high, 2)
    up, down = z_send(up, 1), z_send(down, -1)

    def middle(low, high, up, down, keep, above, below, above_out, below_out, keep_out):
        above_out[:half] = above[:half] + up[rows : rows + half]
        above_out[half:] = (above[half:] + up[rows + half :]) + high[...]
        below_out[:half] = (below[:half] + down[rows : rows + half]) + low[...]
        below_out[half:] = below[half:] + down[rows + half :]
        keep_out[...] = (keep[...] + up[:rows]) + down[:rows]

    keep, above, below = (pltpu.with_memory_space_constraint(part, pltpu.HBM) for part in (keep, above, below))
    above, below, keep = on_chip(middle, [(rows, columns)] * 3)(low, high, up, down, keep, above, below)
    above, below = z_send(above, 2), z_send(below, -2)

    def last(above, below, keep, out):
        out[...] = keep[...] + (above[...] + below[...])

    return on_chip(last, [(rows, columns)])(above, below, keep)[0]


def on_chip(body, shapes):
    return pl.pallas_call(
        body,
        out_shape=[jax.ShapeDtypeStruct(shape, jnp.float32) for shape in shapes],
        compiler_params=pltpu.CompilerParams(vmem_limit_bytes=12 << 20),
    )


def halves_added(parts):
    half = parts.shape[1] // 2

    def body(parts, first, second):
        first[...] = added(parts, slice(0, half))
        second[...] = added(parts, slice(half, None))

    return on_chip(body, [(half, parts.shape[2])] * 2)(parts)


def spots():
    position = lax.axis_index("pair")
    x = position // (NZ * NY)
    return lax.axis_index("sigma") ^ (2 * x), x, (position // NY) & (NZ - 1)


def fetcher(pairs_ref, pair_ref, done):
    col_count = pair_ref.shape[2]
    quarter = spots()[0]

    def first_column(step):
        return pl.multiple_of(((quarter + step) & (QUARTERS - 1)) * col_count, 128)

    def fetch(step):
        part = pairs_ref.at[:, pl.ds(first_column(step), col_count)]
        return pltpu.make_async_copy(part, pair_ref.at[step], done.at[step])

    return first_column, fetch


def multiply(first_column, fetch, pair_ref, scaled_ref, rows_ref, waited):
    for step in range(QUARTERS):
        if step >= waited:
            fetch(step).wait()
        rows_ref[pl.ds(first_column(step), pair_ref.shape[2]), :] = lax.dot_general(
            pair_ref[step],
            scaled_ref[:, : rows_ref.shape[1]],
            (((0,), (0,)), ((), ())),
            preferred_element_type=jnp.float32,
        )


def store(streams, outs, rows_ref):
    _, x, z = spots()
    before = 0
    for k, (stream, stores) in enumerate(streams):
        for out, index, keeps, dz, y in stores:
            at = ((x if keeps else 1 - x) * NZ + ((z + dz) & (NZ - 1))) * NY + y
            row_count = rows_ref.shape[0] // (NX * NZ * NY)
            rows = pl.ds(pl.multiple_of(at * row_count, 8), row_count)
            outs[before + out][index] = rows_ref[rows, k * COLUMNS : k * COLUMNS + COLUMNS]
        before += len(stream)


def first_streams(pairs, bins, table, streams):
    pair_local, width = pairs.shape
    col_count = width // QUARTERS
    total = 2 * col_count
    now = COLUMNS * len(streams)
    shapes = [shape for stream, _ in streams for shape in stream]
    count = len(shapes)

    def body(pairs_ref, bins_hbm, table_hbm, *refs):
        later_ref, bins_ref, table_ref, pair_ref, scaled_ref, rows_ref, done, small = refs[count:]
        first_column, fetch = fetcher(pairs_ref, pair_ref, done)
        bins_copy = pltpu.make_async_copy(bins_hbm, bins_ref, small.at[0])
        table_copy = pltpu.make_async_copy(table_hbm, table_ref, small.at[1])
        bins_copy.start()
        table_copy.start()
        for step in range(QUARTERS):
            fetch(step).start()
        bins_copy.wait()
        table_copy.wait()
        index = bins_ref[...]
        upper = lax.broadcasted_iota(jnp.int32, index.shape, 0) > 0
        picked = jnp.zeros(index.shape, jnp.float32)
        for level in range(table.shape[1]):
            picked = jnp.where(index == level, jnp.where(upper, table_ref[1, level], table_ref[0, level]), picked)
        weight = picked / jnp.float32(pair_local * NX * NZ * NY)
        by_pair = jnp.transpose(jnp.concatenate([weight, jnp.zeros((6, pair_local), jnp.float32)], axis=0))
        fetch(0).wait()

        def scaled(t):
            f, column = divmod(128 * t, col_count)
            product = by_pair[:, f : f + 1] * pair_ref[0, :, column : column + 128].astype(jnp.float32)
            return product.astype(jnp.bfloat16)

        for t in range(now // 128):
            scaled_ref[:, 128 * t : 128 * t + 128] = scaled(t)
        multiply(first_column, fetch, pair_ref, scaled_ref, rows_ref, 1)
        for t in range(now // 128, total // 128):
            later_ref[:, 128 * t - now : 128 * t - now + 128] = scaled(t)
        store(streams, refs, rows_ref)

    held = [pltpu.with_memory_space_constraint(array, pltpu.HBM) for array in (pairs, bins, table)]
    outs = pl.pallas_call(
        body,
        in_specs=[pl.BlockSpec(memory_space=pltpu.HBM)] * 3,
        out_specs=[pl.BlockSpec(memory_space=pltpu.VMEM)] * (count + 1),
        out_shape=[jax.ShapeDtypeStruct(shape, jnp.float32) for shape in shapes]
        + [jax.ShapeDtypeStruct((pair_local, total - now), jnp.bfloat16)],
        scratch_shapes=[
            pltpu.VMEM(bins.shape, jnp.int32),
            pltpu.SMEM(table.shape, jnp.float32),
            pltpu.VMEM((QUARTERS, pair_local, col_count), jnp.bfloat16),
            pltpu.VMEM((pair_local, now), jnp.bfloat16),
            pltpu.VMEM((width, now), jnp.float32),
            pltpu.SemaphoreType.DMA((QUARTERS,)),
            pltpu.SemaphoreType.DMA((2,)),
        ],
        compiler_params=pltpu.CompilerParams(vmem_limit_bytes=36 << 20),
    )(*held)
    return outs[:-1], outs[-1]


def last_stream(pairs, scaled, stream):
    pair_local, width = pairs.shape
    columns = scaled.shape[1]
    shapes = stream[0]

    def body(pairs_ref, scaled_ref, *refs):
        pair_ref, rows_ref, done = refs[len(shapes) :]
        first_column, fetch = fetcher(pairs_ref, pair_ref, done)
        for step in range(QUARTERS):
            fetch(step).start()
        multiply(first_column, fetch, pair_ref, scaled_ref, rows_ref, 0)
        store([stream], refs, rows_ref)

    return pl.pallas_call(
        body,
        in_specs=[pl.BlockSpec(memory_space=pltpu.HBM), pl.BlockSpec(memory_space=pltpu.VMEM)],
        out_specs=[pl.BlockSpec(shape, lambda: (0, 0)) for shape in shapes],
        out_shape=[pltpu.HBM(shape, jnp.float32) for shape in shapes],
        scratch_shapes=[
            pltpu.VMEM((QUARTERS, pair_local, width // QUARTERS), jnp.bfloat16),
            pltpu.VMEM((width, columns), jnp.float32),
            pltpu.SemaphoreType.DMA((QUARTERS,)),
        ],
        compiler_params=pltpu.CompilerParams(vmem_limit_bytes=24 << 20),
    )(pltpu.with_memory_space_constraint(pairs, pltpu.HBM), scaled)


def local(pair_density_matrices, energy_bins, bin_weights, coulomb, state_matrices):
    width = pair_density_matrices.shape[1]
    pair_count = lax.axis_size("pair")
    sigma_count = lax.axis_size("sigma")
    row_count = width // pair_count
    col_count = width // sigma_count
    pair_position = lax.axis_index("pair")
    quarter = spots()[0]
    rc, n = row_count, COLUMNS
    slots = [(y, keeps, k) for y in range(NY) for keeps in (0, 1) for k in range(NZ)]

    def block(k):
        return slice(k * rc, k * rc + rc)

    b_stores = [(0, (y, block(keeps * NZ + k)), keeps, Z_ORDER[k], y) for y, keeps, k in slots]
    c_stores = [(keeps, (block(y * NZ + k),), keeps, Z_ORDER[k], y) for y, keeps, k in slots]
    a_shapes = [(NY * NX * rc // 2, n)] * 2
    a_shapes += [((high - low) * NY * NX * rc, n) for low, high in Z_SLICES[1:]]
    a_stores = []
    for y, keeps, k in slots:
        if k == 0:
            out, row = divmod(y * NX + keeps, NY * NX // 2)
        else:
            out, (low, _) = next((j, span) for j, span in enumerate(Z_SLICES) if span[0] <= k < span[1])
            out, row = out + 1, ((k - low) * NY + y) * NX + keeps
        a_stores.append((out, (block(row),), keeps, Z_ORDER[k], y))

    (b, *c), scaled = first_streams(
        pair_density_matrices,
        energy_bins.T,
        bin_weights,
        [([(NY, NX * NZ * rc, n)], b_stores), ([(NY * NZ * rc, n)] * 2, c_stores)],
    )
    a = last_stream(pair_density_matrices, scaled, (a_shapes, a_stores))

    c = x_swap(*c)
    b = y_parts(b)
    b = x_swap(*halves_added(b))
    c = y_parts(c.reshape(NY, NZ * rc, n))
    bc = []
    for low, high in Z_SLICES:
        for k in range(low, high):
            bc.append(jnp.concatenate([b[block(k)], added(c, block(k))], axis=0))
    bc = lax.optimization_barrier(
        (bc[0], jnp.concatenate(bc[1:3]), jnp.concatenate(bc[3:5]), bc[5], bc[6], bc[7])
    )
    bc = z_sum(*bc)
    a = z_sum_both(*a).reshape(NY, NX * rc, n)
    a = y_parts(a)
    a = x_swap(added(a, slice(0, rc)), added(a, slice(rc, None)))
    polar = jnp.concatenate([bc[:rc], bc[rc:], a], axis=1)

    root = jnp.sqrt(coulomb)
    root_rows = lax.dynamic_slice_in_dim(root, pair_position * row_count, row_count, 0)
    root_columns = lax.dynamic_slice_in_dim(root, quarter * col_count, col_count, 0)
    screened = -root_rows[:, None, None] * polar.reshape(row_count, -1, col_count) * root_columns[None, None, :]
    parts = [screened] + [
        lax.ppermute(screened, "sigma", [(s, s ^ k) for s in range(sigma_count)]) for k in range(1, sigma_count)
    ]
    for bit in (1, 2):
        odd = (quarter & bit) != 0
        parts = [jnp.where(odd, parts[k ^ bit], parts[k]) for k in range(sigma_count)]
    states_wide = state_matrices.astype(jnp.float32)
    applied = jnp.einsum(
        "rfc,cn->rfn", jnp.concatenate(parts, axis=2), states_wide, precision=lax.Precision.HIGHEST
    )
    own_states = lax.dynamic_slice_in_dim(states_wide, pair_position * row_count, row_count, 0)
    total = jnp.sum(own_states[:, None, :] * applied, axis=0) / jnp.float32(width)
    spread = jnp.broadcast_to(total.reshape(8, -1)[None], (pair_count, 8, total.size // 8))
    total = jnp.sum(lax.all_to_all(spread, "pair", 0, 0, tiled=True), axis=0).reshape(total.shape)
    return (applied, total)


def solution(mesh):
    return jax.shard_map(
        local,
        mesh=mesh,
        in_specs=(P("pair", None), P("pair", None), P(), P(), P(None, "sigma")),
        out_specs=(P("pair", None, "sigma"), P(None, "sigma")),
        check_vma=False,
    )
```

time: 125 us -> 123 us (0.984)
  starting transfers between devices: 47.4 us -> 54.5 us
  other arithmetic: 8.83 us -> 3.49 us
  waiting for transfers between devices: 48 us -> 43.1 us
  Pallas kernels: 14.4 us -> 16.2 us
    ppermute x10 -> x11, starting transfers between devices: 18.7 us -> 26.9 us  [z_send(): return lax.ppermute(part, 'pair', z_perm(dz))]
    all_to_all x3, waiting for transfers between devices: 7.08 us -> 0.51 us  [y_parts(): lax.all_to_all(block, 'pair', 0, 0, axis_index_groups=Y_GROUPS, tiled=True)]
    add x3, other arithmetic: 3.41 us -> 1.03 us  [x_swap(): return keep + lax.ppermute(away, ('pair', 'sigma'), moves)]
    all_to_all x1, starting transfers between devices: 10 us -> 7.77 us  [local(): lax.all_to_all(spread, 'pair', 0, 0, tiled=True)]
    add x4 -> x2, other arithmetic: 1.94 us -> 0.02 us  [the longest x1 0.01 us: z_sum(): below = z_send(below + down[rows:] + far, -2)]
    ppermute x3, waiting for transfers between devices: 3.38 us -> 5.27 us  [x_swap(): return keep + lax.ppermute(away, ('pair', 'sigma'), moves)]
    ppermute x3, starting transfers between devices: 2.9 us -> 4.73 us  [x_swap(): return keep + lax.ppermute(away, ('pair', 'sigma'), moves)]
    pallas_call x2 -> x5, Pallas kernels: 14.4 us -> 16.2 us  [the longest x1 7.73 us: first_streams(): pl.pallas_call(body, in_specs=[pl.BlockSpec(memory_space=pltpu.HBM)] * 3,...]
  transfers between devices with their start and end apart: 20 -> 21, of which waited for: 11 -> 12; matrix products, arithmetic and copies ran while one was open for 8% -> 3% of each run, Pallas kernels for 5% -> 7%
where the time goes in v4:
time: 123 us; the launch traced here: 122 us
  starting transfers between devices  54.5 us (44%)
  waiting for transfers between devices  43.1 us (35%)
  Pallas kernels  16.2 us (13%)
  other arithmetic  3.49 us (3%)
  local copies, waits for them, and re-layouts  3.04 us (2%)
    ppermute x11, starting transfers between devices, z_send(): return lax.ppermute(part, 'pair', z_perm(dz))  26.9 us
    ppermute x11, waiting for transfers between devices, z_send(): return lax.ppermute(part, 'pair', z_perm(dz))  19.6 us
    all_to_all x1, waiting for transfers between devices, local(): lax.all_to_all(spread, 'pair', 0, 0, tiled=True)  14.3 us
    all_to_all x3, starting transfers between devices, y_parts(): lax.all_to_all(block, 'pair', 0, 0, axis_index_groups=Y_GROUPS, tiled=True)  12.3 us
    all_to_all x1, starting transfers between devices, local(): lax.all_to_all(spread, 'pair', 0, 0, tiled=True)  7.77 us
    pallas_call x1, Pallas kernels, first_streams(): pl.pallas_call(body, in_specs=[pl.BlockSpec(memory_space=pltpu.HBM)] * 3,...  7.73 us
    pallas_call x1, Pallas kernels, last_stream(): pl.pallas_call(body, in_specs=[pl.BlockSpec(memory_space=pltpu.HBM), pl.B...  6.5 us
    ppermute x3, waiting for transfers between devices, x_swap(): return keep + lax.ppermute(away, ('pair', 'sigma'), moves)  5.27 us
  transfers between devices with their start and end apart: 21, of which 12 were waited for; matrix products, arithmetic and copies ran while one was open for 3% of the time, Pallas kernels for 7%

profile of v4, /device:TPU:2, one launch (start us, length us, event | category | flops | bytes accessed | tf_op | source)
XLA Modules:
  0.0 122.1 jit_solution(8905956236591523481)
XLA Ops:
  0.6 7.7 %shard_map.68 = (f32[4,384,256]{2,1,0:T(8,128)}, f32[768,256]{1,0:T(8,128)S(1)}, f32[768,256]{1,0:T(8,128)S(1)}, bf16[2048,256]{1,0:T(8,128)(2,1)S(1)}) custom-call(bf16[2048,1536]{1,0:T(8,128)(2,1)} %pairs_ref.3, s32[2,2048]{1,0:T(2,128)} %bitcast.40, f32[2,64]{1,0:T(2,128)} %table_hbm.1), custom_call_target="tpu_custom_call" | custom-call | tf_op jit(solution)/shard_map/pallas_call | solution.py:185
  8.4 0.0 copy-start
  8.4 0.9 copy-done
  9.3 4.5 %all-to-all-start = ((f32[4,384,256]{2,1,0:T(8,128)}), f32[4,384,256]{2,1,0:T(8,128)S(1)}, u32[]{:S(2)}, u32[]{:S(2)}) async-start(f32[4,384,256]{2,1,0:T(8,128)} %get-tuple-element.24), calls=%async_computation | async-start | bytes 3145728 | tf_op jit(solution)/shard_map/all_to_all | solution.py:40
  13.7 1.5 %collective-permute-start.1 = (f32[768,256]{1,0:T(8,128)}, f32[768,256]{1,0:T(8,128)S(1)}, u32[]{:S(2)}, u32[]{:S(2)}) collective-permute-start(f32[768,256]{1,0:T(8,128)} %copy-done), channel_id=1, source_target_pairs={{0,130},{1,131},{2,128},{3,129},{4,134},{5,135},{6,132},{7,133},{8... | collective-permute-start | bytes 2359304 | tf_op jit(solution)/shard_map/ppermute | solution.py:36
  15.2 6.5 %shard_map.70 = (f32[96,256]{1,0:T(8,128)}, f32[96,256]{1,0:T(8,128)}, f32[384,256]{1,0:T(8,128)}, f32[384,256]{1,0:T(8,128)}, f32[192,256]{1,0:T(8,128)}, /*index=5*/f32[192,256]{1,0:T(8,128)}, f32[192,256]{1,0:T(8,128)}) custom-call(bf16[2048,1536]{1,0:T(8,128)(2,1)} %pairs_ref.3, bf16[2048,256]{1,0:T(8,128)(2,1)S(1)} %get-tuple-element.35.scaled_ref), custom_call_target="tpu_custom_call" | custom-call | tf_op jit(solution)/shard_map/pallas_call | solution.py:218
  21.7 5.9 %collective-permute-start.10 = (f32[384,256]{1,0:T(8,128)}, f32[384,256]{1,0:T(8,128)S(1)}, u32[]{:S(2)}, u32[]{:S(2)}) collective-permute-start(f32[384,256]{1,0:T(8,128)} %get-tuple-element.39), channel_id=1, source_target_pairs={{0,112},{4,116},{8,120},{12,124},{16,0},{20,4},{24,8},{28,12},{32,... | collective-permute-start | bytes 1179656 | tf_op jit(solution)/shard_map/ppermute | solution.py:48
  27.7 0.0 collective-permute-start.9
  27.7 5.3 %collective-permute-done.1 = f32[768,256]{1,0:T(8,128)S(1)} collective-permute-done((f32[768,256]{1,0:T(8,128)}, f32[768,256]{1,0:T(8,128)S(1)}, u32[]{:S(2)}, u32[]{:S(2)}) %collective-permute-start.1) | collective-permute-done | bytes 786464 | tf_op jit(solution)/shard_map/ppermute | solution.py:36
  32.9 1.0 add.180
  33.9 0.5 all-to-all-done.parts
  34.4 4.2 %all-to-all-start.1 = ((f32[4,192,256]{2,1,0:T(8,128)}), f32[4,192,256]{2,1,0:T(8,128)}, u32[]{:S(2)}, u32[]{:S(2)}) async-start(f32[4,192,256]{2,1,0:T(8,128)} %bitcast.37), calls=%async_computation.1 | async-start | bytes 1572864 | tf_op jit(solution)/shard_map/all_to_all | solution.py:40
  38.6 0.0 copy-done.4
  38.6 6.4 %collective-permute-start.7 = (f32[96,256]{1,0:T(8,128)S(1)}, f32[96,256]{1,0:T(8,128)S(1)}, u32[]{:S(2)}, u32[]{:S(2)}) collective-permute-start(f32[96,256]{1,0:T(8,128)S(1)} %copy-done.4), channel_id=1, source_target_pairs={{0,96},{4,100},{8,104},{12,108},{16,112},{20,116},{24,120},{28,124... | collective-permute-start | bytes 294920 | tf_op jit(solution)/shard_map/ppermute | solution.py:48
  45.0 0.0 copy-done.3
  45.0 0.0 collective-permute-start.8
  45.0 3.2 %collective-permute-done.7.low = f32[96,256]{1,0:T(8,128)S(1)} collective-permute-done((f32[96,256]{1,0:T(8,128)S(1)}, f32[96,256]{1,0:T(8,128)S(1)}, u32[]{:S(2)}, u32[]{:S(2)}) %collective-permute-start.7) | collective-permute-done | bytes 98336 | tf_op jit(solution)/shard_map/ppermute | solution.py:48
  48.2 4.0 %collective-permute-done.8.high = f32[96,256]{1,0:T(8,128)S(1)} collective-permute-done((f32[96,256]{1,0:T(8,128)S(1)}, f32[96,256]{1,0:T(8,128)S(1)}, u32[]{:S(2)}, u32[]{:S(2)}) %collective-permute-start.8) | collective-permute-done | bytes 98336 | tf_op jit(solution)/shard_map/ppermute | solution.py:48
  52.2 0.0 collective-permute-done.10.down
  52.2 0.0 collective-permute-done.9.up
  52.2 1.2 shard_map.71
  53.4 0.1 collective-permute-start.11
  53.5 4.1 %collective-permute-start.12 = (f32[192,256]{1,0:T(8,128)S(1)}, f32[192,256]{1,0:T(8,128)S(1)}, u32[]{:S(2)}, u32[]{:S(2)}) collective-permute-start(f32[192,256]{1,0:T(8,128)S(1)} %get-tuple-element.44), channel_id=1, source_target_pairs={{0,96},{4,100},{8,104},{12,108},{16,112},{20,116},{24,120},{28,124... | collective-permute-start | bytes 589832 | tf_op jit(solution)/shard_map/ppermute | solution.py:48
  57.6 0.1 shard_map.69
  57.7 1.6 %collective-permute-start = (f32[192,256]{1,0:T(8,128)S(1)}, f32[192,256]{1,0:T(8,128)S(1)}, u32[]{:S(2)}, u32[]{:S(2)}) collective-permute-start(f32[192,256]{1,0:T(8,128)S(1)} %get-tuple-element.26), channel_id=1, source_target_pairs={{0,130},{1,131},{2,128},{3,129},{4,134},{5,135},{6,132},{7,133},{8... | collective-permute-start | bytes 589832 | tf_op jit(solution)/shard_map/ppermute | solution.py:36
  59.3 0.1 dynamic_slice.10
  59.4 0.1 dynamic-slice_negate_fusion
  59.5 4.6 %collective-permute-done.11.above = f32[192,256]{1,0:T(8,128)S(1)} collective-permute-done((f32[192,256]{1,0:T(8,128)S(1)}, f32[192,256]{1,0:T(8,128)S(1)}, u32[]{:S(2)}, u32[]{:S(2)}) %collective-permute-start.11) | collective-permute-done | bytes 196640 | tf_op jit(solution)/shard_map/ppermute | solution.py:48
  64.1 0.0 collective-permute-done.12.below
  64.1 0.7 shard_map.72
  64.8 0.0 collective-permute-done
  64.8 0.0 all-to-all-done.1
  64.9 3.7 %all-to-all-start.2 = ((f32[4,48,256]{2,1,0:T(8,128)}), f32[4,48,256]{2,1,0:T(8,128)S(1)}, u32[]{:S(2)}, u32[]{:S(2)}) async-start(f32[4,48,256]{2,1,0:T(8,128)} %bitcast.10), calls=%async_computation.2 | async-start | bytes 393216 | tf_op jit(solution)/shard_map/all_to_all | solution.py:40
  68.5 1.1 fusion.18
  69.6 1.0 fusion.22
  70.6 4.3 %collective-permute-start.3 = (f32[96,256]{1,0:T(8,128)S(1)}, f32[96,256]{1,0:T(8,128)S(1)}, u32[]{:S(2)}, u32[]{:S(2)}) collective-permute-start(f32[96,256]{1,0:T(8,128)S(1)} %get-tuple-element.31), channel_id=1, source_target_pairs={{0,112},{4,116},{8,120},{12,124},{16,0},{20,4},{24,8},{28,12},{32,... | collective-permute-start | bytes 294920 | tf_op jit(solution)/shard_map/ppermute | solution.py:48
  74.9 0.0 collective-permute-start.5
  74.9 0.0 all-to-all-done.2
  75.0 1.6 %collective-permute-start.13 = (f32[24,256]{1,0:T(8,128)S(1)}, f32[24,256]{1,0:T(8,128)S(1)}, u32[]{:S(2)}, u32[]{:S(2)}) collective-permute-start(f32[24,256]{1,0:T(8,128)S(1)} %fusion.13), channel_id=1, source_target_pairs={{0,130},{1,131},{2,128},{3,129},{4,134},{5,135},{6,132},{7,133},{8... | collective-permute-start | bytes 73736 | tf_op jit(solution)/shard_map/ppermute | solution.py:36
  76.6 2.1 %collective-permute-start.2 = (f32[96,256]{1,0:T(8,128)S(1)}, f32[96,256]{1,0:T(8,128)S(1)}, u32[]{:S(2)}, u32[]{:S(2)}) collective-permute-start(f32[96,256]{1,0:T(8,128)S(1)} %get-tuple-element.30), channel_id=1, source_target_pairs={{0,16},{4,20},{8,24},{12,28},{16,32},{20,36},{24,40},{28,44},{32,4... | collective-permute-start | bytes 294920 | tf_op jit(solution)/shard_map/ppermute | solution.py:48
  78.7 1.4 %collective-permute-done.5 = f32[48,256]{1,0:T(8,128)S(1)} collective-permute-done((f32[48,256]{1,0:T(8,128)S(1)}, f32[48,256]{1,0:T(8,128)S(1)}, u32[]{:S(2)}, u32[]{:S(2)}) %collective-permute-start.5) | collective-permute-done | bytes 49184 | tf_op jit(solution)/shard_map/ppermute | solution.py:48
  80.0 0.0 collective-permute-done.3
  80.1 3.6 %collective-permute-start.6 = (f32[48,256]{1,0:T(8,128)S(1)}, f32[48,256]{1,0:T(8,128)S(1)}, u32[]{:S(2)}, u32[]{:S(2)}) collective-permute-start(f32[48,256]{1,0:T(8,128)S(1)} %fusion.10), channel_id=1, source_target_pairs={{0,96},{4,100},{8,104},{12,108},{16,112},{20,116},{24,120},{28,124... | collective-permute-start | bytes 147464 | tf_op jit(solution)/shard_map/ppermute | solution.py:48
  83.7 0.2 collective-permute-done.2
  83.9 0.4 collective-permute-start.4
  84.2 0.0 collective-permute-done.13
  84.3 1.6 %collective-permute-done.6 = f32[48,256]{1,0:T(8,128)S(1)} collective-permute-done((f32[48,256]{1,0:T(8,128)S(1)}, f32[48,256]{1,0:T(8,128)S(1)}, u32[]{:S(2)}, u32[]{:S(2)}) %collective-permute-start.6) | collective-permute-done | bytes 49184 | tf_op jit(solution)/shard_map/ppermute | solution.py:48
  85.8 4.7 %collective-permute-done.4 = f32[48,256]{1,0:T(8,128)S(1)} collective-permute-done((f32[48,256]{1,0:T(8,128)S(1)}, f32[48,256]{1,0:T(8,128)S(1)}, u32[]{:S(2)}, u32[]{:S(2)}) %collective-permute-start.4) | collective-permute-done | bytes 49184 | tf_op jit(solution)/shard_map/ppermute | solution.py:48
  90.6 0.1 fusion.9
  90.7 0.0 collective-permute-start.14
  90.7 2.8 %collective-permute-start.15 = (f32[24,2,384]{2,0,1:T(8,128)S(1)}, f32[24,2,384]{2,0,1:T(8,128)S(1)}, u32[]{:S(2)}, u32[]{:S(2)}) collective-permute-start(f32[24,2,384]{2,0,1:T(8,128)S(1)} %fusion.9), channel_id=1, source_target_pairs={{0,2},{1,3},{2,0},{3,1},{4,6},{5,7},{6,4},{7,5},{8,10},{9,11},{10,... | collective-permute-start | bytes 221192 | tf_op jit(solution)/shard_map/ppermute | solution.py:289
  93.5 0.0 collective-permute-start.16
  93.5 0.0 copy-done.1
  93.5 1.0 collective-permute-done.14
  94.5 2.4 %collective-permute-done.15 = f32[24,2,384]{2,0,1:T(8,128)S(1)} collective-permute-done((f32[24,2,384]{2,0,1:T(8,128)S(1)}, f32[24,2,384]{2,0,1:T(8,128)S(1)}, u32[]{:S(2)}, u32[]{:S(2)}) %collective-permute-start.15) | collective-permute-done | bytes 73760 | tf_op jit(solution)/shard_map/ppermute | solution.py:289
  96.9 0.0 collective-permute-done.16
  96.9 0.1 broadcast_select_fusion.7
  97.0 0.9 multiply_reduce_fusion
  98.0 0.7 broadcast_in_dim.2
  98.7 7.8 %all-to-all-start.3 = ((f32[64,8,128]{2,1,0:T(8,128)}), f32[64,8,128]{2,1,0:T(8,128)S(1)}, u32[]{:S(2)}, u32[]{:S(2)}) async-start(f32[64,8,128]{2,1,0:T(8,128)} %broadcast_in_dim.2), calls=%async_computation.3 | async-start | bytes 524288 | tf_op jit(solution)/shard_map/all_to_all | solution.py:301
  106.4 0.7 copy.10
  107.2 14.3 %all-to-all-done.3 = f32[64,8,128]{2,1,0:T(8,128)S(1)} async-done(((f32[64,8,128]{2,1,0:T(8,128)}), f32[64,8,128]{2,1,0:T(8,128)S(1)}, u32[]{:S(2)}, u32[]{:S(2)}) %all-to-all-start.3) | async-done | bytes 262176 | tf_op jit(solution)/shard_map/all_to_all | solution.py:301
  121.5 0.1 reduce_sum.19
  121.5 0.6 reshape.60
  (21 shorter events, 0.2 us)
Async XLA Ops:
  8.4 0.9 copy-start
  9.3 25.2 %all-to-all-start = ((f32[4,384,256]{2,1,0:T(8,128)}), f32[4,384,256]{2,1,0:T(8,128)S(1)}, u32[]{:S(2)}, u32[]{:S(2)}) async-start(f32[4,384,256]{2,1,0:T(8,128)} %get-tuple-element.24), calls=%async_computation | async-start | bytes 3145728 | tf_op jit(solution)/shard_map/all_to_all | solution.py:40
  13.7 19.2 %collective-permute-start.1 = (f32[768,256]{1,0:T(8,128)}, f32[768,256]{1,0:T(8,128)S(1)}, u32[]{:S(2)}, u32[]{:S(2)}) collective-permute-start(f32[768,256]{1,0:T(8,128)} %copy-done), channel_id=1, source_target_pairs={{0,130},{1,131},{2,128},{3,129},{4,134},{5,135},{6,132},{7,133},{8... | collective-permute-start | bytes 2359304 | tf_op jit(solution)/shard_map/ppermute | solution.py:36
  21.7 30.5 %collective-permute-start.10 = (f32[384,256]{1,0:T(8,128)}, f32[384,256]{1,0:T(8,128)S(1)}, u32[]{:S(2)}, u32[]{:S(2)}) collective-permute-start(f32[384,256]{1,0:T(8,128)} %get-tuple-element.39), channel_id=1, source_target_pairs={{0,112},{4,116},{8,120},{12,124},{16,0},{20,4},{24,8},{28,12},{32,... | collective-permute-start | bytes 1179656 | tf_op jit(solution)/shard_map/ppermute | solution.py:48
  27.7 24.5 %collective-permute-start.9 = (f32[384,256]{1,0:T(8,128)}, f32[384,256]{1,0:T(8,128)S(1)}, u32[]{:S(2)}, u32[]{:S(2)}) collective-permute-start(f32[384,256]{1,0:T(8,128)} %get-tuple-element.38), channel_id=1, source_target_pairs={{0,16},{4,20},{8,24},{12,28},{16,32},{20,36},{24,40},{28,44},{32,4... | collective-permute-start | bytes 1179656 | tf_op jit(solution)/shard_map/ppermute | solution.py:48
  32.9 5.7 %copy-start.4 = (f32[96,256]{1,0:T(8,128)S(1)}, f32[96,256]{1,0:T(8,128)}, u32[]{:S(2)}) copy-start(f32[96,256]{1,0:T(8,128)} %get-tuple-element.36) | copy-start | bytes 294916
  32.9 12.1 %copy-start.3 = (f32[96,256]{1,0:T(8,128)S(1)}, f32[96,256]{1,0:T(8,128)}, u32[]{:S(2)}) copy-start(f32[96,256]{1,0:T(8,128)} %get-tuple-element.37) | copy-start | bytes 294916
  34.4 30.4 %all-to-all-start.1 = ((f32[4,192,256]{2,1,0:T(8,128)}), f32[4,192,256]{2,1,0:T(8,128)}, u32[]{:S(2)}, u32[]{:S(2)}) async-start(f32[4,192,256]{2,1,0:T(8,128)} %bitcast.37), calls=%async_computation.1 | async-start | bytes 1572864 | tf_op jit(solution)/shard_map/all_to_all | solution.py:40
  38.6 9.6 %collective-permute-start.7 = (f32[96,256]{1,0:T(8,128)S(1)}, f32[96,256]{1,0:T(8,128)S(1)}, u32[]{:S(2)}, u32[]{:S(2)}) collective-permute-start(f32[96,256]{1,0:T(8,128)S(1)} %copy-done.4), channel_id=1, source_target_pairs={{0,96},{4,100},{8,104},{12,108},{16,112},{20,116},{24,120},{28,124... | collective-permute-start | bytes 294920 | tf_op jit(solution)/shard_map/ppermute | solution.py:48
  45.0 7.2 %collective-permute-start.8 = (f32[96,256]{1,0:T(8,128)S(1)}, f32[96,256]{1,0:T(8,128)S(1)}, u32[]{:S(2)}, u32[]{:S(2)}) collective-permute-start(f32[96,256]{1,0:T(8,128)S(1)} %copy-done.3), channel_id=1, source_target_pairs={{0,32},{4,36},{8,40},{12,44},{16,48},{20,52},{24,56},{28,60},{32,6... | collective-permute-start | bytes 294920 | tf_op jit(solution)/shard_map/ppermute | solution.py:48
  52.2 7.1 %copy-start.2 = (f32[1536]{0:T(1024)S(1)}, f32[1536]{0:T(1024)}, u32[]{:S(2)}) copy-start(f32[1536]{0:T(1024)} %param.8) | copy-start | bytes 18436
  53.4 10.7 %collective-permute-start.11 = (f32[192,256]{1,0:T(8,128)S(1)}, f32[192,256]{1,0:T(8,128)S(1)}, u32[]{:S(2)}, u32[]{:S(2)}) collective-permute-start(f32[192,256]{1,0:T(8,128)S(1)} %get-tuple-element.43), channel_id=1, source_target_pairs={{0,32},{4,36},{8,40},{12,44},{16,48},{20,52},{24,56},{28,60},{32,6... | collective-permute-start | bytes 589832 | tf_op jit(solution)/shard_map/ppermute | solution.py:48
  53.5 10.6 %collective-permute-start.12 = (f32[192,256]{1,0:T(8,128)S(1)}, f32[192,256]{1,0:T(8,128)S(1)}, u32[]{:S(2)}, u32[]{:S(2)}) collective-permute-start(f32[192,256]{1,0:T(8,128)S(1)} %get-tuple-element.44), channel_id=1, source_target_pairs={{0,96},{4,100},{8,104},{12,108},{16,112},{20,116},{24,120},{28,124... | collective-permute-start | bytes 589832 | tf_op jit(solution)/shard_map/ppermute | solution.py:48
  57.7 7.1 %collective-permute-start = (f32[192,256]{1,0:T(8,128)S(1)}, f32[192,256]{1,0:T(8,128)S(1)}, u32[]{:S(2)}, u32[]{:S(2)}) collective-permute-start(f32[192,256]{1,0:T(8,128)S(1)} %get-tuple-element.26), channel_id=1, source_target_pairs={{0,130},{1,131},{2,128},{3,129},{4,134},{5,135},{6,132},{7,133},{8... | collective-permute-start | bytes 589832 | tf_op jit(solution)/shard_map/ppermute | solution.py:36
  64.9 10.1 %all-to-all-start.2 = ((f32[4,48,256]{2,1,0:T(8,128)}), f32[4,48,256]{2,1,0:T(8,128)S(1)}, u32[]{:S(2)}, u32[]{:S(2)}) async-start(f32[4,48,256]{2,1,0:T(8,128)} %bitcast.10), calls=%async_computation.2 | async-start | bytes 393216 | tf_op jit(solution)/shard_map/all_to_all | solution.py:40
  68.5 25.0 %copy-start.1 = (bf16[1536,512]{1,0:T(8,128)(2,1)S(1)}, bf16[1536,512]{1,0:T(8,128)(2,1)}, u32[]{:S(2)}) copy-start(bf16[1536,512]{1,0:T(8,128)(2,1)} %param.9) | copy-start | bytes 4718596
  70.6 9.4 %collective-permute-start.3 = (f32[96,256]{1,0:T(8,128)S(1)}, f32[96,256]{1,0:T(8,128)S(1)}, u32[]{:S(2)}, u32[]{:S(2)}) collective-permute-start(f32[96,256]{1,0:T(8,128)S(1)} %get-tuple-element.31), channel_id=1, source_target_pairs={{0,112},{4,116},{8,120},{12,124},{16,0},{20,4},{24,8},{28,12},{32,... | collective-permute-start | bytes 294920 | tf_op jit(solution)/shard_map/ppermute | solution.py:48
  74.9 5.1 %collective-permute-start.5 = (f32[48,256]{1,0:T(8,128)S(1)}, f32[48,256]{1,0:T(8,128)S(1)}, u32[]{:S(2)}, u32[]{:S(2)}) collective-permute-start(f32[48,256]{1,0:T(8,128)S(1)} %get-tuple-element.34), channel_id=1, source_target_pairs={{0,96},{4,100},{8,104},{12,108},{16,112},{20,116},{24,120},{28,124... | collective-permute-start | bytes 147464 | tf_op jit(solution)/shard_map/ppermute | solution.py:48
  75.0 9.3 %collective-permute-start.13 = (f32[24,256]{1,0:T(8,128)S(1)}, f32[24,256]{1,0:T(8,128)S(1)}, u32[]{:S(2)}, u32[]{:S(2)}) collective-permute-start(f32[24,256]{1,0:T(8,128)S(1)} %fusion.13), channel_id=1, source_target_pairs={{0,130},{1,131},{2,128},{3,129},{4,134},{5,135},{6,132},{7,133},{8... | collective-permute-start | bytes 73736 | tf_op jit(solution)/shard_map/ppermute | solution.py:36
  76.6 7.3 %collective-permute-start.2 = (f32[96,256]{1,0:T(8,128)S(1)}, f32[96,256]{1,0:T(8,128)S(1)}, u32[]{:S(2)}, u32[]{:S(2)}) collective-permute-start(f32[96,256]{1,0:T(8,128)S(1)} %get-tuple-element.30), channel_id=1, source_target_pairs={{0,16},{4,20},{8,24},{12,28},{16,32},{20,36},{24,40},{28,44},{32,4... | collective-permute-start | bytes 294920 | tf_op jit(solution)/shard_map/ppermute | solution.py:48
  80.1 5.8 %collective-permute-start.6 = (f32[48,256]{1,0:T(8,128)S(1)}, f32[48,256]{1,0:T(8,128)S(1)}, u32[]{:S(2)}, u32[]{:S(2)}) collective-permute-start(f32[48,256]{1,0:T(8,128)S(1)} %fusion.10), channel_id=1, source_target_pairs={{0,96},{4,100},{8,104},{12,108},{16,112},{20,116},{24,120},{28,124... | collective-permute-start | bytes 147464 | tf_op jit(solution)/shard_map/ppermute | solution.py:48
  83.9 6.6 %collective-permute-start.4 = (f32[48,256]{1,0:T(8,128)S(1)}, f32[48,256]{1,0:T(8,128)S(1)}, u32[]{:S(2)}, u32[]{:S(2)}) collective-permute-start(f32[48,256]{1,0:T(8,128)S(1)} %slice_add_fusion.1), channel_id=1, source_target_pairs={{0,32},{4,36},{8,40},{12,44},{16,48},{20,52},{24,56},{28,60},{32,6... | collective-permute-start | bytes 147464 | tf_op jit(solution)/shard_map/ppermute | solution.py:48
  90.7 3.8 %collective-permute-start.14 = (f32[24,2,384]{2,0,1:T(8,128)S(1)}, f32[24,2,384]{2,0,1:T(8,128)S(1)}, u32[]{:S(2)}, u32[]{:S(2)}) collective-permute-start(f32[24,2,384]{2,0,1:T(8,128)S(1)} %fusion.9), channel_id=1, source_target_pairs={{0,3},{1,2},{2,1},{3,0},{4,7},{5,6},{6,5},{7,4},{8,11},{9,10},{10,... | collective-permute-start | bytes 221192 | tf_op jit(solution)/shard_map/ppermute | solution.py:289
  90.7 6.2 %collective-permute-start.15 = (f32[24,2,384]{2,0,1:T(8,128)S(1)}, f32[24,2,384]{2,0,1:T(8,128)S(1)}, u32[]{:S(2)}, u32[]{:S(2)}) collective-permute-start(f32[24,2,384]{2,0,1:T(8,128)S(1)} %fusion.9), channel_id=1, source_target_pairs={{0,2},{1,3},{2,0},{3,1},{4,6},{5,7},{6,4},{7,5},{8,10},{9,11},{10,... | collective-permute-start | bytes 221192 | tf_op jit(solution)/shard_map/ppermute | solution.py:289
  93.5 3.4 %collective-permute-start.16 = (f32[24,2,384]{2,0,1:T(8,128)S(1)}, f32[24,2,384]{2,0,1:T(8,128)S(1)}, u32[]{:S(2)}, u32[]{:S(2)}) collective-permute-start(f32[24,2,384]{2,0,1:T(8,128)S(1)} %fusion.9), channel_id=1, source_target_pairs={{0,1},{1,0},{2,3},{3,2},{4,5},{5,4},{6,7},{7,6},{8,9},{9,8},{10,11... | collective-permute-start | bytes 221192 | tf_op jit(solution)/shard_map/ppermute | solution.py:289
  98.7 22.8 %all-to-all-start.3 = ((f32[64,8,128]{2,1,0:T(8,128)}), f32[64,8,128]{2,1,0:T(8,128)S(1)}, u32[]{:S(2)}, u32[]{:S(2)}) async-start(f32[64,8,128]{2,1,0:T(8,128)} %broadcast_in_dim.2), calls=%async_computation.3 | async-start | bytes 524288 | tf_op jit(solution)/shard_map/all_to_all | solution.py:301

commit v5 on v4

--- a/solution.py
+++ b/solution.py
@@ -11,6 +11,7 @@
 QUARTERS = 4
 Z_ORDER = (4, 1, 3, -1, -3, 0, 2, -2)
 Z_SLICES = ((0, 1), (1, 3), (3, 5), (5, 6), (6, 7), (7, 8))
+X_GROUPS = [list(range(x * NZ * NY, (x + 1) * NZ * NY)) for x in range(NX)]
 Y_GROUPS = [[base + y for y in range(NY)] for base in range(0, NX * NZ * NY, NY)]
 
 
@@ -101,6 +102,20 @@
     position = lax.axis_index("pair")
     x = position // (NZ * NY)
     return lax.axis_index("sigma") ^ (2 * x), x, (position // NY) & (NZ - 1)
+
+
+def interleaved(one, two, row_count):
+    columns = one.shape[1]
+
+    def body(one, two, *outs):
+        for out, (low, high) in zip(outs, Z_SLICES):
+            for k in range(low, high):
+                rows = slice(k * row_count, k * row_count + row_count)
+                at = 2 * (k - low) * row_count
+                out[at : at + row_count] = one[rows]
+                out[at + row_count : at + 2 * row_count] = added(two, rows)
+
+    return on_chip(body, [(2 * (high - low) * row_count, columns) for low, high in Z_SLICES])(one, two)
 
 
 def fetcher(pairs_ref, pair_ref, done):
@@ -207,12 +222,28 @@
     columns = scaled.shape[1]
     shapes = stream[0]
 
+    part = pair_local // QUARTERS
+
     def body(pairs_ref, scaled_ref, *refs):
-        pair_ref, rows_ref, done = refs[len(shapes) :]
-        first_column, fetch = fetcher(pairs_ref, pair_ref, done)
+        pair_ref, turned_ref, sum_ref, rows_ref, done = refs[len(shapes) :]
+
+        def fetch(step):
+            return pltpu.make_async_copy(pairs_ref.at[step * part : step * part + part], pair_ref.at[step], done.at[step])
+
         for step in range(QUARTERS):
             fetch(step).start()
-        multiply(first_column, fetch, pair_ref, scaled_ref, rows_ref, 0)
+        turned_ref[...] = jnp.transpose(scaled_ref[...])
+        for step in range(QUARTERS):
+            fetch(step).wait()
+            product = jnp.dot(
+                turned_ref[:, step * part : step * part + part], pair_ref[step], preferred_element_type=jnp.float32
+            )
+            if step == 0:
+                sum_ref[...] = product
+            elif step < QUARTERS - 1:
+                sum_ref[...] += product
+            else:
+                rows_ref[...] = jnp.transpose(sum_ref[...] + product)
         store([stream], refs, rows_ref)
 
     return pl.pallas_call(
@@ -221,7 +252,9 @@
         out_specs=[pl.BlockSpec(shape, lambda: (0, 0)) for shape in shapes],
         out_shape=[pltpu.HBM(shape, jnp.float32) for shape in shapes],
         scratch_shapes=[
-            pltpu.VMEM((QUARTERS, pair_local, width // QUARTERS), jnp.bfloat16),
+            pltpu.VMEM((QUARTERS, part, width), jnp.bfloat16),
+            pltpu.VMEM((columns, pair_local), jnp.bfloat16),
+            pltpu.VMEM((columns, width), jnp.float32),
             pltpu.VMEM((width, columns), jnp.float32),
             pltpu.SemaphoreType.DMA((QUARTERS,)),
         ],
@@ -268,13 +301,7 @@
     b = y_parts(b)
     b = x_swap(*halves_added(b))
     c = y_parts(c.reshape(NY, NZ * rc, n))
-    bc = []
-    for low, high in Z_SLICES:
-        for k in range(low, high):
-            bc.append(jnp.concatenate([b[block(k)], added(c, block(k))], axis=0))
-    bc = lax.optimization_barrier(
-        (bc[0], jnp.concatenate(bc[1:3]), jnp.concatenate(bc[3:5]), bc[5], bc[6], bc[7])
-    )
+    bc = interleaved(b, c, rc)
     bc = z_sum(*bc)
     a = z_sum_both(*a).reshape(NY, NX * rc, n)
     a = y_parts(a)
@@ -285,20 +312,19 @@
     root_rows = lax.dynamic_slice_in_dim(root, pair_position * row_count, row_count, 0)
     root_columns = lax.dynamic_slice_in_dim(root, quarter * col_count, col_count, 0)
     screened = -root_rows[:, None, None] * polar.reshape(row_count, -1, col_count) * root_columns[None, None, :]
-    parts = [screened] + [
-        lax.ppermute(screened, "sigma", [(s, s ^ k) for s in range(sigma_count)]) for k in range(1, sigma_count)
-    ]
-    for bit in (1, 2):
-        odd = (quarter & bit) != 0
-        parts = [jnp.where(odd, parts[k ^ bit], parts[k]) for k in range(sigma_count)]
+    gathered = lax.all_gather(screened, "sigma")
+    upper = quarter != lax.axis_index("sigma")
+    parts = [jnp.where(upper, gathered[k ^ 2], gathered[k]) for k in range(sigma_count)]
     states_wide = state_matrices.astype(jnp.float32)
     applied = jnp.einsum(
         "rfc,cn->rfn", jnp.concatenate(parts, axis=2), states_wide, precision=lax.Precision.HIGHEST
     )
     own_states = lax.dynamic_slice_in_dim(states_wide, pair_position * row_count, row_count, 0)
     total = jnp.sum(own_states[:, None, :] * applied, axis=0) / jnp.float32(width)
-    spread = jnp.broadcast_to(total.reshape(8, -1)[None], (pair_count, 8, total.size // 8))
-    total = jnp.sum(lax.all_to_all(spread, "pair", 0, 0, tiled=True), axis=0).reshape(total.shape)
+    tile = total.reshape(8, -1)
+    tile += lax.ppermute(tile, "pair", [(p, p ^ (NZ * NY)) for p in range(pair_count)])
+    spread = jnp.broadcast_to(tile[None], (NZ * NY,) + tile.shape)
+    total = jnp.sum(lax.all_to_all(spread, "pair", 0, 0, axis_index_groups=X_GROUPS, tiled=True), axis=0).reshape(total.shape)
     return (applied, total)
 
 

time: 123 us -> 123 us (level)
  blocking collectives: 0 us -> 7.18 us
  starting transfers between devices: 54.5 us -> 52.6 us
  waiting for transfers between devices: 43.1 us -> 41.2 us
  other arithmetic: 3.49 us -> 2.05 us
  Pallas kernels: 16.2 us -> 14.8 us
    all_gather x0 -> x1, blocking collectives: none -> 7.18 us  [local(): gathered = lax.all_gather(screened, 'sigma')]
    all_to_all x1, waiting for transfers between devices: 14.3 us -> 9.82 us  [local(): lax.all_to_all(spread, 'pair', 0, 0, axis_index_groups=X_GROUPS, tiled=True)]
    add x3 -> x1, other arithmetic: 2.05 us -> 0.01 us  [added(): return parts[0, rows] + parts[1, rows] + (parts[2, rows] + parts[3, rows])]
    all_to_all x1, starting transfers between devices: 7.77 us -> 5.87 us  [local(): lax.all_to_all(spread, 'pair', 0, 0, axis_index_groups=X_GROUPS, tiled=True)]
    ppermute x3, waiting for transfers between devices: 5.27 us -> 6.97 us  [x_swap(): return keep + lax.ppermute(away, ('pair', 'sigma'), moves)]
    pallas_call x1, Pallas kernels: 6.5 us -> 4.81 us  [last_stream(): pl.pallas_call(body, in_specs=[pl.BlockSpec(memory_space=pltpu.HBM), pl.B...]
    ppermute x11, waiting for transfers between devices: 19.6 us -> 21.1 us  [z_send(): return lax.ppermute(part, 'pair', z_perm(dz))]
    ppermute x3 -> x1, waiting for transfers between devices: 3.41 us -> 2.1 us  [local(): lax.ppermute(tile, 'pair', [(p, p ^ NZ * NY) for p in range(pair_count)])]
  transfers between devices with their start and end apart: 21 -> 19, of which waited for: 12 -> 13; matrix products, arithmetic and copies ran while one was open for 3% -> 2% of each run, Pallas kernels for 7% -> 6%
where the time goes in v5:
time: 123 us
  starting transfers between devices  52.6 us (43%)
  waiting for transfers between devices  41.2 us (33%)
  Pallas kernels  14.8 us (12%)
  blocking collectives  7.18 us (6%)
  local copies, waits for them, and re-layouts  3.03 us (2%)
  other arithmetic  2.05 us (2%)
    ppermute x11, starting transfers between devices, z_send(): return lax.ppermute(part, 'pair', z_perm(dz))  27.4 us
    ppermute x11, waiting for transfers between devices, z_send(): return lax.ppermute(part, 'pair', z_perm(dz))  21.1 us
    all_to_all x3, starting transfers between devices, y_parts(): lax.all_to_all(block, 'pair', 0, 0, axis_index_groups=Y_GROUPS, tiled=True)  12.3 us
    all_to_all x1, waiting for transfers between devices, local(): lax.all_to_all(spread, 'pair', 0, 0, axis_index_groups=X_GROUPS, tiled=True)  9.82 us
    pallas_call x1, Pallas kernels, first_streams(): pl.pallas_call(body, in_specs=[pl.BlockSpec(memory_space=pltpu.HBM)] * 3,...  7.74 us
    all_gather x1, blocking collectives, local(): gathered = lax.all_gather(screened, 'sigma')  7.18 us
    ppermute x3, waiting for transfers between devices, x_swap(): return keep + lax.ppermute(away, ('pair', 'sigma'), moves)  6.97 us
    all_to_all x1, starting transfers between devices, local(): lax.all_to_all(spread, 'pair', 0, 0, axis_index_groups=X_GROUPS, tiled=True)  5.87 us
  transfers between devices with their start and end apart: 19, of which 13 were waited for; matrix products, arithmetic and copies ran while one was open for 2% of the time, Pallas kernels for 6%

profile of v5, /device:TPU:2, one launch (start us, length us, event | category | flops | bytes accessed | tf_op | source)
XLA Modules:
  0.0 122.5 jit_solution(2575543281764735207)
XLA Ops:
  0.6 7.7 %shard_map.68 = (f32[4,384,256]{2,1,0:T(8,128)}, f32[768,256]{1,0:T(8,128)S(1)}, f32[768,256]{1,0:T(8,128)S(1)}, bf16[2048,256]{1,0:T(8,128)(2,1)S(1)}) custom-call(bf16[2048,1536]{1,0:T(8,128)(2,1)} %pairs_ref.3, s32[2,2048]{1,0:T(2,128)} %bitcast.22, f32[2,64]{1,0:T(2,128)} %table_hbm.1), custom_call_target="tpu_custom_call" | custom-call | tf_op jit(solution)/shard_map/pallas_call | solution.py:200
  8.4 0.0 copy-start
  8.4 0.9 copy-done
  9.3 4.5 %all-to-all-start = ((f32[4,384,256]{2,1,0:T(8,128)}), f32[4,384,256]{2,1,0:T(8,128)S(1)}, u32[]{:S(2)}, u32[]{:S(2)}) async-start(f32[4,384,256]{2,1,0:T(8,128)} %get-tuple-element.24), calls=%async_computation | async-start | bytes 3145728 | tf_op jit(solution)/shard_map/all_to_all | solution.py:41
  13.7 1.5 %collective-permute-start.1 = (f32[768,256]{1,0:T(8,128)}, f32[768,256]{1,0:T(8,128)S(1)}, u32[]{:S(2)}, u32[]{:S(2)}) collective-permute-start(f32[768,256]{1,0:T(8,128)} %copy-done), channel_id=1, source_target_pairs={{0,130},{1,131},{2,128},{3,129},{4,134},{5,135},{6,132},{7,133},{8... | collective-permute-start | bytes 2359304 | tf_op jit(solution)/shard_map/ppermute | solution.py:37
  15.2 4.8 %shard_map.71 = (f32[96,256]{1,0:T(8,128)}, f32[96,256]{1,0:T(8,128)}, f32[384,256]{1,0:T(8,128)}, f32[384,256]{1,0:T(8,128)}, f32[192,256]{1,0:T(8,128)}, /*index=5*/f32[192,256]{1,0:T(8,128)}, f32[192,256]{1,0:T(8,128)}) custom-call(bf16[2048,1536]{1,0:T(8,128)(2,1)} %pairs_ref.3, bf16[2048,256]{1,0:T(8,128)(2,1)S(1)} %get-tuple-element.35.scaled_ref), custom_call_target="tpu_custom_call" | custom-call | tf_op jit(solution)/shard_map/pallas_call | solution.py:249
  20.0 5.9 %collective-permute-start.10 = (f32[384,256]{1,0:T(8,128)}, f32[384,256]{1,0:T(8,128)}, u32[]{:S(2)}, u32[]{:S(2)}) collective-permute-start(f32[384,256]{1,0:T(8,128)} %get-tuple-element.39), channel_id=1, source_target_pairs={{0,112},{4,116},{8,120},{12,124},{16,0},{20,4},{24,8},{28,12},{32,... | collective-permute-start | bytes 1179656 | tf_op jit(solution)/shard_map/ppermute | solution.py:49
  26.0 0.0 collective-permute-start.9
  26.0 7.0 %collective-permute-done.1 = f32[768,256]{1,0:T(8,128)S(1)} collective-permute-done((f32[768,256]{1,0:T(8,128)}, f32[768,256]{1,0:T(8,128)S(1)}, u32[]{:S(2)}, u32[]{:S(2)}) %collective-permute-start.1) | collective-permute-done | bytes 786464 | tf_op jit(solution)/shard_map/ppermute | solution.py:37
  33.0 0.0 copy-start.4
  33.0 0.0 copy-start.3
  33.0 1.0 add.71
  34.0 0.5 all-to-all-done.parts
  34.5 0.0 copy-start.2
  34.5 4.2 %all-to-all-start.1 = ((f32[4,192,256]{2,1,0:T(8,128)}), f32[4,192,256]{2,1,0:T(8,128)S(1)}, u32[]{:S(2)}, u32[]{:S(2)}) async-start(f32[4,192,256]{2,1,0:T(8,128)} %bitcast.1), calls=%async_computation.1 | async-start | bytes 1572864 | tf_op jit(solution)/shard_map/all_to_all | solution.py:41
  38.6 0.0 copy-done.4
  38.6 6.3 %collective-permute-start.7 = (f32[96,256]{1,0:T(8,128)S(1)}, f32[96,256]{1,0:T(8,128)S(1)}, u32[]{:S(2)}, u32[]{:S(2)}) collective-permute-start(f32[96,256]{1,0:T(8,128)S(1)} %copy-done.4), channel_id=1, source_target_pairs={{0,96},{4,100},{8,104},{12,108},{16,112},{20,116},{24,120},{28,124... | collective-permute-start | bytes 294920 | tf_op jit(solution)/shard_map/ppermute | solution.py:49
  44.9 0.0 copy-done.3
  44.9 0.0 collective-permute-start.8
  44.9 3.2 %collective-permute-done.7.low = f32[96,256]{1,0:T(8,128)S(1)} collective-permute-done((f32[96,256]{1,0:T(8,128)S(1)}, f32[96,256]{1,0:T(8,128)S(1)}, u32[]{:S(2)}, u32[]{:S(2)}) %collective-permute-start.7) | collective-permute-done | bytes 98336 | tf_op jit(solution)/shard_map/ppermute | solution.py:49
  48.1 4.0 %collective-permute-done.8.high = f32[96,256]{1,0:T(8,128)S(1)} collective-permute-done((f32[96,256]{1,0:T(8,128)S(1)}, f32[96,256]{1,0:T(8,128)S(1)}, u32[]{:S(2)}, u32[]{:S(2)}) %collective-permute-start.8) | collective-permute-done | bytes 98336 | tf_op jit(solution)/shard_map/ppermute | solution.py:49
  52.2 0.0 collective-permute-done.10.down
  52.2 0.0 collective-permute-done.9.up
  52.2 1.4 %shard_map.72 = (f32[192,256]{1,0:T(8,128)S(1)}, f32[192,256]{1,0:T(8,128)S(1)}, f32[192,256]{1,0:T(8,128)S(1)}) custom-call(f32[96,256]{1,0:T(8,128)S(1)} %collective-permute-done.7.low, f32[96,256]{1,0:T(8,128)S(1)} %collective-permute-done.8.high, f32[384,256]{1,0:T(8,128)} %collective-permute-done.9.up, f32[384,256]{1,0:T(8,128)} %collective-permute-done.10.down, ...), custom_call_target="tpu_custom_call" | custom-call | tf_op jit(solution)/shard_map/pallas_call | solution.py:74
  53.6 0.1 collective-permute-start.11
  53.7 4.1 %collective-permute-start.12 = (f32[192,256]{1,0:T(8,128)S(1)}, f32[192,256]{1,0:T(8,128)S(1)}, u32[]{:S(2)}, u32[]{:S(2)}) collective-permute-start(f32[192,256]{1,0:T(8,128)S(1)} %get-tuple-element.44), channel_id=1, source_target_pairs={{0,96},{4,100},{8,104},{12,108},{16,112},{20,116},{24,120},{28,124... | collective-permute-start | bytes 589832 | tf_op jit(solution)/shard_map/ppermute | solution.py:49
  57.8 0.0 copy-done.2
  57.8 5.5 %collective-permute-done.11.above = f32[192,256]{1,0:T(8,128)S(1)} collective-permute-done((f32[192,256]{1,0:T(8,128)S(1)}, f32[192,256]{1,0:T(8,128)S(1)}, u32[]{:S(2)}, u32[]{:S(2)}) %collective-permute-start.11) | collective-permute-done | bytes 196640 | tf_op jit(solution)/shard_map/ppermute | solution.py:49
  63.3 0.4 collective-permute-done.12.below
  63.7 0.7 shard_map.73
  64.4 0.1 shard_map.69
  64.5 1.7 %collective-permute-start = (f32[192,256]{1,0:T(8,128)S(1)}, f32[192,256]{1,0:T(8,128)S(1)}, u32[]{:S(2)}, u32[]{:S(2)}) collective-permute-start(f32[192,256]{1,0:T(8,128)S(1)} %get-tuple-element.26), channel_id=1, source_target_pairs={{0,130},{1,131},{2,128},{3,129},{4,134},{5,135},{6,132},{7,133},{8... | collective-permute-start | bytes 589832 | tf_op jit(solution)/shard_map/ppermute | solution.py:37
  66.3 0.0 all-to-all-done.1.two
  66.3 3.6 %all-to-all-start.2 = ((f32[4,48,256]{2,1,0:T(8,128)}), f32[4,48,256]{2,1,0:T(8,128)S(1)}, u32[]{:S(2)}, u32[]{:S(2)}) async-start(f32[4,48,256]{2,1,0:T(8,128)} %bitcast.2), calls=%async_computation.2 | async-start | bytes 393216 | tf_op jit(solution)/shard_map/all_to_all | solution.py:41
  69.9 0.1 dynamic-slice_negate_fusion
  70.0 0.1 dynamic_slice.10
  70.0 0.7 dynamic-slice_convert_fusion
  70.8 0.0 collective-permute-done
  70.8 0.0 copy-start.1
  70.8 0.1 shard_map.70
  70.9 4.6 %collective-permute-start.3 = (f32[96,256]{1,0:T(8,128)S(1)}, f32[96,256]{1,0:T(8,128)S(1)}, u32[]{:S(2)}, u32[]{:S(2)}) collective-permute-start(f32[96,256]{1,0:T(8,128)S(1)} %get-tuple-element.31), channel_id=1, source_target_pairs={{0,112},{4,116},{8,120},{12,124},{16,0},{20,4},{24,8},{28,12},{32,... | collective-permute-start | bytes 294920 | tf_op jit(solution)/shard_map/ppermute | solution.py:49
  75.5 0.0 collective-permute-start.5
  75.5 0.7 all-to-all-done.2
  76.2 0.7 collective-permute-start.13
  76.9 2.7 %collective-permute-start.2 = (f32[96,256]{1,0:T(8,128)S(1)}, f32[96,256]{1,0:T(8,128)S(1)}, u32[]{:S(2)}, u32[]{:S(2)}) collective-permute-start(f32[96,256]{1,0:T(8,128)S(1)} %get-tuple-element.30), channel_id=1, source_target_pairs={{0,16},{4,20},{8,24},{12,28},{16,32},{20,36},{24,40},{28,44},{32,4... | collective-permute-start | bytes 294920 | tf_op jit(solution)/shard_map/ppermute | solution.py:49
  79.6 0.8 collective-permute-done.5
  80.5 0.0 collective-permute-done.3
  80.5 3.6 %collective-permute-start.6 = (f32[48,256]{1,0:T(8,128)S(1)}, f32[48,256]{1,0:T(8,128)S(1)}, u32[]{:S(2)}, u32[]{:S(2)}) collective-permute-start(f32[48,256]{1,0:T(8,128)S(1)} %fusion.10), channel_id=1, source_target_pairs={{0,96},{4,100},{8,104},{12,108},{16,112},{20,116},{24,120},{28,124... | collective-permute-start | bytes 147464 | tf_op jit(solution)/shard_map/ppermute | solution.py:49
  84.1 0.4 collective-permute-done.2
  84.5 0.1 collective-permute-start.4
  84.6 0.0 collective-permute-done.13
  84.6 1.2 %collective-permute-done.6 = f32[48,256]{1,0:T(8,128)S(1)} collective-permute-done((f32[48,256]{1,0:T(8,128)S(1)}, f32[48,256]{1,0:T(8,128)S(1)}, u32[]{:S(2)}, u32[]{:S(2)}) %collective-permute-start.6) | collective-permute-done | bytes 49184 | tf_op jit(solution)/shard_map/ppermute | solution.py:49
  85.8 5.4 %collective-permute-done.4 = f32[48,256]{1,0:T(8,128)S(1)} collective-permute-done((f32[48,256]{1,0:T(8,128)S(1)}, f32[48,256]{1,0:T(8,128)S(1)}, u32[]{:S(2)}, u32[]{:S(2)}) %collective-permute-start.4) | collective-permute-done | bytes 49184 | tf_op jit(solution)/shard_map/ppermute | solution.py:49
  91.4 0.1 fusion.9
  91.4 7.2 %all_gather.4 = f32[4,24,2,384]{3,1,2,0:T(8,128)S(1)} all-gather(f32[1,24,2,384]{3,1,2,0:T(8,128)S(1)} %fusion.9), channel_id=1, replica_groups=mesh['pair'=64,'sigma'=4] {'sigma'}, dimensions={0}, use_global_device_ids=true | all-gather | bytes 368640 | tf_op jit(solution)/shard_map/all_gather | solution.py:315
  98.7 0.0 copy-done.1
  98.7 0.9 multiply_reduce_fusion
  99.6 3.1 %collective-permute-start.14 = (f32[8,128]{1,0:T(8,128)S(1)}, f32[8,128]{1,0:T(8,128)S(1)}, u32[]{:S(2)}, u32[]{:S(2)}) collective-permute-start(f32[8,128]{1,0:T(8,128)S(1)} %div.21), channel_id=1, source_target_pairs={{0,128},{4,132},{8,136},{12,140},{16,144},{20,148},{24,152},{28,15... | collective-permute-start | bytes 12296 | tf_op jit(solution)/shard_map/ppermute | solution.py:325
  102.7 2.1 %collective-permute-done.14 = f32[8,128]{1,0:T(8,128)S(1)} collective-permute-done((f32[8,128]{1,0:T(8,128)S(1)}, f32[8,128]{1,0:T(8,128)S(1)}, u32[]{:S(2)}, u32[]{:S(2)}) %collective-permute-start.14) | collective-permute-done | bytes 4128 | tf_op jit(solution)/shard_map/ppermute | solution.py:325
  104.8 0.7 broadcast_in_dim.2
  105.5 5.9 %all-to-all-start.3 = ((f32[32,8,128]{2,1,0:T(8,128)}), f32[32,8,128]{2,1,0:T(8,128)S(1)}, u32[]{:S(2)}, u32[]{:S(2)}) async-start(f32[32,8,128]{2,1,0:T(8,128)} %broadcast_in_dim.2), calls=%async_computation.3 | async-start | bytes 262144 | tf_op jit(solution)/shard_map/all_to_all | solution.py:327
  111.3 0.7 copy.12
  112.1 9.8 %all-to-all-done.3 = f32[32,8,128]{2,1,0:T(8,128)S(1)} async-done(((f32[32,8,128]{2,1,0:T(8,128)}), f32[32,8,128]{2,1,0:T(8,128)S(1)}, u32[]{:S(2)}, u32[]{:S(2)}) %all-to-all-start.3) | async-done | bytes 131104 | tf_op jit(solution)/shard_map/all_to_all | solution.py:327
  121.9 0.6 reshape.55
  (15 shorter events, 0.2 us)
Async XLA Ops:
  8.4 0.9 copy-start
  9.3 25.2 %all-to-all-start = ((f32[4,384,256]{2,1,0:T(8,128)}), f32[4,384,256]{2,1,0:T(8,128)S(1)}, u32[]{:S(2)}, u32[]{:S(2)}) async-start(f32[4,384,256]{2,1,0:T(8,128)} %get-tuple-element.24), calls=%async_computation | async-start | bytes 3145728 | tf_op jit(solution)/shard_map/all_to_all | solution.py:41
  13.7 19.2 %collective-permute-start.1 = (f32[768,256]{1,0:T(8,128)}, f32[768,256]{1,0:T(8,128)S(1)}, u32[]{:S(2)}, u32[]{:S(2)}) collective-permute-start(f32[768,256]{1,0:T(8,128)} %copy-done), channel_id=1, source_target_pairs={{0,130},{1,131},{2,128},{3,129},{4,134},{5,135},{6,132},{7,133},{8... | collective-permute-start | bytes 2359304 | tf_op jit(solution)/shard_map/ppermute | solution.py:37
  20.0 32.1 %collective-permute-start.10 = (f32[384,256]{1,0:T(8,128)}, f32[384,256]{1,0:T(8,128)}, u32[]{:S(2)}, u32[]{:S(2)}) collective-permute-start(f32[384,256]{1,0:T(8,128)} %get-tuple-element.39), channel_id=1, source_target_pairs={{0,112},{4,116},{8,120},{12,124},{16,0},{20,4},{24,8},{28,12},{32,... | collective-permute-start | bytes 1179656 | tf_op jit(solution)/shard_map/ppermute | solution.py:49
  26.0 26.2 %collective-permute-start.9 = (f32[384,256]{1,0:T(8,128)}, f32[384,256]{1,0:T(8,128)}, u32[]{:S(2)}, u32[]{:S(2)}) collective-permute-start(f32[384,256]{1,0:T(8,128)} %get-tuple-element.38), channel_id=1, source_target_pairs={{0,16},{4,20},{8,24},{12,28},{16,32},{20,36},{24,40},{28,44},{32,4... | collective-permute-start | bytes 1179656 | tf_op jit(solution)/shard_map/ppermute | solution.py:49
  33.0 5.7 %copy-start.4 = (f32[96,256]{1,0:T(8,128)S(1)}, f32[96,256]{1,0:T(8,128)}, u32[]{:S(2)}) copy-start(f32[96,256]{1,0:T(8,128)} %get-tuple-element.36) | copy-start | bytes 294916
  33.0 12.0 %copy-start.3 = (f32[96,256]{1,0:T(8,128)S(1)}, f32[96,256]{1,0:T(8,128)}, u32[]{:S(2)}) copy-start(f32[96,256]{1,0:T(8,128)} %get-tuple-element.37) | copy-start | bytes 294916
  34.5 23.3 %copy-start.2 = (f32[1536]{0:T(1024)S(1)}, f32[1536]{0:T(1024)}, u32[]{:S(2)}) copy-start(f32[1536]{0:T(1024)} %param.8) | copy-start | bytes 18436
  34.5 31.8 %all-to-all-start.1 = ((f32[4,192,256]{2,1,0:T(8,128)}), f32[4,192,256]{2,1,0:T(8,128)S(1)}, u32[]{:S(2)}, u32[]{:S(2)}) async-start(f32[4,192,256]{2,1,0:T(8,128)} %bitcast.1), calls=%async_computation.1 | async-start | bytes 1572864 | tf_op jit(solution)/shard_map/all_to_all | solution.py:41
  38.6 9.5 %collective-permute-start.7 = (f32[96,256]{1,0:T(8,128)S(1)}, f32[96,256]{1,0:T(8,128)S(1)}, u32[]{:S(2)}, u32[]{:S(2)}) collective-permute-start(f32[96,256]{1,0:T(8,128)S(1)} %copy-done.4), channel_id=1, source_target_pairs={{0,96},{4,100},{8,104},{12,108},{16,112},{20,116},{24,120},{28,124... | collective-permute-start | bytes 294920 | tf_op jit(solution)/shard_map/ppermute | solution.py:49
  44.9 7.2 %collective-permute-start.8 = (f32[96,256]{1,0:T(8,128)S(1)}, f32[96,256]{1,0:T(8,128)S(1)}, u32[]{:S(2)}, u32[]{:S(2)}) collective-permute-start(f32[96,256]{1,0:T(8,128)S(1)} %copy-done.3), channel_id=1, source_target_pairs={{0,32},{4,36},{8,40},{12,44},{16,48},{20,52},{24,56},{28,60},{32,6... | collective-permute-start | bytes 294920 | tf_op jit(solution)/shard_map/ppermute | solution.py:49
  53.6 9.7 %collective-permute-start.11 = (f32[192,256]{1,0:T(8,128)S(1)}, f32[192,256]{1,0:T(8,128)S(1)}, u32[]{:S(2)}, u32[]{:S(2)}) collective-permute-start(f32[192,256]{1,0:T(8,128)S(1)} %get-tuple-element.43), channel_id=1, source_target_pairs={{0,32},{4,36},{8,40},{12,44},{16,48},{20,52},{24,56},{28,60},{32,6... | collective-permute-start | bytes 589832 | tf_op jit(solution)/shard_map/ppermute | solution.py:49
  53.7 10.1 %collective-permute-start.12 = (f32[192,256]{1,0:T(8,128)S(1)}, f32[192,256]{1,0:T(8,128)S(1)}, u32[]{:S(2)}, u32[]{:S(2)}) collective-permute-start(f32[192,256]{1,0:T(8,128)S(1)} %get-tuple-element.44), channel_id=1, source_target_pairs={{0,96},{4,100},{8,104},{12,108},{16,112},{20,116},{24,120},{28,124... | collective-permute-start | bytes 589832 | tf_op jit(solution)/shard_map/ppermute | solution.py:49
  64.5 6.3 %collective-permute-start = (f32[192,256]{1,0:T(8,128)S(1)}, f32[192,256]{1,0:T(8,128)S(1)}, u32[]{:S(2)}, u32[]{:S(2)}) collective-permute-start(f32[192,256]{1,0:T(8,128)S(1)} %get-tuple-element.26), channel_id=1, source_target_pairs={{0,130},{1,131},{2,128},{3,129},{4,134},{5,135},{6,132},{7,133},{8... | collective-permute-start | bytes 589832 | tf_op jit(solution)/shard_map/ppermute | solution.py:37
  66.3 10.0 %all-to-all-start.2 = ((f32[4,48,256]{2,1,0:T(8,128)}), f32[4,48,256]{2,1,0:T(8,128)S(1)}, u32[]{:S(2)}, u32[]{:S(2)}) async-start(f32[4,48,256]{2,1,0:T(8,128)} %bitcast.2), calls=%async_computation.2 | async-start | bytes 393216 | tf_op jit(solution)/shard_map/all_to_all | solution.py:41
  70.8 27.8 %copy-start.1 = (bf16[1536,512]{1,0:T(8,128)(2,1)S(1)}, bf16[1536,512]{1,0:T(8,128)(2,1)}, u32[]{:S(2)}) copy-start(bf16[1536,512]{1,0:T(8,128)(2,1)} %param.9) | copy-start | bytes 4718596
  70.9 9.6 %collective-permute-start.3 = (f32[96,256]{1,0:T(8,128)S(1)}, f32[96,256]{1,0:T(8,128)S(1)}, u32[]{:S(2)}, u32[]{:S(2)}) collective-permute-start(f32[96,256]{1,0:T(8,128)S(1)} %get-tuple-element.31), channel_id=1, source_target_pairs={{0,112},{4,116},{8,120},{12,124},{16,0},{20,4},{24,8},{28,12},{32,... | collective-permute-start | bytes 294920 | tf_op jit(solution)/shard_map/ppermute | solution.py:49
  75.5 5.0 %collective-permute-start.5 = (f32[48,256]{1,0:T(8,128)S(1)}, f32[48,256]{1,0:T(8,128)S(1)}, u32[]{:S(2)}, u32[]{:S(2)}) collective-permute-start(f32[48,256]{1,0:T(8,128)S(1)} %get-tuple-element.34), channel_id=1, source_target_pairs={{0,96},{4,100},{8,104},{12,108},{16,112},{20,116},{24,120},{28,124... | collective-permute-start | bytes 147464 | tf_op jit(solution)/shard_map/ppermute | solution.py:49
  76.2 8.3 %collective-permute-start.13 = (f32[24,256]{1,0:T(8,128)S(1)}, f32[24,256]{1,0:T(8,128)S(1)}, u32[]{:S(2)}, u32[]{:S(2)}) collective-permute-start(f32[24,256]{1,0:T(8,128)S(1)} %fusion.13), channel_id=1, source_target_pairs={{0,130},{1,131},{2,128},{3,129},{4,134},{5,135},{6,132},{7,133},{8... | collective-permute-start | bytes 73736 | tf_op jit(solution)/shard_map/ppermute | solution.py:37
  76.9 7.5 %collective-permute-start.2 = (f32[96,256]{1,0:T(8,128)S(1)}, f32[96,256]{1,0:T(8,128)S(1)}, u32[]{:S(2)}, u32[]{:S(2)}) collective-permute-start(f32[96,256]{1,0:T(8,128)S(1)} %get-tuple-element.30), channel_id=1, source_target_pairs={{0,16},{4,20},{8,24},{12,28},{16,32},{20,36},{24,40},{28,44},{32,4... | collective-permute-start | bytes 294920 | tf_op jit(solution)/shard_map/ppermute | solution.py:49
  80.5 5.4 %collective-permute-start.6 = (f32[48,256]{1,0:T(8,128)S(1)}, f32[48,256]{1,0:T(8,128)S(1)}, u32[]{:S(2)}, u32[]{:S(2)}) collective-permute-start(f32[48,256]{1,0:T(8,128)S(1)} %fusion.10), channel_id=1, source_target_pairs={{0,96},{4,100},{8,104},{12,108},{16,112},{20,116},{24,120},{28,124... | collective-permute-start | bytes 147464 | tf_op jit(solution)/shard_map/ppermute | solution.py:49
  84.5 6.8 %collective-permute-start.4 = (f32[48,256]{1,0:T(8,128)S(1)}, f32[48,256]{1,0:T(8,128)S(1)}, u32[]{:S(2)}, u32[]{:S(2)}) collective-permute-start(f32[48,256]{1,0:T(8,128)S(1)} %slice_add_fusion.1), channel_id=1, source_target_pairs={{0,32},{4,36},{8,40},{12,44},{16,48},{20,52},{24,56},{28,60},{32,6... | collective-permute-start | bytes 147464 | tf_op jit(solution)/shard_map/ppermute | solution.py:49
  99.6 5.2 %collective-permute-start.14 = (f32[8,128]{1,0:T(8,128)S(1)}, f32[8,128]{1,0:T(8,128)S(1)}, u32[]{:S(2)}, u32[]{:S(2)}) collective-permute-start(f32[8,128]{1,0:T(8,128)S(1)} %div.21), channel_id=1, source_target_pairs={{0,128},{4,132},{8,136},{12,140},{16,144},{20,148},{24,152},{28,15... | collective-permute-start | bytes 12296 | tf_op jit(solution)/shard_map/ppermute | solution.py:325
  105.5 16.4 %all-to-all-start.3 = ((f32[32,8,128]{2,1,0:T(8,128)}), f32[32,8,128]{2,1,0:T(8,128)S(1)}, u32[]{:S(2)}, u32[]{:S(2)}) async-start(f32[32,8,128]{2,1,0:T(8,128)} %broadcast_in_dim.2), calls=%async_computation.3 | async-start | bytes 262144 | tf_op jit(solution)/shard_map/all_to_all | solution.py:327
